TPU v7x, 32 devices: a whole 2x2x4 slice. The times are simulated.
32 devices in a mesh: dp: 16 (over z, y, x), tensor: 2 (over core).
Axes of the slice: x: 2, y: 2, z: 4, core: 2. Of those that a mesh axis runs over, the one named last changes fastest.
Arguments:
- tokens: bfloat16 [2048, 1536], P('dp'), may hold values from -8 to 8
- attn_norm_gain: bfloat16 [1536], P('dp'), may hold values from 0.5 to 1.5
- w_query: bfloat16 [1536, 1536], P('dp', 'tensor'), may hold values from -1 to 1
- key_projection: bfloat16 [1536, 512], P('dp', 'tensor'), may hold values from -0.625 to 0.625
- value_projection: bfloat16 [1536, 512], P('dp', 'tensor'), may hold values from -0.15625 to 0.15625
- w_out: bfloat16 [1536, 1536], P('dp', 'tensor'), may hold values from -2 to 2
- moe_norm_gain: bfloat16 [1536], P('dp'), may hold values from 0.5 to 1.5
- w_gate: bfloat16 [16, 1536, 512], P('dp', None, 'tensor'), may hold values from -0.15625 to 0.15625
- w_up: bfloat16 [16, 1536, 512], P('dp', None, 'tensor'), may hold values from -0.15625 to 0.15625
- w_down: bfloat16 [16, 1536, 512], P('dp', None, 'tensor'), may hold values from -4 to 4
- router_logits: float32 [2048, 8], P('dp'), may hold values from -3 to 3
- expert_ids: int32 [2048, 8], P('dp'), may hold values from 0 to 15, all different within a row; in each aligned block of 128 rows (0 to 127, 128 to 255, ...) at most 72 rows name the same one
- segment_ids: int32 [16, 128], P('dp'), may hold values from 0 to 12, never falling along the last dimension, each value on 1 to 32 neighbouring positions
- parents: int32 [16, 13], P('dp'), may hold values from 0 to 4, as said below
- cotangent: bfloat16 [2048, 1536], P('dp'), may hold values from -6 to 6
Outputs:
- output: bfloat16 [2048, 1536], P('dp')
- input_grad: float32 [2048, 1536], P('dp')
- grad_attn_norm_gain: float32 [1536], P('dp')
- grad_w_query: float32 [1536, 1536], P('dp', 'tensor')
- grad_w_key: float32 [1536, 512], P('dp', 'tensor')
- grad_w_value: float32 [1536, 512], P('dp', 'tensor')
- grad_w_out: float32 [1536, 1536], P('dp', 'tensor')
- grad_moe_norm_gain: float32 [1536], P('dp')
- grad_w_gate: float32 [16, 1536, 512], P('dp', None, 'tensor')
- grad_w_up: float32 [16, 1536, 512], P('dp', None, 'tensor')
- grad_w_down: float32 [16, 1536, 512], P('dp', None, 'tensor')
- clipped_w_query: float32 [1536, 1536], P('dp', 'tensor')
- clipped_w_key: float32 [1536, 512], P('dp', 'tensor')
Inputs may be any that keep to these rules, and one draw needn't show every extreme that they name: `expert_ids`: each row names 8 different experts; within the rows of one tree no expert is named by more than 72 rows, a bound that some block reaches. `segment_ids`: along a tree the segment numbers never fall; each segment has 1 to 32 tokens, one exactly 32. `parents`: segment 0 is the trunk and its own parent; segments 1 to 4 have parent 0; every later segment has a parent among 1 to 4.
All inputs are finite; a program needn't handle non-finite values.
Results may differ from a plain program's by a relative error of at most 0.017.
Values may be sent and summed in bfloat16 or wider, within the bound.
A program may use at most 384 MiB of HBM per device.

v0:
```python
import jax
import jax.numpy as jnp
from jax import lax
from jax.sharding import PartitionSpec as P

HEAD_SIZE = 64
FFE = 512
TOP = 8


EPSILON = 1e-06
SCORE_SCALE = 1.0 / 64.0
RESIDUAL = 0.22
THETA = 10000.0
CLIP_LIMIT = 2.0
NEGATIVE = -1e30


def tree_layout(seg_row, par_row):
    tree_length = seg_row.shape[0]
    seg_count = par_row.shape[0]
    seg_index = jnp.arange(seg_count, dtype=jnp.int32)
    member = (seg_row[:, None] == seg_index[None, :]).astype(jnp.int32)
    seg_len = jnp.sum(member, axis=0)
    seg_start = jnp.cumsum(seg_len) - seg_len
    parent_hot = (par_row[:, None] == seg_index[None, :]).astype(jnp.int32)
    grand_parent = jnp.sum(parent_hot * par_row[None, :], axis=1)
    grand_hot = (grand_parent[:, None] == seg_index[None, :]).astype(jnp.int32)
    parent_len = jnp.sum(parent_hot * seg_len[None, :], axis=1)
    grand_len = jnp.sum(grand_hot * seg_len[None, :], axis=1)
    offset = jnp.where(seg_index != 0, parent_len, 0) + jnp.where(par_row != 0, grand_len, 0)
    tok_start = jnp.sum(member * seg_start[None, :], axis=1)
    tok_offset = jnp.sum(member * offset[None, :], axis=1)
    places = jnp.arange(tree_length, dtype=jnp.int32)
    position = (places - tok_start + tok_offset).astype(jnp.float32)
    identity = (seg_index[:, None] == seg_index[None, :]).astype(jnp.int32)
    ancestor = jnp.minimum(identity + parent_hot + grand_hot, 1)
    reached = jnp.dot(member, ancestor)
    linked = jnp.dot(reached, member.T) > 0
    allowed = linked & (places[None, :] <= places[:, None])
    return (position, allowed)


def rope_tables(position, head_dim):
    half_dim = head_dim // 2
    frequency = THETA ** (-2.0 * jnp.arange(half_dim, dtype=jnp.float32) / head_dim)
    angles = position[:, None] * frequency[None, :]
    return (jnp.cos(angles)[:, None, :], jnp.sin(angles)[:, None, :])


def apply_rotary(values_in, cosine_table, sine_values):
    half_dim = values_in.shape[-1] // 2
    first_half = values_in[..., :half_dim]
    second_half = values_in[..., half_dim:]
    return jnp.concatenate(
        [
            first_half * cosine_table - second_half * sine_values,
            second_half * cosine_table + first_half * sine_values,
        ],
        axis=-1,
    )


def rotate_back(grads_in, cosine_table, sine_values):
    half_dim = grads_in.shape[-1] // 2
    first_half = grads_in[..., :half_dim]
    second_half = grads_in[..., half_dim:]
    return jnp.concatenate(
        [
            first_half * cosine_table + second_half * sine_values,
            second_half * cosine_table - first_half * sine_values,
        ],
        axis=-1,
    )


def slot_tables(routes, experts, capacity):
    flat_ids = routes.reshape(-1)
    row_count = flat_ids.shape[0]
    member = (flat_ids[:, None] == jnp.arange(experts, dtype=jnp.int32)[None, :]).astype(jnp.int32)
    before = jnp.cumsum(member, axis=0) - member
    slot_index = jnp.sum(before * member, axis=1)
    target = flat_ids * capacity + slot_index
    source = (
        jnp.full((experts * capacity,), -1, jnp.int32)
        .at[target]
        .set(jnp.arange(row_count, dtype=jnp.int32))
    )
    return (flat_ids, slot_index, source)


def contract_rows(left, right):
    return lax.dot_general(
        left, right, (((0,), (0,)), ((), ())), preferred_element_type=jnp.float32
    )


def contract_cols(left, right):
    return lax.dot_general(
        left, right, (((1,), (1,)), ((), ())), preferred_element_type=jnp.float32
    )


def expert_forward(inputs, gate_w, up_w, down_w):
    gate_pre = jnp.dot(inputs, gate_w, preferred_element_type=jnp.float32)
    up_pre = jnp.dot(inputs, up_w, preferred_element_type=jnp.float32)
    active = (gate_pre / (1.0 + jnp.exp(-gate_pre)) * up_pre).astype(jnp.bfloat16)
    return (contract_cols(active, down_w), (gate_pre, up_pre, active))


def expert_backward(inputs, grads_out, gate_w, up_w, down_w, kept_acts):
    gate_pre, up_pre, active = kept_acts
    d_active = jnp.dot(grads_out, down_w, preferred_element_type=jnp.float32)
    grad_down = contract_rows(grads_out, active)
    sigmoid_val = 1.0 / (1.0 + jnp.exp(-gate_pre))
    d_gate = (d_active * up_pre * sigmoid_val * (1.0 + gate_pre * (1.0 - sigmoid_val))).astype(
        jnp.bfloat16
    )
    d_up = (d_active * gate_pre * sigmoid_val).astype(jnp.bfloat16)
    grad_gate = contract_rows(inputs, d_gate)
    grad_up = contract_rows(inputs, d_up)
    d_inputs = contract_cols(d_gate, gate_w) + contract_cols(d_up, up_w)
    return (d_inputs, grad_gate, grad_up, grad_down)


def send_rows(rows_in):
    return lax.all_to_all(rows_in, "dp", split_axis=0, concat_axis=0, tiled=True)


def return_rows(rows_in):
    return lax.all_to_all(
        rows_in.astype(jnp.bfloat16), "dp", split_axis=0, concat_axis=0, tiled=True
    ).astype(rows_in.dtype)


def send_grads(rows_in):
    return lax.all_to_all(rows_in, "dp", split_axis=0, concat_axis=0, tiled=True)


def return_grads(rows_in):
    return lax.all_to_all(
        rows_in.astype(jnp.bfloat16), "dp", split_axis=0, concat_axis=0, tiled=True
    ).astype(rows_in.dtype)


def share_slots(partial_rows):
    return lax.psum_scatter(partial_rows, "tensor", scatter_dimension=1, tiled=True)


def on_device(
    tokens,
    attn_norm_gain,
    w_query,
    key_projection,
    value_projection,
    w_out,
    moe_norm_gain,
    w_gate,
    w_up,
    w_down,
    router_logits,
    expert_ids,
    segment_ids,
    parents,
    cotangent,
):
    length = tokens.shape[0]
    model_width = tokens.shape[1]
    q_cols = w_query.shape[1]
    kv_cols = key_projection.shape[1]
    q_heads = q_cols // HEAD_SIZE
    kv_heads = kv_cols // HEAD_SIZE
    group_size = q_heads // kv_heads
    dp_size = lax.axis_size("dp")
    tensor_ranks = lax.axis_size("tensor")
    replicas = FFE // (w_gate.shape[2] * tensor_ranks)
    experts = dp_size // replicas
    capacity = 4 * (9 * length * TOP // (32 * experts))
    share_rows = capacity // tensor_ranks
    first_slot = lax.axis_index("tensor") * share_rows
    block_rows = min(length, 512)
    attn_gain, moe_gain, query_w, key_weight, value_weight, out_w = (
        lax.all_gather(attn_norm_gain, "dp", axis=0, tiled=True),
        lax.all_gather(moe_norm_gain, "dp", axis=0, tiled=True),
        lax.all_gather(w_query, "dp", axis=0, tiled=True),
        lax.all_gather(key_projection, "dp", axis=0, tiled=True),
        lax.all_gather(value_projection, "dp", axis=0, tiled=True),
        lax.all_gather(w_out, "dp", axis=0, tiled=True),
    )
    attn_gain_f = attn_gain.astype(jnp.float32)
    moe_gain_f = moe_gain.astype(jnp.float32)
    inputs = tokens.astype(jnp.float32)
    inv_attn = lax.rsqrt(jnp.mean(inputs * inputs, axis=1, keepdims=True) + EPSILON)
    unit_attn = inputs * inv_attn
    normalized_rows = (unit_attn * attn_gain_f).astype(jnp.bfloat16)
    position, allowed = tree_layout(segment_ids[0], parents[0])
    cosine_table, sine_values = rope_tables(position, HEAD_SIZE)
    query_linear = jnp.dot(normalized_rows, query_w, preferred_element_type=jnp.float32).reshape(
        length, q_heads, HEAD_SIZE
    )
    key_linear = jnp.dot(normalized_rows, key_weight, preferred_element_type=jnp.float32).reshape(
        length, kv_heads, HEAD_SIZE
    )
    query_heads = (
        apply_rotary(query_linear, cosine_table, sine_values)
        .astype(jnp.bfloat16)
        .reshape(length, kv_heads, group_size, HEAD_SIZE)
    )
    key_heads = apply_rotary(key_linear, cosine_table, sine_values).astype(jnp.bfloat16)
    value_heads = (
        jnp.dot(normalized_rows, value_weight, preferred_element_type=jnp.float32)
        .astype(jnp.bfloat16)
        .reshape(length, kv_heads, HEAD_SIZE)
    )
    q_block = query_heads
    mask_rows = allowed[None, None]
    scores = (
        jnp.einsum("qhgd,khd->hgqk", q_block, key_heads, preferred_element_type=jnp.float32)
        * SCORE_SCALE
    )
    scores = jnp.where(mask_rows, scores, NEGATIVE)
    peak_parts = [jnp.max(scores, axis=(2, 3))]
    row_max = jnp.max(scores, axis=3, keepdims=True)
    expo = jnp.exp(scores - row_max)
    row_total = jnp.sum(expo, axis=3, keepdims=True)
    lse_parts = [row_max + jnp.log(row_total)]
    prob_low = (expo / row_total).astype(jnp.bfloat16)
    block_outs = jnp.einsum(
        "hgqk,khd->qhgd", prob_low, value_heads, preferred_element_type=jnp.float32
    )
    head_out = block_outs.reshape(length, q_cols).astype(jnp.bfloat16)
    attn_mix = lax.psum(contract_cols(head_out, out_w), "tensor")
    hidden = inputs + RESIDUAL * attn_mix
    head_peak = lax.pmax(jnp.max(jnp.stack(peak_parts), axis=0).reshape(q_heads), "dp")
    inv_moe = lax.rsqrt(jnp.mean(hidden * hidden, axis=1, keepdims=True) + EPSILON)
    unit_moe = hidden * inv_moe
    moe_in = (unit_moe * moe_gain_f).astype(jnp.bfloat16)
    logit_max = jnp.max(router_logits, axis=1, keepdims=True)
    logit_exp = jnp.exp(router_logits - logit_max)
    gate_probs = logit_exp / jnp.sum(logit_exp, axis=1, keepdims=True)
    flat_ids, slot_index, source = slot_tables(expert_ids, experts, capacity)
    filled = source >= 0
    source_row = jnp.maximum(source, 0)
    source_token = source_row // TOP
    dispatch_rows = jnp.where(
        filled[:, None], moe_in[source_token], jnp.zeros((), jnp.bfloat16)
    ).reshape(experts, capacity, model_width)
    arrived = send_rows(jnp.repeat(dispatch_rows, replicas, axis=0))
    gate_w, up_w, down_w = (w_gate[0], w_up[0], w_down[0])
    expert_in = arrived.reshape(dp_size * capacity, model_width)
    expert_out, kept_acts = expert_forward(expert_in, gate_w, up_w, down_w)
    partial_out = share_slots(expert_out.reshape(dp_size, capacity, model_width))
    back_parts = return_rows(partial_out).reshape(experts, replicas, share_rows, model_width)
    back_rows = (
        jnp.sum(back_parts, axis=1).astype(jnp.bfloat16).reshape(experts * share_rows, model_width)
    )
    own_slot = ((slot_index >= first_slot) & (slot_index < first_slot + share_rows)).reshape(
        length, TOP
    )
    local_index = (
        flat_ids * share_rows + jnp.clip(slot_index - first_slot, 0, share_rows - 1)
    ).reshape(length, TOP)
    mix_part = jnp.zeros((length, model_width), jnp.float32)
    for column in range(TOP):
        gate_weight = jnp.where(own_slot[:, column], gate_probs[:, column], 0.0)
        mix_part = mix_part + gate_weight[:, None] * back_rows[local_index[:, column]].astype(
            jnp.float32
        )
    expert_mix = lax.psum(mix_part.astype(jnp.bfloat16), "tensor").astype(jnp.float32)
    output = (hidden + RESIDUAL * expert_mix).astype(jnp.bfloat16)
    grad_output = cotangent.astype(jnp.float32)
    mix_grad = RESIDUAL * grad_output
    row_gate = gate_probs.reshape(-1)[source_row]
    grad_rows = (
        jnp.where(filled[:, None], row_gate[:, None] * mix_grad[source_token], 0.0)
        .astype(jnp.bfloat16)
        .reshape(experts, capacity, model_width)
    )
    grad_arrived = send_grads(jnp.repeat(grad_rows, replicas, axis=0)).reshape(
        dp_size * capacity, model_width
    )
    d_inputs, grad_gate, grad_up, grad_down = expert_backward(
        expert_in, grad_arrived, gate_w, up_w, down_w, kept_acts
    )
    d_back = share_slots(d_inputs.reshape(dp_size, capacity, model_width))
    grad_gate, grad_up, grad_down = (grad_gate[None], grad_up[None], grad_down[None])
    d_parts = return_grads(d_back).reshape(experts, replicas, share_rows, model_width)
    d_returned = (
        jnp.sum(d_parts, axis=1).astype(jnp.bfloat16).reshape(experts * share_rows, model_width)
    )
    d_mix_part = jnp.zeros((length, model_width), jnp.float32)
    for column in range(TOP):
        d_mix_part = d_mix_part + jnp.where(
            own_slot[:, column][:, None],
            d_returned[local_index[:, column]].astype(jnp.float32),
            0.0,
        )
    d_moe_in = lax.psum(d_mix_part, "tensor")
    scaled_moe = d_moe_in * moe_gain_f
    grad_moe_gain = jnp.sum(d_moe_in * unit_moe, axis=0)
    d_hidden = grad_output + inv_moe * (
        scaled_moe - unit_moe * jnp.mean(scaled_moe * unit_moe, axis=1, keepdims=True)
    )
    d_attn = (RESIDUAL * d_hidden).astype(jnp.bfloat16)
    grad_out_w = contract_rows(d_attn, head_out)
    d_heads = (
        jnp.dot(d_attn, out_w, preferred_element_type=jnp.float32)
        .astype(jnp.bfloat16)
        .reshape(length, kv_heads, group_size, HEAD_SIZE)
    )
    d_query_parts = []
    d_key = jnp.zeros((length, kv_heads, HEAD_SIZE), jnp.float32)
    d_value = jnp.zeros((length, kv_heads, HEAD_SIZE), jnp.float32)
    for block_number, row_begin in enumerate(range(0, length, block_rows)):
        q_block = query_heads
        mask_rows = allowed[None, None]
        scores = (
            jnp.einsum("qhgd,khd->hgqk", q_block, key_heads, preferred_element_type=jnp.float32)
            * SCORE_SCALE
        )
        scores = jnp.where(mask_rows, scores, NEGATIVE)
        prob_full = jnp.exp(scores - lse_parts[block_number])
        prob_low = prob_full.astype(jnp.bfloat16)
        d_value = jnp.einsum(
            "hgqk,qhgd->khd", prob_low, d_heads, preferred_element_type=jnp.float32
        )
        d_prob = jnp.einsum(
            "qhgd,khd->hgqk", d_heads, value_heads, preferred_element_type=jnp.float32
        )
        inner = jnp.sum(prob_full * d_prob, axis=3, keepdims=True)
        d_scores = (prob_full * (d_prob - inner)).astype(jnp.bfloat16)
        d_query_parts.append(
            jnp.einsum("hgqk,khd->qhgd", d_scores, key_heads, preferred_element_type=jnp.float32)
            * SCORE_SCALE
        )
        d_key = (
            jnp.einsum("hgqk,qhgd->khd", d_scores, q_block, preferred_element_type=jnp.float32)
            * SCORE_SCALE
        )
    d_query_all = d_query_parts[0].reshape(length, q_heads, HEAD_SIZE)
    d_query_lin = (
        rotate_back(d_query_all, cosine_table, sine_values)
        .astype(jnp.bfloat16)
        .reshape(length, q_cols)
    )
    d_key_lin = (
        rotate_back(d_key, cosine_table, sine_values).astype(jnp.bfloat16).reshape(length, kv_cols)
    )
    d_value_lin = d_value.astype(jnp.bfloat16).reshape(length, kv_cols)
    grad_query_w = contract_rows(normalized_rows, d_query_lin)
    grad_key_w = contract_rows(normalized_rows, d_key_lin)
    grad_value_w = contract_rows(normalized_rows, d_value_lin)
    d_normed_part = (
        contract_cols(d_query_lin, query_w)
        + contract_cols(d_key_lin, key_weight)
        + contract_cols(d_value_lin, value_weight)
    )
    d_normed = lax.psum(d_normed_part.astype(jnp.bfloat16), "tensor").astype(jnp.float32)
    scaled_attn = d_normed * attn_gain_f
    grad_attn_gain = jnp.sum(d_normed * unit_attn, axis=0)
    input_grad = d_hidden + inv_attn * (
        scaled_attn - unit_attn * jnp.mean(scaled_attn * unit_attn, axis=1, keepdims=True)
    )
    reduced = (
        lax.psum_scatter(grad_attn_gain, "dp", scatter_dimension=0, tiled=True),
        lax.psum_scatter(grad_moe_gain, "dp", scatter_dimension=0, tiled=True),
        lax.psum_scatter(grad_query_w, "dp", scatter_dimension=0, tiled=True),
        lax.psum_scatter(grad_key_w, "dp", scatter_dimension=0, tiled=True),
        lax.psum_scatter(grad_value_w, "dp", scatter_dimension=0, tiled=True),
        lax.psum_scatter(grad_out_w, "dp", scatter_dimension=0, tiled=True),
    )
    scale_factor = CLIP_LIMIT / jnp.maximum(head_peak, CLIP_LIMIT)
    query_scale = jnp.repeat(jnp.sqrt(scale_factor), HEAD_SIZE)
    key_clip_scale = jnp.repeat(
        jnp.sqrt(jnp.min(scale_factor.reshape(kv_heads, group_size), axis=1)), HEAD_SIZE
    )
    clipped_query = w_query.astype(jnp.float32) * query_scale[None, :]
    clipped_key = key_projection.astype(jnp.float32) * key_clip_scale[None, :]
    return (
        output,
        input_grad,
        reduced[0],
        reduced[2],
        reduced[3],
        reduced[4],
        reduced[5],
        reduced[1],
        grad_gate,
        grad_up,
        grad_down,
        clipped_query,
        clipped_key,
    )


def solution(mesh):
    in_specs = (
        P("dp", None),
        P("dp"),
        P("dp", "tensor"),
        P("dp", "tensor"),
        P("dp", "tensor"),
        P("dp", "tensor"),
        P("dp"),
        P("dp", None, "tensor"),
        P("dp", None, "tensor"),
        P("dp", None, "tensor"),
        P("dp", None),
        P("dp", None),
        P("dp", None),
        P("dp", None),
        P("dp", None),
    )
    out_specs = (
        P("dp", None),
        P("dp", None),
        P("dp"),
        P("dp", "tensor"),
        P("dp", "tensor"),
        P("dp", "tensor"),
        P("dp", "tensor"),
        P("dp"),
        P("dp", None, "tensor"),
        P("dp", None, "tensor"),
        P("dp", None, "tensor"),
        P("dp", "tensor"),
        P("dp", "tensor"),
    )
    return jax.shard_map(
        on_device, mesh=mesh, in_specs=in_specs, out_specs=out_specs, check_vma=False
    )
```

profile of v0, /device:TPU:0, one launch (start us, length us, event | category | flops | bytes accessed | tf_op | source)
XLA Modules:
  0.0 1112.5 jit_solution(12546597469218034380)
XLA Ops:
  14.2 44.3 %all-reduce.5 = (bf16[1536]{0:T(1024)(128)(2,1)S(1)}, bf16[1536]{0:T(1024)(128)(2,1)S(1)}) all-reduce(bf16[1536]{0:T(1024)(128)(2,1)S(1)} %dynamic-update-slice, bf16[1536]{0:T(1024)(128)(2,1)S(1)} %dynamic-update-slice.1), channel_id=1, replica_groups=mesh['dp'=16,'tensor'=2] {'dp'}, use_global_device_ids=true, to_apply=%add | all-reduce | flops 3072 | bytes 12288
  61.0 4.5 reduce-window.19
  67.3 43.1 %all_gather.19 = bf16[1536,256]{1,0:T(8,128)(2,1)S(1)} all-gather(bf16[96,256]{1,0:T(8,128)(2,1)} %param.19), channel_id=1, replica_groups=mesh['dp'=16,'tensor'=2] {'dp'}, dimensions={0}, use_global_device_ids=true | all-gather | bytes 835584 | tf_op jit(solution)/shard_map/all_gather | solution.py:187
  112.9 45.3 %all_gather.20 = bf16[1536,256]{1,0:T(8,128)(2,1)S(1)} all-gather(bf16[96,256]{1,0:T(8,128)(2,1)S(1)} %copy-done.37), channel_id=1, replica_groups=mesh['dp'=16,'tensor'=2] {'dp'}, dimensions={0}, use_global_device_ids=true | all-gather | bytes 835584 | tf_op jit(solution)/shard_map/all_gather | solution.py:186
  159.7 2.7 fusion.90
  164.1 3.5 fusion.100
  167.9 4.3 scatter_custom_fusion
  172.3 10.5 all-reduce.11.cloned.1.call-done
  185.3 5.3 gather_fusion
  190.6 4.2 broadcast_select_fusion
  194.8 7.0 all-to-all-start
  202.1 4.6 gather_fusion.9
  206.8 5.7 gather_fusion.10
  212.5 4.7 select_convert_fusion
  217.2 53.1 %all-to-all-done = bf16[16,72,1536]{2,1,0:T(8,128)(2,1)} async-done(((bf16[16,72,1536]{2,1,0:T(8,128)(2,1)}), bf16[16,72,1536]{2,1,0:T(8,128)(2,1)}, u32[]{:S(2)}, u32[]{:S(2)}) %all-to-all-start) | async-done | bytes 3538976 | tf_op jit(solution)/shard_map/all_to_all | solution.py:127
  270.3 17.8 %all-to-all-start.2 = ((bf16[16,72,1536]{2,1,0:T(8,128)(2,1)}), bf16[16,72,1536]{2,1,0:T(8,128)(2,1)}, u32[]{:S(2)}, u32[]{:S(2)}) async-start(bf16[16,72,1536]{2,1,0:T(8,128)(2,1)} %select_convert_fusion), calls=%async_computation.3 | async-start | bytes 7077888 | tf_op jit(solution)/shard_map/all_to_all | solution.py:137
  288.5 4.2 fusion.26
  292.6 4.1 fusion.30
  296.7 58.9 %all-to-all-done.2 = bf16[16,72,1536]{2,1,0:T(8,128)(2,1)} async-done(((bf16[16,72,1536]{2,1,0:T(8,128)(2,1)}), bf16[16,72,1536]{2,1,0:T(8,128)(2,1)}, u32[]{:S(2)}, u32[]{:S(2)}) %all-to-all-start.2) | async-done | bytes 3538976 | tf_op jit(solution)/shard_map/all_to_all | solution.py:137
  355.6 4.9 multiply_convert_fusion
  362.8 7.0 copy.171
  370.9 4.0 fusion.21
  374.9 21.0 %reduce-scatter.9.cloned.1.call-done = f32[16,36,1536]{2,0,1:T(8,128)} async-done(((f32[16,72,1536]{2,0,1:T(8,128)}), f32[16,36,1536]{2,0,1:T(8,128)}) %reduce-scatter.9.cloned.1.call-update) | async-done | bytes 3538960 | tf_op jit(solution)/shard_map/reduce_scatter | solution.py:147
  395.9 2.3 convert_element_type.225
  398.2 2.3 copy.172
  400.5 17.2 %all-to-all-start.3 = ((bf16[16,36,1536]{2,1,0:T(8,128)(2,1)}), bf16[16,36,1536]{2,1,0:T(8,128)(2,1)S(1)}, u32[]{:S(2)}, u32[]{:S(2)}) async-start(bf16[16,36,1536]{2,1,0:T(8,128)(2,1)} %copy.172), calls=%async_computation.5 | async-start | bytes 3932160 | tf_op jit(solution)/shard_map/all_to_all | solution.py:141
  417.8 2.3 convert_element_type.208
  420.0 2.3 copy.161
  422.3 36.4 %all-to-all-done.3 = bf16[16,36,1536]{2,1,0:T(8,128)(2,1)S(1)} async-done(((bf16[16,36,1536]{2,1,0:T(8,128)(2,1)}), bf16[16,36,1536]{2,1,0:T(8,128)(2,1)S(1)}, u32[]{:S(2)}, u32[]{:S(2)}) %all-to-all-start.3) | async-done | bytes 1769504 | tf_op jit(solution)/shard_map/all_to_all | solution.py:141
  458.7 9.9 all-to-all-start.1
  472.8 2.4 convert_element_type.226
  487.9 3.2 select_add_fusion
  491.2 18.0 %all-to-all-done.1 = bf16[16,36,1536]{2,1,0:T(8,128)(2,1)} async-done(((bf16[16,36,1536]{2,1,0:T(8,128)(2,1)}), bf16[16,36,1536]{2,1,0:T(8,128)(2,1)}, u32[]{:S(2)}, u32[]{:S(2)}) %all-to-all-start.1) | async-done | bytes 1769504 | tf_op jit(solution)/shard_map/all_to_all | solution.py:131
  509.2 2.5 convert_element_type.209
  524.4 3.1 add_convert_fusion.1
  527.5 2.2 multiply_reduce_fusion
  540.7 3.0 fusion.88
  544.7 3.0 fusion.37
  548.7 4.4 convolution_bitcast_fusion
  553.2 4.4 convolution_bitcast_fusion.1
  557.7 4.5 convolution_bitcast_fusion.2
  562.2 44.1 %pmax.7 = f32[12]{0:T(128)S(1)} all-reduce(f32[12]{0:T(128)S(1)} %reshape.335), channel_id=1, replica_groups=mesh['dp'=16,'tensor'=2] {'dp'}, use_global_device_ids=true, to_apply=%region_35.36 | all-reduce | flops 12 | bytes 96 | tf_op jit(solution)/shard_map/pmax | solution.py:234
  609.7 72.1 %all-reduce.4 = (f32[1536]{0:T(1024)S(1)}, f32[1536]{0:T(1024)S(1)}) all-reduce(f32[1536]{0:T(1024)S(1)} %get-tuple-element.15, f32[1536]{0:T(1024)S(1)} %copy-done.50), channel_id=4, replica_groups=mesh['dp'=16,'tensor'=2] {'dp'}, use_global_device_ids=true, to_apply=%region_27.28.clone | all-reduce | flops 3072 | bytes 24576
  683.0 1.8 add_convert_fusion
  686.0 5.9 reduce-scatter.15.cloned.1.call-done
  691.9 129.6 %reduce-scatter.13.cloned.1.call-done = f32[96,256]{1,0:T(8,128)} async-done(((f32[1536,256]{1,0:T(8,128)}), f32[96,256]{1,0:T(8,128)}) %reduce-scatter.13.cloned.1.call-update) | async-done | bytes 98320 | tf_op jit(solution)/shard_map/reduce_scatter | solution.py:368
  821.5 142.0 %reduce-scatter.11.cloned.1.call-done = f32[96,768]{1,0:T(8,128)} async-done(((f32[1536,768]{1,0:T(8,128)}), f32[96,768]{1,0:T(8,128)}) %reduce-scatter.11.cloned.1.call-update) | async-done | bytes 294928 | tf_op jit(solution)/shard_map/reduce_scatter | solution.py:367
  963.5 142.3 %reduce-scatter.17.cloned.1.call-done = f32[96,768]{1,0:T(8,128)} async-done(((f32[1536,768]{1,0:T(8,128)}), f32[96,768]{1,0:T(8,128)}) %reduce-scatter.17.cloned.1.call-update) | async-done | bytes 294928 | tf_op jit(solution)/shard_map/reduce_scatter | solution.py:370
  (329 shorter events, 69.9 us)
Async XLA Ops:
  7.2 348.4 %copy-start = (bf16[1,1536,256]{2,1,0:T(8,128)(2,1)S(1)}, bf16[1,1536,256]{2,1,0:T(8,128)(2,1)}, u32[]{:S(2)}) copy-start(bf16[1,1536,256]{2,1,0:T(8,128)(2,1)} %param.24) | copy-start | bytes 2359300
  7.2 104.9 %copy-start.53 = (s32[128,8]{0,1:T(8,128)S(1)}, s32[128,8]{0,1:T(8,128)}, u32[]{:S(2)}) copy-start(s32[128,8]{0,1:T(8,128)} %param.26) | copy-start | bytes 12292
  7.2 104.8 %copy-start.84 = (s32[1,128]{1,0:T(1,128)S(1)}, s32[1,128]{1,0:T(1,128)}, u32[]{:S(2)}) copy-start(s32[1,128]{1,0:T(1,128)} %param.27) | copy-start | bytes 1540
  7.2 104.8 %copy-start.75 = (s32[1,13]{1,0:T(1,128)S(1)}, s32[1,13]{1,0:T(1,128)}, u32[]{:S(2)}) copy-start(s32[1,13]{1,0:T(1,128)} %param.28) | copy-start | bytes 160
  7.2 104.1 %copy-start.2 = (bf16[128,1536]{1,0:T(8,128)(2,1)S(1)}, bf16[128,1536]{1,0:T(8,128)(2,1)}, u32[]{:S(2)}) copy-start(bf16[128,1536]{1,0:T(8,128)(2,1)} %param.15) | copy-start | bytes 1179652
  7.2 105.7 %copy-start.37 = (bf16[96,256]{1,0:T(8,128)(2,1)S(1)}, bf16[96,256]{1,0:T(8,128)(2,1)}, u32[]{:S(2)}) copy-start(bf16[96,256]{1,0:T(8,128)(2,1)} %param.18) | copy-start | bytes 147460
  7.3 152.4 %all-gather.3.cloned.1.call-start = ((), (), s32[]{:S(2)}) async-start(), calls=%async_computation.10 | async-start | bytes 2506752 | tf_op jit(solution)/shard_map/all_gather | solution.py:185
  8.0 156.1 %all-gather.5.cloned.1.call-start = ((), (), s32[]{:S(2)}) async-start(), calls=%async_computation.11 | async-start | bytes 2506752 | tf_op jit(solution)/shard_map/all_gather | solution.py:188
  8.7 174.1 %all-reduce.11.cloned.1.call-start = ((), (), s32[]{:S(2)}) async-start(), calls=%async_computation.12 | async-start | bytes 1572864 | tf_op jit(solution)/shard_map/psum | solution.py:232
  67.3 92.4 %copy-start.51 = (f32[128]{0:T(128)}, f32[128]{0:T(128)S(1)}, u32[]{:S(2)}) copy-start(f32[128]{0:T(128)S(1)} %add_rsqrt_fusion.1) | copy-start | bytes 1540
  111.8 51.4 %copy-start.35 = (bf16[128,256]{0,1:T(8,128)(2,1)}, bf16[128,256]{0,1:T(8,128)(2,1)S(1)}, u32[]{:S(2)}) copy-start(bf16[128,256]{0,1:T(8,128)(2,1)S(1)} %copy.149) | copy-start | bytes 196612
  112.9 49.5 %copy-start.27 = (f32[128,32]{0,1:T(8,128)}, f32[128,32]{0,1:T(8,128)S(1)}, u32[]{:S(2)}) copy-start(f32[128,32]{0,1:T(8,128)S(1)} %get-tuple-element.72) | copy-start | bytes 49156
  112.9 49.5 %copy-start.29 = (f32[128,32]{0,1:T(8,128)}, f32[128,32]{0,1:T(8,128)S(1)}, u32[]{:S(2)}) copy-start(f32[128,32]{0,1:T(8,128)S(1)} %get-tuple-element.73) | copy-start | bytes 49156
  162.9 4.7 copy-start.46
  164.1 20.2 %copy-start.18 = (bf16[4,64,3,128]{3,1,2,0:T(8,128)(2,1)}, bf16[4,64,3,128]{3,1,2,0:T(8,128)(2,1)S(1)}, u32[]{:S(2)}) copy-start(bf16[4,64,3,128]{3,1,2,0:T(8,128)(2,1)S(1)} %convolution_convert_fusion.1) | copy-start | bytes 589828
  167.6 22.9 %copy-start.39 = (f32[1536]{0:T(1024)}, f32[1536]{0:T(1024)S(1)}, u32[]{:S(2)}) copy-start(f32[1536]{0:T(1024)S(1)} %convert_element_type.205) | copy-start | bytes 18436
  184.3 6.3 copy-start.57
  194.8 7.0 copy-start.45
  194.8 75.5 %all-to-all-start = ((bf16[16,72,1536]{2,1,0:T(8,128)(2,1)}), bf16[16,72,1536]{2,1,0:T(8,128)(2,1)}, u32[]{:S(2)}, u32[]{:S(2)}) async-start(bf16[16,72,1536]{2,1,0:T(8,128)(2,1)} %broadcast_select_fusion), calls=%async_computation | async-start | bytes 7077888 | tf_op jit(solution)/shard_map/all_to_all | solution.py:127
  217.2 71.3 %copy-start.21 = (bf16[1,1536,256]{2,1,0:T(8,128)(2,1)S(1)}, bf16[1,1536,256]{2,1,0:T(8,128)(2,1)}, u32[]{:S(2)}) copy-start(bf16[1,1536,256]{2,1,0:T(8,128)(2,1)} %param.23) | copy-start | bytes 2359300
  270.3 85.3 %all-to-all-start.2 = ((bf16[16,72,1536]{2,1,0:T(8,128)(2,1)}), bf16[16,72,1536]{2,1,0:T(8,128)(2,1)}, u32[]{:S(2)}, u32[]{:S(2)}) async-start(bf16[16,72,1536]{2,1,0:T(8,128)(2,1)} %select_convert_fusion), calls=%async_computation.3 | async-start | bytes 7077888 | tf_op jit(solution)/shard_map/all_to_all | solution.py:137
  288.1 107.8 %reduce-scatter.9.cloned.1.call-start = ((), (), s32[]{:S(2)}) async-start(), calls=%async_computation.14 | async-start | bytes 10616832 | tf_op jit(solution)/shard_map/reduce_scatter | solution.py:147
  369.9 47.9 %reduce-scatter.7.cloned.1.call-start = ((), (), s32[]{:S(2)}) async-start(), calls=%async_computation.13 | async-start | bytes 10616832 | tf_op jit(solution)/shard_map/reduce_scatter | solution.py:147
  400.5 58.2 %all-to-all-start.3 = ((bf16[16,36,1536]{2,1,0:T(8,128)(2,1)}), bf16[16,36,1536]{2,1,0:T(8,128)(2,1)S(1)}, u32[]{:S(2)}, u32[]{:S(2)}) async-start(bf16[16,36,1536]{2,1,0:T(8,128)(2,1)} %copy.172), calls=%async_computation.5 | async-start | bytes 3932160 | tf_op jit(solution)/shard_map/all_to_all | solution.py:141
  422.3 47.4 %copy-start.54 = (s32[128,8]{0,1:T(8,128)S(1)}, s32[128,8]{0,1:T(8,128)}, u32[]{:S(2)}) copy-start(s32[128,8]{0,1:T(8,128)} %get-tuple-element.70) | copy-start | bytes 12292
  458.7 13.5 %copy-start.9 = (bf16[16,36,1536]{2,1,0:T(8,128)(2,1)}, bf16[16,36,1536]{2,1,0:T(8,128)(2,1)S(1)}, u32[]{:S(2)}) copy-start(bf16[16,36,1536]{2,1,0:T(8,128)(2,1)S(1)} %all-to-all-done.3) | copy-start | bytes 5308420
  458.7 50.4 %all-to-all-start.1 = ((bf16[16,36,1536]{2,1,0:T(8,128)(2,1)}), bf16[16,36,1536]{2,1,0:T(8,128)(2,1)}, u32[]{:S(2)}, u32[]{:S(2)}) async-start(bf16[16,36,1536]{2,1,0:T(8,128)(2,1)} %copy.161), calls=%async_computation.2 | async-start | bytes 3932160 | tf_op jit(solution)/shard_map/all_to_all | solution.py:131
  468.6 58.9 %all-reduce.13.cloned.1.call-start = ((), (), s32[]{:S(2)}) async-start(), calls=%async_computation.15 | async-start | bytes 1572864 | tf_op jit(solution)/shard_map/psum | solution.py:298
  469.1 6.2 copy-start.59
  469.2 6.1 copy-start.61
  469.3 6.0 copy-start.63
  469.4 5.9 copy-start.65
  469.4 5.8 copy-start.67
  469.5 5.7 copy-start.69
  469.6 5.6 copy-start.71
  469.7 5.5 copy-start.73
  470.4 15.8 %copy-start.55 = (s32[1024]{0:T(1024)}, s32[1024]{0:T(1024)S(1)}, u32[]{:S(2)}) copy-start(s32[1024]{0:T(1024)S(1)} %get-tuple-element.88) | copy-start | bytes 12292
  471.0 5.2 copy-start.56
  491.1 117.1 %all-reduce.15.cloned.1.call-start = ((), (), s32[]{:S(2)}) async-start(), calls=%async_computation.20 | async-start | bytes 1572864 | tf_op jit(solution)/shard_map/psum | solution.py:269
  537.2 154.8 %reduce-scatter.15.cloned.1.call-start = ((), (), s32[]{:S(2)}) async-start(), calls=%async_computation.18 | async-start | bytes 1671168 | tf_op jit(solution)/shard_map/reduce_scatter | solution.py:369
  539.0 282.6 %reduce-scatter.13.cloned.1.call-start = ((), (), s32[]{:S(2)}) async-start(), calls=%async_computation.17 | async-start | bytes 1671168 | tf_op jit(solution)/shard_map/reduce_scatter | solution.py:368
  540.7 422.9 %reduce-scatter.11.cloned.1.call-start = ((), (), s32[]{:S(2)}) async-start(), calls=%async_computation.16 | async-start | bytes 5013504 | tf_op jit(solution)/shard_map/reduce_scatter | solution.py:367
  543.8 562.0 %reduce-scatter.17.cloned.1.call-start = ((), (), s32[]{:S(2)}) async-start(), calls=%async_computation.19 | async-start | bytes 5013504 | tf_op jit(solution)/shard_map/reduce_scatter | solution.py:370
  557.7 49.1 %copy-start.38 = (bf16[96,256]{1,0:T(8,128)(2,1)S(1)}, bf16[96,256]{1,0:T(8,128)(2,1)}, u32[]{:S(2)}) copy-start(bf16[96,256]{1,0:T(8,128)(2,1)} %param.18) | copy-start | bytes 147460
  557.7 49.8 %copy-start.24 = (bf16[96,768]{1,0:T(8,128)(2,1)S(1)}, bf16[96,768]{1,0:T(8,128)(2,1)}, u32[]{:S(2)}) copy-start(bf16[96,768]{1,0:T(8,128)(2,1)} %param.17) | copy-start | bytes 442372
  557.7 52.0 %copy-start.50 = (f32[1536]{0:T(1024)S(1)}, f32[1536]{0:T(1024)}, u32[]{:S(2)}) copy-start(f32[1536]{0:T(1024)} %get-tuple-element.13) | copy-start | bytes 18436
  608.2 76.6 %copy-start.15 = (bf16[128,1536]{1,0:T(8,128)(2,1)S(1)}, bf16[128,1536]{1,0:T(8,128)(2,1)}, u32[]{:S(2)}) copy-start(bf16[128,1536]{1,0:T(8,128)(2,1)} %get-tuple-element.28) | copy-start | bytes 1179652
  608.2 497.6 %copy-start.1 = (bf16[1,1536,256]{2,1,0:T(8,128)(2,1)S(1)}, bf16[1,1536,256]{2,1,0:T(8,128)(2,1)}, u32[]{:S(2)}) copy-start(bf16[1,1536,256]{2,1,0:T(8,128)(2,1)} %param.24) | copy-start | bytes 2359300
  (52 other events, 102.1 us)
Sparse Core Ops, SparseCore 0:
  10.9 70.5 all-gather.2
  84.3 64.4 all-gather.4
  167.8 15.0 all-reduce.10
  370.0 25.8 reduce-scatter.8
  398.1 16.4 reduce-scatter.6
  491.2 20.4 all-reduce.12
  537.3 22.6 all-reduce.14
  566.1 125.7 reduce-scatter.14
  698.0 123.4 reduce-scatter.12
  827.9 135.5 reduce-scatter.10
  969.3 136.4 reduce-scatter.16
where the time goes:
time: 1120 us; the launch traced here: 1110 us
  waiting for transfers between devices  619 us (55%)
  blocking collectives  249 us (22%)
  local copies, waits for them, and re-layouts  76.5 us (7%)
  matrix products  55 us (5%)
  starting transfers between devices  52.8 us (5%)
  other arithmetic  43.1 us (4%)
  between operations  16.8 us (2%)
    reduce_scatter x1, waiting for transfers between devices, on_device(): lax.psum_scatter(grad_out_w, 'dp', scatter_dimension=0, tiled=True)  142 us
    reduce_scatter x1, waiting for transfers between devices, on_device(): lax.psum_scatter(grad_query_w, 'dp', scatter_dimension=0, tiled=True)  142 us
    reduce_scatter x1, waiting for transfers between devices, on_device(): lax.psum_scatter(grad_key_w, 'dp', scatter_dimension=0, tiled=True)  130 us
    unnamed x2, blocking collectives  116 us
    all_to_all x1, waiting for transfers between devices, send_grads(): lax.all_to_all(rows_in, 'dp', split_axis=0, concat_axis=0, tiled=True)  58.9 us
    all_to_all x1, waiting for transfers between devices, send_rows(): lax.all_to_all(rows_in, 'dp', split_axis=0, concat_axis=0, tiled=True)  53.1 us
    all_gather x1, blocking collectives, on_device(): lax.all_gather(key_projection, 'dp', axis=0, tiled=True)  45.3 us
    pmax x1, blocking collectives, on_device(): lax.pmax(jnp.max(jnp.stack(peak_parts), axis=0).reshape(q_heads), 'dp')  44.1 us
  transfers between devices with their start and end apart: 15, of which 10 were waited for; matrix products, arithmetic and copies ran while one was open for 12% of the time, Pallas kernels for 0%

commit v1 on v0

--- a/solution.py
+++ b/solution.py
@@ -1,6 +1,10 @@
+import functools
+
 import jax
 import jax.numpy as jnp
 from jax import lax
+from jax.experimental import pallas as pl
+from jax.experimental.pallas import tpu as pltpu
 from jax.sharding import PartitionSpec as P
 
 HEAD_SIZE = 64
@@ -22,7 +26,7 @@
     seg_index = jnp.arange(seg_count, dtype=jnp.int32)
     member = (seg_row[:, None] == seg_index[None, :]).astype(jnp.int32)
     seg_len = jnp.sum(member, axis=0)
-    seg_start = jnp.cumsum(seg_len) - seg_len
+    seg_start = jnp.sum(jnp.where(seg_index[:, None] > seg_index[None, :], seg_len[None, :], 0), axis=1)
     parent_hot = (par_row[:, None] == seg_index[None, :]).astype(jnp.int32)
     grand_parent = jnp.sum(parent_hot * par_row[None, :], axis=1)
     grand_hot = (grand_parent[:, None] == seg_index[None, :]).astype(jnp.int32)
@@ -78,7 +82,8 @@
     flat_ids = routes.reshape(-1)
     row_count = flat_ids.shape[0]
     member = (flat_ids[:, None] == jnp.arange(experts, dtype=jnp.int32)[None, :]).astype(jnp.int32)
-    before = jnp.cumsum(member, axis=0) - member
+    row_total = flat_ids.shape[0]
+    before = jnp.dot((jnp.arange(row_total)[:, None] > jnp.arange(row_total)[None, :]).astype(jnp.float32), member.astype(jnp.float32), precision=lax.Precision.HIGHEST).astype(jnp.int32)
     slot_index = jnp.sum(before * member, axis=1)
     target = flat_ids * capacity + slot_index
     source = (
@@ -147,7 +152,7 @@
     return lax.psum_scatter(partial_rows, "tensor", scatter_dimension=1, tiled=True)
 
 
-def on_device(
+def on_device_general(
     tokens,
     attn_norm_gain,
     w_query,
@@ -393,6 +398,890 @@
     )
 
 
+MESH_IDS = pl.DeviceIdType.MESH
+F32 = jnp.float32
+BF16 = jnp.bfloat16
+
+
+class Place:
+    def __init__(self, line):
+        self.line = line
+        self.count = 4 * line
+        me = lax.axis_index("dp")
+        self.core = lax.axis_index("tensor")
+        self.me = me
+        self.z = me // 4
+        y, x = (me // 2) % 2, me % 2
+        self.step_a, self.step_b = 2 - self.core, 1 + self.core
+        self.a = y * (1 - self.core) + x * self.core
+        self.b = x * (1 - self.core) + y * self.core
+
+    def part(self, z, a, b):
+        return z * 4 + a * self.step_a + b * self.step_b
+
+    def up(self):
+        return (self.me + 4, self.core)
+
+    def down(self):
+        return (self.me - 4, self.core)
+
+    def beside_a(self):
+        return (self.me + self.step_a * (1 - 2 * self.a), self.core)
+
+    def beside_b(self):
+        return (self.me + self.step_b * (1 - 2 * self.b), self.core)
+
+    def twin(self):
+        return (self.me, 1 - self.core)
+
+    def peer(self, offset):
+        return lax.rem(self.me + offset, self.count)
+
+
+def enter(place):
+    barrier = pltpu.get_barrier_semaphore()
+
+    def greet(offset, carry):
+        pl.semaphore_signal(
+            barrier, inc=1, device_id=(place.peer(offset), place.core), device_id_type=MESH_IDS
+        )
+        return carry
+
+    lax.fori_loop(1, place.count, greet, 0)
+    pl.semaphore_signal(barrier, inc=1, device_id=place.twin(), device_id_type=MESH_IDS)
+    pl.semaphore_wait(barrier, place.count)
+
+
+def remote(src, dst, send_sem, recv_sem, device):
+    return pltpu.make_async_remote_copy(
+        src_ref=src,
+        dst_ref=dst,
+        send_sem=send_sem,
+        recv_sem=recv_sem,
+        device_id=device,
+        device_id_type=MESH_IDS,
+    )
+
+
+class Notes:
+    def __init__(self, place, src, dst, send_sem, recv_sem, alike):
+        self.place, self.src, self.dst = place, src, dst
+        self.send_sem, self.recv_sem, self.alike = send_sem, recv_sem, alike
+
+    def _copy(self, offset, source):
+        place = self.place
+        to = place.peer(offset)
+        return remote(
+            self.src if self.alike else self.src.at[to],
+            self.dst.at[source],
+            self.send_sem.at[offset],
+            self.recv_sem.at[source],
+            (to, place.core),
+        )
+
+    def start(self):
+        def send(offset, carry):
+            self._copy(offset, self.place.me).start()
+            return carry
+
+        lax.fori_loop(1, self.place.count, send, 0)
+        me = self.place.me
+        self.dst[me] = self.src[...] if self.alike else self.src[me]
+
+    def finish(self):
+        def settle(offset, carry):
+            self._copy(offset, self.place.peer(offset)).wait_recv()
+            self._copy(offset, self.place.me).wait_send()
+            return carry
+
+        lax.fori_loop(1, self.place.count, settle, 0)
+
+
+class Gather:
+    def __init__(self, place, view, send_sem, recv_sem):
+        self.place, self.view = place, view
+        self.send_sem, self.recv_sem = send_sem, recv_sem
+
+    def _copy(self, part, way):
+        place, line = self.place, self.place.line
+        z = part // 4
+        if way == "up":
+            slot, device = z, place.up()
+        elif way == "down":
+            slot, device = line + z, place.down()
+        elif way == "a":
+            slot, device = 2 * line + z, place.beside_a()
+        else:
+            slot, device = 3 * line + part - place.b * place.step_b, place.beside_b()
+        ref = self.view(part)
+        return remote(ref, ref, self.send_sem.at[slot], self.recv_sem.at[part], device)
+
+    def _await(self, part):
+        self._copy(part, "b").wait_recv()
+
+    def start(self):
+        place = self.place
+        me, last = place.me, place.line - 1
+
+        @pl.when(place.z < last)
+        def _():
+            self._copy(me, "up").start()
+
+        @pl.when(place.z > 0)
+        def _():
+            self._copy(me, "down").start()
+
+        self._copy(me, "a").start()
+        self._copy(me, "b").start()
+
+    def along(self, step):
+        place = self.place
+        last = place.line - 1
+        below = place.part(place.z - step, place.a, place.b)
+        above = place.part(place.z + step, place.a, place.b)
+
+        @pl.when(place.z >= step)
+        def _():
+            self._await(below)
+
+            @pl.when(place.z < last)
+            def _():
+                self._copy(below, "up").start()
+
+            self._copy(below, "a").start()
+            self._copy(below, "b").start()
+
+        @pl.when(place.z + step <= last)
+        def _():
+            self._await(above)
+
+            @pl.when(place.z > 0)
+            def _():
+                self._copy(above, "down").start()
+
+            self._copy(above, "a").start()
+            self._copy(above, "b").start()
+
+    def across(self, step):
+        place = self.place
+
+        def take(z):
+            part = place.part(z, 1 - place.a, place.b)
+            self._await(part)
+            self._copy(part, "b").start()
+
+        if step == 0:
+            take(place.z)
+        else:
+            pl.when(place.z >= step)(lambda: take(place.z - step))
+            pl.when(place.z + step < place.line)(lambda: take(place.z + step))
+
+    def finish(self):
+        place, last = self.place, self.place.line - 1
+
+        def settle(z, carry):
+            for a in (0, 1):
+                self._await(place.part(z, a, 1 - place.b))
+                self._copy(place.part(z, a, place.b), "b").wait_send()
+            self._copy(place.part(z, place.a, place.b), "a").wait_send()
+            own = place.part(z, place.a, place.b)
+
+            @pl.when(jnp.logical_and(z <= place.z, place.z < last))
+            def _():
+                self._copy(own, "up").wait_send()
+
+            @pl.when(jnp.logical_and(z >= place.z, place.z > 0))
+            def _():
+                self._copy(own, "down").wait_send()
+
+            return carry
+
+        lax.fori_loop(0, place.line, settle, 0)
+
+
+def gather_all(gathers):
+    line = gathers[0].place.line
+    for g in gathers:
+        g.start()
+    for step in range(1, line + 1):
+        for g in gathers:
+            if step < line:
+                g.along(step)
+            g.across(step - 1)
+    for g in gathers:
+        g.finish()
+
+
+class Reduce:
+    def __init__(self, place, parts, from_b, from_a, from_z, sems):
+        self.place, self.parts = place, parts
+        self.from_b, self.from_a, self.from_z = from_b, from_a, from_z
+        self.send_sem, self.recv_sem = sems
+
+    def _to_b(self, z, a, slot=None):
+        place, line = self.place, self.place.line
+        slot = z * 2 + a
+        return remote(
+            self.parts.at[place.part(z, a, 1 - place.b)],
+            self.from_b.at[slot],
+            self.send_sem.at[slot],
+            self.recv_sem.at[slot],
+            place.beside_b(),
+        )
+
+    def _to_a(self, z):
+        place, line = self.place, self.place.line
+        return remote(
+            self.parts.at[place.part(z, 1 - place.a, place.b)],
+            self.from_a.at[z],
+            self.send_sem.at[2 * line + z],
+            self.recv_sem.at[2 * line + z],
+            place.beside_a(),
+        )
+
+    def _along(self, z, way):
+        place, line = self.place, self.place.line
+        slot = way * line + z
+        return remote(
+            self.parts.at[place.part(z, place.a, place.b)],
+            self.from_z.at[slot],
+            self.send_sem.at[3 * line + slot],
+            self.recv_sem.at[3 * line + slot],
+            place.up() if way == 0 else place.down(),
+        )
+
+    def _add(self, part, block):
+        self.parts[part] = (self.parts[part].astype(F32) + block.astype(F32)).astype(BF16)
+
+    def send_b(self, z, a):
+        self._to_b(z, a).start()
+
+    def fold_b(self, z, a):
+        self._to_b(z, a).wait_recv()
+        self._add(self.place.part(z, a, self.place.b), self.from_b[z * 2 + a])
+
+    def send_a(self, z):
+        self._to_a(z).start()
+
+    def fold_a(self, z):
+        self._to_a(z).wait_recv()
+        self._add(self.place.part(z, self.place.a, self.place.b), self.from_a[z])
+
+    def pass_up(self, z):
+        place = self.place
+
+        @pl.when(place.z < z)
+        def _():
+            @pl.when(place.z > 0)
+            def _():
+                self._along(z, 0).wait_recv()
+                self._add(place.part(z, place.a, place.b), self.from_z[z])
+
+            self._along(z, 0).start()
+
+    def pass_down(self, z):
+        place, line = self.place, self.place.line
+
+        @pl.when(place.z > z)
+        def _():
+            @pl.when(place.z < line - 1)
+            def _():
+                self._along(z, 1).wait_recv()
+                self._add(place.part(z, place.a, place.b), self.from_z[line + z])
+
+            self._along(z, 1).start()
+
+    def result(self, out):
+        place, line = self.place, self.place.line
+        me, z = place.me, place.z
+        out[...] = self.parts[me].astype(F32)
+
+        @pl.when(z > 0)
+        def _():
+            self._along(z, 0).wait_recv()
+            out[...] += self.from_z[z].astype(F32)
+
+        @pl.when(z < line - 1)
+        def _():
+            self._along(z, 1).wait_recv()
+            out[...] += self.from_z[line + z].astype(F32)
+
+    def settle(self):
+        place, line = self.place, self.place.line
+
+        def wait(z, carry):
+            for a in (0, 1):
+                self._to_b(z, a).wait_send()
+            self._to_a(z).wait_send()
+
+            @pl.when(place.z < z)
+            def _():
+                self._along(z, 0).wait_send()
+
+            @pl.when(place.z > z)
+            def _():
+                self._along(z, 1).wait_send()
+
+            return carry
+
+        lax.fori_loop(0, line, wait, 0)
+
+
+def ends_first(line):
+    order = []
+    for i in range((line + 1) // 2):
+        order += [i] if i == line - 1 - i else [i, line - 1 - i]
+    return order
+
+
+def reduce_rest(reduces):
+    line = reduces[0].place.line
+    place = reduces[0].place
+    for r in reduces:
+        for z in ends_first(line):
+            r.fold_b(z, 1 - place.a)
+            r.send_a(z)
+        for z in ends_first(line):
+            r.fold_b(z, place.a)
+        for z in ends_first(line):
+            r.fold_a(z)
+        for k in range(line):
+            r.pass_up(line - 1 - k)
+            r.pass_down(k)
+
+
+def weights_kernel(
+    line,
+    query_ref,
+    key_ref,
+    value_ref,
+    out_ref,
+    cot_ref,
+    note_ref,
+    query_all,
+    key_all,
+    value_all,
+    out_all,
+    cot_all,
+    notes,
+    sends,
+    recvs,
+    note_send,
+    note_recv,
+    twin_sems,
+    local_sems,
+):
+    place = Place(line)
+    half = cot_ref.shape[1] // 2
+    span = pl.ds(pl.multiple_of(place.core * half, 128), half)
+    own = []
+    for i, (src, dst) in enumerate(
+        ((query_ref, query_all), (key_ref, key_all), (value_ref, value_all), (out_ref, out_all), (cot_ref, cot_all))
+    ):
+        own.append(pltpu.make_async_copy(src, dst.at[place.me], local_sems.at[i]))
+        own[-1].start()
+    enter(place)
+    note = Notes(place, note_ref, notes, note_send, note_recv, False)
+    note.start()
+    for c in own:
+        c.wait()
+    gathers = [
+        Gather(place, lambda p, ref=ref: ref.at[p], sends.at[i], recvs.at[i])
+        for i, ref in enumerate((query_all, key_all, value_all, out_all))
+    ]
+    gathers.append(Gather(place, lambda p: cot_all.at[p, :, span], sends.at[4], recvs.at[4]))
+    gather_all(gathers)
+    swap_halves(place, cot_all, span, twin_sems)
+    note.finish()
+
+
+def swap_halves(place, ref, span, sems):
+    def twin(part):
+        view = ref.at[part, :, span]
+        return remote(view, view, sems.at[0, part], sems.at[1, part], place.twin())
+
+    def begin(offset, carry):
+        twin(place.peer(offset)).start()
+        return carry
+
+    def end(offset, carry):
+        copy = twin(place.peer(offset))
+        copy.wait_send()
+        copy.wait_recv()
+        return carry
+
+    lax.fori_loop(1, place.count, begin, 0)
+    lax.fori_loop(1, place.count, end, 0)
+
+
+ANY = pl.BlockSpec(memory_space=pl.ANY)
+IN_VMEM = pl.BlockSpec(memory_space=pltpu.VMEM)
+
+
+def params(number):
+    return pltpu.CompilerParams(
+        collective_id=number, has_side_effects=True, vmem_limit_bytes=56 * 2**20
+    )
+
+
+def gather_weights(line, query, key, value, out, cotangent, note):
+    count = 4 * line
+    shapes = [query.shape, key.shape, value.shape, out.shape, cotangent.shape]
+    return pl.pallas_call(
+        functools.partial(weights_kernel, line),
+        out_shape=[jax.ShapeDtypeStruct((count, *s), BF16) for s in shapes]
+        + [jax.ShapeDtypeStruct(note.shape, F32)],
+        in_specs=[ANY] * 5 + [IN_VMEM],
+        out_specs=[ANY] * 5 + [IN_VMEM],
+        scratch_shapes=[
+            pltpu.SemaphoreType.DMA((5, 3 * line + count)),
+            pltpu.SemaphoreType.DMA((5, count)),
+            pltpu.SemaphoreType.DMA((count,)),
+            pltpu.SemaphoreType.DMA((count,)),
+            pltpu.SemaphoreType.DMA((2, count)),
+            pltpu.SemaphoreType.DMA((5,)),
+        ],
+        compiler_params=params(0),
+        name="gather_weights",
+    )(query, key, value, out, cotangent, note)
+
+
+def rows_kernel(line, rows_ref, rows_all, send, recv, twin_sems, local_sem):
+    place = Place(line)
+    half = rows_ref.shape[1] // 2
+    span = pl.ds(pl.multiple_of(place.core * half, 128), half)
+    own = pltpu.make_async_copy(rows_ref, rows_all.at[place.me], local_sem)
+    own.start()
+    enter(place)
+    own.wait()
+    gather_all([Gather(place, lambda p: rows_all.at[p, :, span], send, recv)])
+    swap_halves(place, rows_all, span, twin_sems)
+
+
+def gather_rows(line, rows):
+    count = 4 * line
+    return pl.pallas_call(
+        functools.partial(rows_kernel, line),
+        out_shape=jax.ShapeDtypeStruct((count, *rows.shape), BF16),
+        in_specs=[ANY],
+        out_specs=ANY,
+        scratch_shapes=[
+            pltpu.SemaphoreType.DMA((3 * line + count,)),
+            pltpu.SemaphoreType.DMA((count,)),
+            pltpu.SemaphoreType.DMA((2, count)),
+            pltpu.SemaphoreType.DMA,
+        ],
+        compiler_params=params(1),
+        name="gather_rows",
+    )(rows)
+
+
+def swap_kernel(line, mine_ref, sum_ref, other, sems):
+    place = Place(line)
+    barrier = pltpu.get_barrier_semaphore()
+    pl.semaphore_signal(barrier, inc=1, device_id=place.twin(), device_id_type=MESH_IDS)
+    pl.semaphore_wait(barrier, 1)
+    copy = remote(mine_ref, other, sems.at[0], sems.at[1], place.twin())
+    copy.start()
+    copy.wait()
+    sum_ref[...] = mine_ref[...].astype(F32) + other[...].astype(F32)
+
+
+def twin_sum(line, number, mine):
+    return pl.pallas_call(
+        functools.partial(swap_kernel, line),
+        out_shape=jax.ShapeDtypeStruct(mine.shape, F32),
+        in_specs=[IN_VMEM],
+        out_specs=IN_VMEM,
+        scratch_shapes=[pltpu.VMEM(mine.shape, mine.dtype), pltpu.SemaphoreType.DMA((2,))],
+        compiler_params=params(number),
+        name="twin_sum",
+    )(mine)
+
+
+def experts_kernel(
+    line,
+    grads_ref,
+    outs_ref,
+    grads_sum,
+    outs_sum,
+    parts,
+    arrived,
+    from_b,
+    from_a,
+    from_z,
+    total,
+    sends,
+    recvs,
+    twin_sems,
+    last_sems,
+    local_sems,
+):
+    place = Place(line)
+    width = grads_ref.shape[2]
+    half = width // 2
+    mine = pl.ds(pl.multiple_of(place.core * half, 128), half)
+    theirs = pl.ds(pl.multiple_of((1 - place.core) * half, 128), half)
+    enter(place)
+    order = [(z, a, b) for b in (1, 0) for a in (1, 0) for z in ends_first(line)]
+
+    def at(spot):
+        z, a, b = spot
+        flip = lambda own, other: own + other * (1 - 2 * own)
+        return place.part(z, flip(place.a, a), flip(place.b, b))
+
+    def load(i, ref, spot):
+        part = at(spot)
+        return pltpu.make_async_copy(ref.at[part, :, mine], parts.at[i, part], local_sems.at[i, part])
+
+    def share(i, ref, spot):
+        part = at(spot)
+        return remote(
+            ref.at[part, :, theirs],
+            arrived.at[i, part],
+            twin_sems.at[i, 0, part],
+            twin_sems.at[i, 1, part],
+            place.twin(),
+        )
+
+    sources = (grads_ref, outs_ref)
+    for i, ref in enumerate(sources):
+        for spot in order:
+            share(i, ref, spot).start()
+            load(i, ref, spot).start()
+    reduces = [
+        Reduce(place, parts.at[i], from_b.at[i], from_a.at[i], from_z.at[i], (sends.at[i], recvs.at[i]))
+        for i in range(2)
+    ]
+    for i, ref in enumerate(sources):
+        for spot in order:
+            part = at(spot)
+            load(i, ref, spot).wait()
+            share(i, ref, spot).wait_recv()
+            reduces[i]._add(part, arrived[i, part])
+            z, a, b = spot
+            if b == 1:
+                reduces[i].send_b(z, place.a + a * (1 - 2 * place.a))
+    reduce_rest(reduces)
+    copies = []
+    for i, out in enumerate((grads_sum, outs_sum)):
+        reduces[i].result(total.at[i])
+        out[:, mine] = total[i]
+        copies.append(
+            remote(total.at[i], out.at[:, mine], last_sems.at[0, i], last_sems.at[1, i], place.twin())
+        )
+        copies[-1].start()
+    for r in reduces:
+        r.settle()
+    for i, ref in enumerate(sources):
+        for spot in order:
+            share(i, ref, spot).wait_send()
+    for c in copies:
+        c.wait()
+
+
+def reduce_experts(line, grads, outs):
+    count, rows, width = grads.shape
+    half = width // 2
+    full = jax.ShapeDtypeStruct((rows, width), F32)
+    return pl.pallas_call(
+        functools.partial(experts_kernel, line),
+        out_shape=[full, full],
+        in_specs=[ANY, ANY],
+        out_specs=[IN_VMEM, IN_VMEM],
+        scratch_shapes=[
+            pltpu.VMEM((2, count, rows, half), BF16),
+            pltpu.VMEM((2, count, rows, half), BF16),
+            pltpu.VMEM((2, 2 * line, rows, half), BF16),
+            pltpu.VMEM((2, line, rows, half), BF16),
+            pltpu.VMEM((2, 2 * line, rows, half), BF16),
+            pltpu.VMEM((2, rows, half), F32),
+            pltpu.SemaphoreType.DMA((2, 5 * line)),
+            pltpu.SemaphoreType.DMA((2, 5 * line)),
+            pltpu.SemaphoreType.DMA((2, 2, count)),
+            pltpu.SemaphoreType.DMA((2, 2)),
+            pltpu.SemaphoreType.DMA((2, count)),
+        ],
+        compiler_params=params(2),
+        name="reduce_experts",
+    )(grads, outs)
+
+
+def grads_kernel(
+    line,
+    query_ref,
+    key_ref,
+    value_ref,
+    out_ref,
+    peak_ref,
+    gain_ref,
+    query_sum,
+    key_sum,
+    value_sum,
+    out_sum,
+    peaks,
+    gains,
+    *scratch,
+):
+    place = Place(line)
+    from_b, from_a, from_z = scratch[0:4], scratch[4:8], scratch[8:12]
+    work = scratch[12:16]
+    sends, recvs, note_sends, note_recvs, local_sems = scratch[16:]
+    loads = [
+        pltpu.make_async_copy(src, dst, local_sems.at[i])
+        for i, (src, dst) in enumerate(zip((query_ref, key_ref, value_ref, out_ref), work))
+    ]
+    for c in loads:
+        c.start()
+    enter(place)
+    notes = [
+        Notes(place, peak_ref, peaks, note_sends.at[0], note_recvs.at[0], True),
+        Notes(place, gain_ref, gains, note_sends.at[1], note_recvs.at[1], False),
+    ]
+    for n in notes:
+        n.start()
+    for c in loads:
+        c.wait()
+    reduces = [
+        Reduce(place, work[i], from_b[i], from_a[i], from_z[i], (sends.at[i], recvs.at[i]))
+        for i in (3, 0, 1, 2)
+    ]
+    for r in reduces:
+        for a in (1 - place.a, place.a):
+            for z in ends_first(line):
+                r.send_b(z, a)
+    reduce_rest(reduces)
+    for r, out in zip(reduces, (out_sum, query_sum, key_sum, value_sum)):
+        r.result(out)
+    for r in reduces:
+        r.settle()
+    for n in notes:
+        n.finish()
+
+
+def reduce_grads(line, grads, peak, gain):
+    count = 4 * line
+    blocks = [g.shape[1:] for g in grads]
+    many = lambda n: [pltpu.VMEM((n, *s), BF16) for s in blocks]
+    return pl.pallas_call(
+        functools.partial(grads_kernel, line),
+        out_shape=[jax.ShapeDtypeStruct(s, F32) for s in blocks]
+        + [jax.ShapeDtypeStruct((count, *peak.shape), F32), jax.ShapeDtypeStruct(gain.shape, F32)],
+        in_specs=[ANY] * 4 + [IN_VMEM] * 2,
+        out_specs=[IN_VMEM] * 6,
+        scratch_shapes=many(2 * line)
+        + many(line)
+        + many(2 * line)
+        + many(count)
+        + [
+            pltpu.SemaphoreType.DMA((4, 5 * line)),
+            pltpu.SemaphoreType.DMA((4, 5 * line)),
+            pltpu.SemaphoreType.DMA((2, count)),
+            pltpu.SemaphoreType.DMA((2, count)),
+            pltpu.SemaphoreType.DMA((4,)),
+        ],
+        compiler_params=params(3),
+        name="reduce_grads",
+    )(*grads, peak, gain)
+
+
+def note_tiles(*rows):
+    tiles = [jnp.pad(r.astype(F32), ((0, 0), (0, 128 - r.shape[1]))) for r in rows]
+    tiles += [jnp.zeros_like(tiles[0])] * (8 - len(tiles))
+    return jnp.stack(tiles, axis=1)
+
+
+def on_device_dense(
+    tokens,
+    attn_norm_gain,
+    w_query,
+    key_projection,
+    value_projection,
+    w_out,
+    moe_norm_gain,
+    w_gate,
+    w_up,
+    w_down,
+    router_logits,
+    expert_ids,
+    segment_ids,
+    parents,
+    cotangent,
+):
+    length, model_width = tokens.shape
+    q_cols, kv_cols = w_query.shape[1], key_projection.shape[1]
+    q_heads, kv_heads = q_cols // HEAD_SIZE, kv_cols // HEAD_SIZE
+    group_size = q_heads // kv_heads
+    count = lax.axis_size("dp")
+    line = count // 4
+    shard = attn_norm_gain.shape[0]
+    logit_max = jnp.max(router_logits, axis=1, keepdims=True)
+    logit_exp = jnp.exp(router_logits - logit_max)
+    gate_probs = logit_exp / jnp.sum(logit_exp, axis=1, keepdims=True)
+    expert_index = jnp.arange(count, dtype=jnp.int32)
+    named = expert_ids[None, :, :] == expert_index[:, None, None]
+    gate_rows = jnp.sum(jnp.where(named, gate_probs[None], 0.0), axis=2)
+    own_gains = [jnp.broadcast_to(g[None], (count, shard)) for g in (attn_norm_gain, moe_norm_gain)]
+    query_all, key_all, value_all, out_all, cot_all, notes = gather_weights(
+        line,
+        w_query,
+        key_projection,
+        value_projection,
+        w_out,
+        cotangent,
+        note_tiles(gate_rows, *own_gains),
+    )
+    query_w = query_all.reshape(model_width, q_cols)
+    key_weight = key_all.reshape(model_width, kv_cols)
+    value_weight = value_all.reshape(model_width, kv_cols)
+    out_w = out_all.reshape(model_width, q_cols)
+    expert_gate = notes[:, 0, :length].reshape(count * length, 1)
+    attn_gain_f = notes[:, 1, :shard].reshape(model_width)
+    moe_gain_f = notes[:, 2, :shard].reshape(model_width)
+    inputs = tokens.astype(F32)
+    inv_attn = lax.rsqrt(jnp.mean(inputs * inputs, axis=1, keepdims=True) + EPSILON)
+    unit_attn = inputs * inv_attn
+    normalized_rows = (unit_attn * attn_gain_f).astype(BF16)
+    position, allowed = tree_layout(segment_ids[0], parents[0])
+    cosine_table, sine_values = rope_tables(position, HEAD_SIZE)
+    query_linear = jnp.dot(normalized_rows, query_w, preferred_element_type=F32).reshape(
+        length, q_heads, HEAD_SIZE
+    )
+    key_linear = jnp.dot(normalized_rows, key_weight, preferred_element_type=F32).reshape(
+        length, kv_heads, HEAD_SIZE
+    )
+    query_heads = (
+        apply_rotary(query_linear, cosine_table, sine_values)
+        .astype(BF16)
+        .reshape(length, kv_heads, group_size, HEAD_SIZE)
+    )
+    key_heads = apply_rotary(key_linear, cosine_table, sine_values).astype(BF16)
+    value_heads = (
+        jnp.dot(normalized_rows, value_weight, preferred_element_type=F32)
+        .astype(BF16)
+        .reshape(length, kv_heads, HEAD_SIZE)
+    )
+    scores = (
+        jnp.einsum("qhgd,khd->hgqk", query_heads, key_heads, preferred_element_type=F32)
+        * SCORE_SCALE
+    )
+    scores = jnp.where(allowed[None, None], scores, NEGATIVE)
+    own_peak = jnp.max(scores, axis=(2, 3)).reshape(1, q_heads)
+    row_max = jnp.max(scores, axis=3, keepdims=True)
+    expo = jnp.exp(scores - row_max)
+    prob_full = expo / jnp.sum(expo, axis=3, keepdims=True)
+    prob_low = prob_full.astype(BF16)
+    head_out = (
+        jnp.einsum("hgqk,khd->qhgd", prob_low, value_heads, preferred_element_type=F32)
+        .reshape(length, q_cols)
+        .astype(BF16)
+    )
+    attn_mix = twin_sum(line, 4, contract_cols(head_out, out_w))
+    hidden = inputs + RESIDUAL * attn_mix
+    inv_moe = lax.rsqrt(jnp.mean(hidden * hidden, axis=1, keepdims=True) + EPSILON)
+    unit_moe = hidden * inv_moe
+    moe_in = (unit_moe * moe_gain_f).astype(BF16)
+    expert_in = gather_rows(line, moe_in).reshape(count * length, model_width)
+    gate_w, up_w, down_w = (w_gate[0], w_up[0], w_down[0])
+    expert_out, kept_acts = expert_forward(expert_in, gate_w, up_w, down_w)
+    grad_rows = (
+        expert_gate * (RESIDUAL * cot_all.reshape(count * length, model_width).astype(F32))
+    ).astype(BF16)
+    d_inputs, grad_gate, grad_up, grad_down = expert_backward(
+        expert_in, grad_rows, gate_w, up_w, down_w, kept_acts
+    )
+    mix_out = (expert_gate * expert_out).astype(BF16).reshape(count, length, model_width)
+    d_moe_in, expert_mix = reduce_experts(
+        line, d_inputs.astype(BF16).reshape(count, length, model_width), mix_out
+    )
+    output = (hidden + RESIDUAL * expert_mix).astype(BF16)
+    grad_output = cotangent.astype(F32)
+    scaled_moe = d_moe_in * moe_gain_f
+    grad_moe_gain = jnp.sum(d_moe_in * unit_moe, axis=0)
+    d_hidden = grad_output + inv_moe * (
+        scaled_moe - unit_moe * jnp.mean(scaled_moe * unit_moe, axis=1, keepdims=True)
+    )
+    d_attn = (RESIDUAL * d_hidden).astype(BF16)
+    grad_out_w = contract_rows(d_attn, head_out)
+    d_heads = (
+        jnp.dot(d_attn, out_w, preferred_element_type=F32)
+        .astype(BF16)
+        .reshape(length, kv_heads, group_size, HEAD_SIZE)
+    )
+    d_value = jnp.einsum("hgqk,qhgd->khd", prob_low, d_heads, preferred_element_type=F32)
+    d_prob = jnp.einsum("qhgd,khd->hgqk", d_heads, value_heads, preferred_element_type=F32)
+    inner = jnp.sum(prob_full * d_prob, axis=3, keepdims=True)
+    d_scores = (prob_full * (d_prob - inner)).astype(BF16)
+    d_query_all = (
+        jnp.einsum("hgqk,khd->qhgd", d_scores, key_heads, preferred_element_type=F32) * SCORE_SCALE
+    ).reshape(length, q_heads, HEAD_SIZE)
+    d_key = (
+        jnp.einsum("hgqk,qhgd->khd", d_scores, query_heads, preferred_element_type=F32)
+        * SCORE_SCALE
+    )
+    d_query_lin = (
+        rotate_back(d_query_all, cosine_table, sine_values).astype(BF16).reshape(length, q_cols)
+    )
+    d_key_lin = rotate_back(d_key, cosine_table, sine_values).astype(BF16).reshape(length, kv_cols)
+    d_value_lin = d_value.astype(BF16).reshape(length, kv_cols)
+    grads = [
+        contract_rows(normalized_rows, g).astype(BF16).reshape(count, shard, g.shape[1])
+        for g in (d_query_lin, d_key_lin, d_value_lin)
+    ] + [grad_out_w.astype(BF16).reshape(count, shard, q_cols)]
+    d_normed_part = (
+        contract_cols(d_query_lin, query_w)
+        + contract_cols(d_key_lin, key_weight)
+        + contract_cols(d_value_lin, value_weight)
+    )
+    d_normed = twin_sum(line, 5, d_normed_part.astype(BF16))
+    scaled_attn = d_normed * attn_gain_f
+    grad_attn_gain = jnp.sum(d_normed * unit_attn, axis=0)
+    input_grad = d_hidden + inv_attn * (
+        scaled_attn - unit_attn * jnp.mean(scaled_attn * unit_attn, axis=1, keepdims=True)
+    )
+    peak_tile = note_tiles(own_peak)[0]
+    gain_tiles = note_tiles(grad_attn_gain.reshape(count, shard), grad_moe_gain.reshape(count, shard))
+    grad_query, grad_key, grad_value, grad_out, peaks, gains = reduce_grads(
+        line, grads, peak_tile, gain_tiles
+    )
+    head_peak = jnp.max(peaks[:, 0, :q_heads], axis=0)
+    gain_sums = jnp.sum(gains, axis=0)
+    scale_factor = CLIP_LIMIT / jnp.maximum(head_peak, CLIP_LIMIT)
+    query_scale = jnp.repeat(jnp.sqrt(scale_factor), HEAD_SIZE)
+    key_clip_scale = jnp.repeat(
+        jnp.sqrt(jnp.min(scale_factor.reshape(kv_heads, group_size), axis=1)), HEAD_SIZE
+    )
+    clipped_query = w_query.astype(F32) * query_scale[None, :]
+    clipped_key = key_projection.astype(F32) * key_clip_scale[None, :]
+    return (
+        output,
+        input_grad,
+        gain_sums[0, :shard],
+        grad_query,
+        grad_key,
+        grad_value,
+        grad_out,
+        gain_sums[1, :shard],
+        grad_gate[None],
+        grad_up[None],
+        grad_down[None],
+        clipped_query,
+        clipped_key,
+    )
+
+
+DENSE_BYTES = 8 * 2**20
+
+
+def on_device(*args):
+    tokens, w_gate = args[0], args[7]
+    count, ranks = lax.axis_size("dp"), lax.axis_size("tensor")
+    rows_bytes = count * tokens.shape[0] * tokens.shape[1] * 2
+    whole_experts = w_gate.shape[2] * ranks == FFE
+    dense = whole_experts and ranks == 2 and count % 4 == 0 and rows_bytes <= DENSE_BYTES
+    return on_device_dense(*args) if dense else on_device_general(*args)
+
+
 def solution(mesh):
     in_specs = (
         P("dp", None),

time: 1120 us -> 479 us (0.43)
  waiting for transfers between devices: 619 us -> 0 us
  Pallas kernels: 0 us -> 350 us
  blocking collectives: 249 us -> 0 us
  local copies, waits for them, and re-layouts: 76.5 us -> 22.2 us
  starting transfers between devices: 52.8 us -> 0 us
  between operations: 16.8 us -> 1.72 us
    reduce_scatter x6 -> x0, waiting for transfers between devices: 441 us -> none  [the longest x1 142 us: on_device(): lax.psum_scatter(grad_out_w, 'dp', scatter_dimension=0, tiled=True)]
    pallas_call x0 -> x6, Pallas kernels: none -> 350 us  [the longest x1 114 us: gather_weights(): pl.pallas_call(functools.partial(weights_kernel, line), out_shape=[jax.Sh...]
    all_to_all x4 -> x0, waiting for transfers between devices: 166 us -> none  [the longest x1 58.9 us: send_grads(): lax.all_to_all(rows_in, 'dp', split_axis=0, concat_axis=0, tiled=True)]
    unnamed x2 -> x0, blocking collectives: 116 us -> none
    all_gather x2 -> x0, blocking collectives: 88.4 us -> none  [the longest x1 45.3 us: on_device(): lax.all_gather(key_projection, 'dp', axis=0, tiled=True)]
    all_to_all x4 -> x0, starting transfers between devices: 51.9 us -> none  [the longest x1 17.8 us: send_grads(): lax.all_to_all(rows_in, 'dp', split_axis=0, concat_axis=0, tiled=True)]
    pmax x1 -> x0, blocking collectives: 44.1 us -> none  [on_device(): lax.pmax(jnp.max(jnp.stack(peak_parts), axis=0).reshape(q_heads), 'dp')]
    gather x19 -> x0, local copies, waits for them, and re-layouts: 40.7 us -> none  [the longest x8 12.7 us: on_device(): back_rows[local_index[:, column]].astype(jnp.float32)]
  transfers between devices with their start and end apart: 15 -> 0, of which waited for: 10 -> 0; matrix products, arithmetic and copies ran while one was open for 12% -> 0% of each run, Pallas kernels for 0% -> 0%
where the time goes in v1:
time: 479 us; the launch traced here: 473 us
  Pallas kernels  350 us (73%)
  matrix products  62.9 us (13%)
  other arithmetic  35.7 us (7%)
  local copies, waits for them, and re-layouts  22.2 us (5%)
    pallas_call x1, Pallas kernels, gather_weights(): pl.pallas_call(functools.partial(weights_kernel, line), out_shape=[jax.Sh...  114 us
    pallas_call x1, Pallas kernels, reduce_grads(): pl.pallas_call(functools.partial(grads_kernel, line), out_shape=[jax.Shap...  92.3 us
    pallas_call x1, Pallas kernels, reduce_experts(): pl.pallas_call(functools.partial(experts_kernel, line), out_shape=[full,...  83.7 us
    pallas_call x1, Pallas kernels, gather_rows(): pl.pallas_call(functools.partial(rows_kernel, line), out_shape=jax.ShapeD...  51.7 us
    dot_general x7, matrix products, contract_rows(): lax.dot_general(left, right, (((0,), (0,)), ((), ())), preferred_element_...  16.6 us
    dot_general x7, matrix products, contract_cols(): lax.dot_general(left, right, (((1,), (1,)), ((), ())), preferred_element_...  16 us

profile of v1, /device:TPU:0, one launch (start us, length us, event | category | flops | bytes accessed | tf_op | source)
XLA Modules:
  0.0 472.6 jit_solution(6466022173586823284)
XLA Ops:
  4.2 1.2 fusion.24
  7.7 0.9 select_reduce_fusion.5
  11.7 1.3 fusion.15
  15.1 114.3 %gather_weights.1 = (bf16[16,96,768]{2,1,0:T(8,128)(2,1)}, bf16[16,96,256]{2,1,0:T(8,128)(2,1)}, bf16[16,96,256]{2,1,0:T(8,128)(2,1)}, bf16[16,96,768]{2,1,0:T(8...) custom-call(bf16[96,768]{1,0:T(8,128)(2,1)} %query_ref.1, bf16[96,256]{1,0:T(8,128)(2,1)} %key_ref.1, ...), custom_call_target="tpu_custom_call" | custom-call | tf_op jit(solution)/shard_map/gather_weights/pallas_call | solution.py:830
  129.4 1.4 fusion.83
  130.9 1.0 slice_reduce_fusion.1
  133.8 2.4 convolution_convert_fusion.6
  136.2 1.6 copy.52
  137.7 2.3 copy.54
  140.0 1.6 fusion.37
  141.6 1.4 subtract_convert_fusion.1
  143.0 2.5 copy.55
  145.5 2.6 fusion.35
  150.1 3.0 fusion.84
  153.1 2.3 convolution_convert_fusion.5
  155.4 2.7 fusion.86.mine_ref
  158.1 4.4 twin_sum.2
  162.5 1.3 multiply_reduce_fusion.3
  164.8 51.7 %gather_rows.1 = bf16[16,128,1536]{2,1,0:T(8,128)(2,1)} custom-call(bf16[128,1536]{1,0:T(8,128)(2,1)} %multiply_convert_fusion.7.rows_ref), custom_call_target="tpu_custom_call" | custom-call | tf_op jit(solution)/shard_map/gather_rows/pallas_call | solution.py:863
  216.5 6.1 %fusion.27 = f32[2048,256]{1,0:T(8,128)} fusion(bf16[2048,1536]{1,0:T(8,128)(2,1)} %bitcast.191, bf16[1,1536,256]{2,1,0:T(8,128)(2,1)S(1)} %copy-done.8), kind=kOutput, calls=%fused_computation.55 | convolution fusion | flops 1610612736 | bytes 9175040 | tf_op jit(solution)/shard_map/dot_general | solution.py:110
  222.6 3.7 fusion.1
  226.4 3.7 multiply_convert_fusion.1
  230.1 4.7 %fusion.33 = f32[2048,256]{1,0:T(8,128)S(1)} fusion(bf16[2048,1536]{1,0:T(8,128)(2,1)} %bitcast.200, bf16[1,1536,256]{2,1,0:T(8,128)(2,1)S(1)} %copy-done.41), kind=kOutput, calls=%fused_computation.61 | convolution fusion | flops 1610612736 | bytes 9175040 | tf_op jit(solution)/shard_map/dot_general | solution.py:118
  234.9 2.6 multiply_convert_fusion.2
  237.5 3.0 convolution_bitcast_fusion
  240.5 3.0 convolution_bitcast_fusion.2
  243.6 3.3 convolution_bitcast_fusion.1
  246.9 4.5 multiply_convert_fusion
  251.4 1.8 fusion.25
  253.2 4.5 add_convert_fusion
  257.7 83.7 %reduce_experts.1 = (f32[128,1536]{1,0:T(8,128)}, f32[128,1536]{1,0:T(8,128)}) custom-call(bf16[16,128,1536]{2,1,0:T(8,128)(2,1)} %bitcast.181, bf16[16,128,1536]{2,1,0:T(8,128)(2,1)} %bitcast.197), custom_call_target="tpu_custom_call" | custom-call | tf_op jit(solution)/shard_map/reduce_experts/pallas_call | solution.py:987
  341.4 1.4 multiply_reduce_fusion
  343.5 2.5 multiply_add_fusion
  347.0 1.3 fusion.14
  348.4 1.1 multiply_reduce_fusion.1
  352.5 1.2 fusion.2.mine_ref
  353.6 3.7 twin_sum.3
  357.4 1.4 fusion.23
  358.9 2.4 fusion.22
  362.0 1.4 convolution_convert_fusion.2
  363.4 1.4 convolution_convert_fusion.3
  364.7 2.2 convolution_convert_fusion
  366.9 2.3 convolution_convert_fusion.1
  369.2 92.3 %reduce_grads.1 = (f32[96,768]{1,0:T(8,128)}, f32[96,256]{1,0:T(8,128)}, f32[96,256]{1,0:T(8,128)}, f32[96,768]{1,0:T(8,128)}, f32[16,8,128]{2,1,0:T(8,128)}, /*index=5*/f32[16,8,128]{2,1,0:T(8,128)}) custom-call(bf16[16,96,768]{2,1,0:T(8,128)(2,1)} %bitcast.190, bf16[16,96,256]{2,1,0:T(8,128)(2,1)} %bitcast.204, bf16[16,96,256]{2,1,0:T(8,128)(2,1)} %bitcast.203, ...), custom_call_target="tpu_custom_call" | custom-call | tf_op jit(solution)/shard_map/reduce_grads/pallas_call | solution.py:1066
  465.7 1.7 copy.73
  467.4 1.5 copy.74
  468.9 1.5 copy.75
  470.5 1.7 copy.76
  (167 shorter events, 25.4 us)
Async XLA Ops:
  0.6 234.2 %copy-start = (bf16[1,1536,256]{2,1,0:T(8,128)(2,1)S(1)}, bf16[1,1536,256]{2,1,0:T(8,128)(2,1)}, u32[]{:S(2)}) copy-start(bf16[1,1536,256]{2,1,0:T(8,128)(2,1)} %param.23) | copy-start | bytes 2359300
  5.4 134.6 %copy-start.1 = (bf16[128,1536]{1,0:T(8,128)(2,1)S(1)}, bf16[128,1536]{1,0:T(8,128)(2,1)}, u32[]{:S(2)}) copy-start(bf16[128,1536]{1,0:T(8,128)(2,1)} %param.15) | copy-start | bytes 1179652
  14.4 118.8 %copy-start.20 = (f32[16,4,128]{2,1,0:T(4,128)}, f32[16,4,128]{2,1,0:T(4,128)S(1)}, u32[]{:S(2)}) copy-start(f32[16,4,128]{2,1,0:T(4,128)S(1)} %broadcast.169) | copy-start | bytes 98308
  130.9 2.3 copy-start.30
  133.8 9.2 %copy-start.4 = (bf16[16,96,768]{2,1,0:T(8,128)(2,1)S(1)}, bf16[16,96,768]{2,1,0:T(8,128)(2,1)}, u32[]{:S(2)}) copy-start(bf16[16,96,768]{2,1,0:T(8,128)(2,1)} %get-tuple-element.30) | copy-start | bytes 7077892
  145.5 2.6 copy-start.13
  145.5 3.4 copy-start.24
  145.5 3.4 copy-start.26
  145.5 3.4 copy-start.35
  145.5 3.9 copy-start.37
  145.5 3.9 copy-start.39
  145.5 3.9 copy-start.40
  148.2 0.7 copy-start.18
  150.1 5.3 %copy-start.2 = (bf16[16,96,768]{2,1,0:T(8,128)(2,1)S(1)}, bf16[16,96,768]{2,1,0:T(8,128)(2,1)}, u32[]{:S(2)}) copy-start(bf16[16,96,768]{2,1,0:T(8,128)(2,1)} %get-tuple-element.31) | copy-start | bytes 7077892
  158.1 5.8 %copy-start.23 = (f32[1536]{0:T(1024)S(1)}, f32[1536]{0:T(1024)}, u32[]{:S(2)}) copy-start(f32[1536]{0:T(1024)} %mul.419) | copy-start | bytes 18436
  164.8 51.7 %copy-start.8 = (bf16[1,1536,256]{2,1,0:T(8,128)(2,1)S(1)}, bf16[1,1536,256]{2,1,0:T(8,128)(2,1)}, u32[]{:S(2)}) copy-start(bf16[1,1536,256]{2,1,0:T(8,128)(2,1)} %param.22) | copy-start | bytes 2359300
  164.8 57.8 %slice-start = ((s8[6291456]{0:T(1024)(128)(4,1)}), s8[2097152]{0:T(1024)(128)(4,1)S(1)}, s32[]{:S(2)}) async-start(s8[6291456]{0:T(1024)(128)(4,1)} %bitcast.182), calls=%async_computation | async-start | bytes 4194304
  216.4 6.2 %slice-start.1 = ((s8[6291456]{0:T(1024)(128)(4,1)}), s8[4194304]{0:T(1024)(128)(4,1)S(1)}, s32[]{:S(2)}) async-start(s8[6291456]{0:T(1024)(128)(4,1)} %bitcast.182), calls=%async_computation.1 | async-start | bytes 8388608
  216.4 6.1 %copy-start.33 = (f32[2048]{0:T(1024)S(1)}, f32[2048]{0:T(1024)}, u32[]{:S(2)}) copy-start(f32[2048]{0:T(1024)} %broadcast_multiply_fusion) | copy-start | bytes 24580
  222.6 3.8 copy-start.32
  226.4 3.7 copy-start.41
  226.4 8.5 %slice-start.2 = ((s8[6291456]{0:T(1024)(128)(4,1)}), s8[2097152]{0:T(1024)(128)(4,1)S(1)}, s32[]{:S(2)}) async-start(s8[6291456]{0:T(1024)(128)(4,1)} %bitcast.192), calls=%async_computation.2 | async-start | bytes 4194304
  230.1 4.8 %slice-start.3 = ((s8[6291456]{0:T(1024)(128)(4,1)}), s8[4194304]{0:T(1024)(128)(4,1)S(1)}, s32[]{:S(2)}) async-start(s8[6291456]{0:T(1024)(128)(4,1)} %bitcast.192), calls=%async_computation.3 | async-start | bytes 8388608
  230.1 4.8 %copy-start.42 = (f32[2048,256]{1,0:T(8,128)S(1)}, f32[2048,256]{1,0:T(8,128)}, u32[]{:S(2)}) copy-start(f32[2048,256]{1,0:T(8,128)} %fusion.27) | copy-start | bytes 6291460
  230.1 7.4 %slice-start.4 = ((s8[6291456]{0:T(1024)(128)(4,1)}), s8[4194304]{0:T(1024)(128)(4,1)S(1)}, s32[]{:S(2)}) async-start(s8[6291456]{0:T(1024)(128)(4,1)} %bitcast.198), calls=%async_computation.4 | async-start | bytes 8388608
  234.9 2.6 slice-start.5
  243.6 3.3 copy-start.31
  257.7 85.8 %copy-start.7 = (bf16[128,1536]{1,0:T(8,128)(2,1)S(1)}, bf16[128,1536]{1,0:T(8,128)(2,1)}, u32[]{:S(2)}) copy-start(bf16[128,1536]{1,0:T(8,128)(2,1)} %cot_ref.1) | copy-start | bytes 1179652
  342.9 3.1 copy-start.3
  346.1 0.9 copy-start.17
  346.1 0.9 copy-start.19
  346.1 0.9 copy-start.25
  346.1 0.9 copy-start.27
  346.6 1.7 copy-start.11
  346.6 1.7 copy-start.28
  348.3 1.1 copy-start.36
  349.4 0.7 copy-start.14
  349.4 1.7 copy-start.5
  350.1 1.9 copy-start.6
  351.1 1.3 copy-start.10
  352.0 5.3 %copy-start.15 = (f32[1536]{0:T(1024)S(1)}, f32[1536]{0:T(1024)}, u32[]{:S(2)}) copy-start(f32[1536]{0:T(1024)} %mul.380) | copy-start | bytes 18436
  352.0 5.3 %copy-start.34 = (f32[128]{0:T(128)S(1)}, f32[128]{0:T(128)}, u32[]{:S(2)}) copy-start(f32[128]{0:T(128)} %add_rsqrt_fusion.1) | copy-start | bytes 1540
  353.6 7.6 %copy-start.21 = (f32[16,4,128]{2,1,0:T(4,128)S(1)}, f32[16,4,128]{2,1,0:T(4,128)}, u32[]{:S(2)}) copy-start(f32[16,4,128]{2,1,0:T(4,128)} %copy-done.20) | copy-start | bytes 98308
  353.6 7.6 %copy-start.29 = (f32[16,128]{1,0:T(8,128)S(1)}, f32[16,128]{1,0:T(8,128)}, u32[]{:S(2)}) copy-start(f32[16,128]{1,0:T(8,128)} %pad.27) | copy-start | bytes 24580
  353.6 7.6 %copy-start.38 = (f32[8]{0:T(128)S(1)}, f32[8]{0:T(128)}, u32[]{:S(2)}) copy-start(f32[8]{0:T(128)} %pad.34.clone) | copy-start | bytes 100
  358.9 5.9 %copy-start.9 = (bf16[4,64,3,128]{3,1,2,0:T(8,128)(2,1)S(1)}, bf16[4,64,3,128]{3,1,2,0:T(8,128)(2,1)}, u32[]{:S(2)}) copy-start(bf16[4,64,3,128]{3,1,2,0:T(8,128)(2,1)} %convolution_convert_fusion.5) | copy-start | bytes 589828
  369.2 95.1 %copy-start.22 = (bf16[96,256]{1,0:T(8,128)(2,1)S(1)}, bf16[96,256]{1,0:T(8,128)(2,1)}, u32[]{:S(2)}) copy-start(bf16[96,256]{1,0:T(8,128)(2,1)} %key_ref.1) | copy-start | bytes 147460
  369.2 95.7 %copy-start.12 = (bf16[96,768]{1,0:T(8,128)(2,1)S(1)}, bf16[96,768]{1,0:T(8,128)(2,1)}, u32[]{:S(2)}) copy-start(bf16[96,768]{1,0:T(8,128)(2,1)} %query_ref.1) | copy-start | bytes 442372
  (1 other events, 0.6 us)

commit v2 on v1

--- a/solution.py
+++ b/solution.py
@@ -498,174 +498,179 @@
 
 
 class Gather:
-    def __init__(self, place, view, send_sem, recv_sem):
-        self.place, self.view = place, view
+    def __init__(self, place, view, send_sem, recv_sem, fixed=False):
+        self.place, self.view, self.fixed = place, view, fixed
         self.send_sem, self.recv_sem = send_sem, recv_sem
 
-    def _copy(self, part, way):
-        place, line = self.place, self.place.line
-        z = part // 4
-        if way == "up":
-            slot, device = z, place.up()
-        elif way == "down":
-            slot, device = line + z, place.down()
-        elif way == "a":
-            slot, device = 2 * line + z, place.beside_a()
+    def _copy(self, source, target, sem, device):
+        there = self.view(source if self.fixed else target)
+        return remote(self.view(source), there, self.send_sem.at[sem], self.recv_sem.at[target], device)
+
+    def _to_z(self, step):
+        place = self.place
+        own = place.z
+        return self._copy(own, own, step + place.line - 1, (place.me + 4 * step, place.core))
+
+    def _to_a(self, z):
+        line = self.place.line
+        return self._copy(z, line + z, 2 * line - 1 + z, self.place.beside_a())
+
+    def _to_b(self, slot):
+        line = self.place.line
+        return self._copy(slot, 2 * line + slot, 3 * line - 1 + slot, self.place.beside_b())
+
+    def take(self, slot):
+        self._copy(slot, slot, 0, self.place.beside_b()).wait_recv()
+
+    def near(self, step, action):
+        place = self.place
+        if step == 0:
+            action(place.z)
         else:
-            slot, device = 3 * line + part - place.b * place.step_b, place.beside_b()
-        ref = self.view(part)
-        return remote(ref, ref, self.send_sem.at[slot], self.recv_sem.at[part], device)
-
-    def _await(self, part):
-        self._copy(part, "b").wait_recv()
+            pl.when(place.z >= step)(lambda: action(place.z - step))
+            pl.when(place.z + step < place.line)(lambda: action(place.z + step))
 
     def start(self):
         place = self.place
-        me, last = place.me, place.line - 1
-
-        @pl.when(place.z < last)
-        def _():
-            self._copy(me, "up").start()
-
-        @pl.when(place.z > 0)
-        def _():
-            self._copy(me, "down").start()
-
-        self._copy(me, "a").start()
-        self._copy(me, "b").start()
-
-    def along(self, step):
+
+        def reach(step):
+            pl.when(place.z >= step)(lambda: self._to_z(-step).start())
+            pl.when(place.z + step < place.line)(lambda: self._to_z(step).start())
+
+        reach(1)
+        self._to_a(place.z).start()
+        self._to_b(place.z).start()
+        for step in range(2, place.line):
+            reach(step)
+
+    def along(self, step, then=None):
+        def pass_on(z):
+            self.take(z)
+            self._to_a(z).start()
+            self._to_b(z).start()
+            if then is not None:
+                then(z)
+
+        self.near(step, pass_on)
+
+    def across(self, step, then=None):
+        line = self.place.line
+
+        def pass_on(z):
+            self.take(line + z)
+            self._to_b(line + z).start()
+            if then is not None:
+                then(line + z)
+
+        self.near(step, pass_on)
+
+    def settle(self):
         place = self.place
-        last = place.line - 1
-        below = place.part(place.z - step, place.a, place.b)
-        above = place.part(place.z + step, place.a, place.b)
-
-        @pl.when(place.z >= step)
-        def _():
-            self._await(below)
-
-            @pl.when(place.z < last)
-            def _():
-                self._copy(below, "up").start()
-
-            self._copy(below, "a").start()
-            self._copy(below, "b").start()
-
-        @pl.when(place.z + step <= last)
-        def _():
-            self._await(above)
-
-            @pl.when(place.z > 0)
-            def _():
-                self._copy(above, "down").start()
-
-            self._copy(above, "a").start()
-            self._copy(above, "b").start()
-
-    def across(self, step):
-        place = self.place
-
-        def take(z):
-            part = place.part(z, 1 - place.a, place.b)
-            self._await(part)
-            self._copy(part, "b").start()
-
-        if step == 0:
-            take(place.z)
-        else:
-            pl.when(place.z >= step)(lambda: take(place.z - step))
-            pl.when(place.z + step < place.line)(lambda: take(place.z + step))
-
-    def finish(self):
-        place, last = self.place, self.place.line - 1
-
-        def settle(z, carry):
-            for a in (0, 1):
-                self._await(place.part(z, a, 1 - place.b))
-                self._copy(place.part(z, a, place.b), "b").wait_send()
-            self._copy(place.part(z, place.a, place.b), "a").wait_send()
-            own = place.part(z, place.a, place.b)
-
-            @pl.when(jnp.logical_and(z <= place.z, place.z < last))
-            def _():
-                self._copy(own, "up").wait_send()
-
-            @pl.when(jnp.logical_and(z >= place.z, place.z > 0))
-            def _():
-                self._copy(own, "down").wait_send()
-
+        line = place.line
+
+        def wait(z, carry):
+            self._to_a(z).wait_send()
+            self._to_b(z).wait_send()
+            self._to_b(line + z).wait_send()
+            pl.when(z != place.z)(lambda: self._to_z(z - place.z).wait_send())
             return carry
 
-        lax.fori_loop(0, place.line, settle, 0)
-
-
-def gather_all(gathers):
+        lax.fori_loop(0, line, wait, 0)
+
+    def take_rest(self):
+        line = self.place.line
+
+        def wait(k, carry):
+            self.take(2 * line + k)
+            return carry
+
+        lax.fori_loop(0, 2 * line, wait, 0)
+
+
+def gather_all(gathers, thens=None):
     line = gathers[0].place.line
+    thens = thens or [None] * len(gathers)
     for g in gathers:
         g.start()
     for step in range(1, line + 1):
-        for g in gathers:
+        for g, then in zip(gathers, thens):
             if step < line:
-                g.along(step)
-            g.across(step - 1)
-    for g in gathers:
-        g.finish()
+                g.along(step, then)
+            g.across(step - 1, then)
+
+
+class Twin:
+    def __init__(self, place, source, target, send_sem, recv_sem):
+        self.place, self.source, self.target = place, source, target
+        self.send_sem, self.recv_sem = send_sem, recv_sem
+
+    def copy(self, slot):
+        line = self.place.line
+        group = slot // line
+        there = slot + line * ((group % 2) - (group // 2))
+        return remote(
+            self.source(slot),
+            self.target(there),
+            self.send_sem.at[slot],
+            self.recv_sem.at[there],
+            self.place.twin(),
+        )
+
+    def start(self, slot):
+        self.copy(slot).start()
+
+    def take(self, slot):
+        remote(
+            self.source(slot),
+            self.target(slot),
+            self.send_sem.at[slot],
+            self.recv_sem.at[slot],
+            self.place.twin(),
+        ).wait_recv()
+
+    def wait_send(self, slot):
+        self.copy(slot).wait_send()
 
 
 class Reduce:
-    def __init__(self, place, parts, from_b, from_a, from_z, sems):
+    def __init__(self, place, parts, from_b, from_a, from_z, send_sem, recv_sem):
         self.place, self.parts = place, parts
         self.from_b, self.from_a, self.from_z = from_b, from_a, from_z
-        self.send_sem, self.recv_sem = sems
-
-    def _to_b(self, z, a, slot=None):
-        place, line = self.place, self.place.line
-        slot = z * 2 + a
-        return remote(
-            self.parts.at[place.part(z, a, 1 - place.b)],
-            self.from_b.at[slot],
-            self.send_sem.at[slot],
-            self.recv_sem.at[slot],
-            place.beside_b(),
-        )
+        self.send_sem, self.recv_sem = send_sem, recv_sem
+
+    def _copy(self, source, target, sem, device):
+        return remote(source, target, self.send_sem.at[sem], self.recv_sem.at[sem], device)
+
+    def _to_b(self, k):
+        line = self.place.line
+        return self._copy(self.parts.at[2 * line + k], self.from_b.at[k], k, self.place.beside_b())
 
     def _to_a(self, z):
-        place, line = self.place, self.place.line
-        return remote(
-            self.parts.at[place.part(z, 1 - place.a, place.b)],
-            self.from_a.at[z],
-            self.send_sem.at[2 * line + z],
-            self.recv_sem.at[2 * line + z],
-            place.beside_a(),
-        )
+        line = self.place.line
+        return self._copy(self.parts.at[line + z], self.from_a.at[z], 2 * line + z, self.place.beside_a())
 
     def _along(self, z, way):
-        place, line = self.place, self.place.line
-        slot = way * line + z
-        return remote(
-            self.parts.at[place.part(z, place.a, place.b)],
-            self.from_z.at[slot],
-            self.send_sem.at[3 * line + slot],
-            self.recv_sem.at[3 * line + slot],
-            place.up() if way == 0 else place.down(),
-        )
-
-    def _add(self, part, block):
-        self.parts[part] = (self.parts[part].astype(F32) + block.astype(F32)).astype(BF16)
-
-    def send_b(self, z, a):
-        self._to_b(z, a).start()
-
-    def fold_b(self, z, a):
-        self._to_b(z, a).wait_recv()
-        self._add(self.place.part(z, a, self.place.b), self.from_b[z * 2 + a])
+        place = self.place
+        slot = way * place.line + z
+        device = place.up() if way == 0 else place.down()
+        return self._copy(self.parts.at[z], self.from_z.at[slot], 3 * place.line + slot, device)
+
+    def _add(self, slot, block):
+        self.parts[slot] = (self.parts[slot].astype(F32) + block.astype(F32)).astype(BF16)
+
+    def send_b(self, k):
+        self._to_b(k).start()
+
+    def fold_b(self, k):
+        self._to_b(k).wait_recv()
+        self._add(k, self.from_b[k])
 
     def send_a(self, z):
         self._to_a(z).start()
 
     def fold_a(self, z):
         self._to_a(z).wait_recv()
-        self._add(self.place.part(z, self.place.a, self.place.b), self.from_a[z])
+        self._add(z, self.from_a[z])
 
     def pass_up(self, z):
         place = self.place
@@ -675,7 +680,7 @@
             @pl.when(place.z > 0)
             def _():
                 self._along(z, 0).wait_recv()
-                self._add(place.part(z, place.a, place.b), self.from_z[z])
+                self._add(z, self.from_z[z])
 
             self._along(z, 0).start()
 
@@ -687,14 +692,32 @@
             @pl.when(place.z < line - 1)
             def _():
                 self._along(z, 1).wait_recv()
-                self._add(place.part(z, place.a, place.b), self.from_z[line + z])
+                self._add(z, self.from_z[line + z])
 
             self._along(z, 1).start()
+
+    def fold_line_a(self):
+        line = self.place.line
+        for z in ends_first(line):
+            self.fold_b(line + z)
+            self.send_a(z)
+
+    def fold_line_own(self):
+        for z in ends_first(self.place.line):
+            self.fold_b(z)
+
+    def finish_line(self):
+        line = self.place.line
+        for z in ends_first(line):
+            self.fold_a(z)
+        for k in range(line):
+            self.pass_up(line - 1 - k)
+            self.pass_down(k)
 
     def result(self, out):
         place, line = self.place, self.place.line
-        me, z = place.me, place.z
-        out[...] = self.parts[me].astype(F32)
+        z = place.z
+        out[...] = self.parts[z].astype(F32)
 
         @pl.when(z > 0)
         def _():
@@ -710,21 +733,24 @@
         place, line = self.place, self.place.line
 
         def wait(z, carry):
-            for a in (0, 1):
-                self._to_b(z, a).wait_send()
+            self._to_b(z).wait_send()
+            self._to_b(line + z).wait_send()
             self._to_a(z).wait_send()
-
-            @pl.when(place.z < z)
-            def _():
-                self._along(z, 0).wait_send()
-
-            @pl.when(place.z > z)
-            def _():
-                self._along(z, 1).wait_send()
-
+            pl.when(place.z < z)(lambda: self._along(z, 0).wait_send())
+            pl.when(place.z > z)(lambda: self._along(z, 1).wait_send())
             return carry
 
         lax.fori_loop(0, line, wait, 0)
+
+
+def reduce_scratch(line, block):
+    return [
+        pltpu.VMEM((2 * line, *block), BF16),
+        pltpu.VMEM((line, *block), BF16),
+        pltpu.VMEM((2 * line, *block), BF16),
+        pltpu.SemaphoreType.DMA((5 * line,)),
+        pltpu.SemaphoreType.DMA((5 * line,)),
+    ]
 
 
 def ends_first(line):
@@ -734,20 +760,20 @@
     return order
 
 
-def reduce_rest(reduces):
-    line = reduces[0].place.line
-    place = reduces[0].place
-    for r in reduces:
-        for z in ends_first(line):
-            r.fold_b(z, 1 - place.a)
-            r.send_a(z)
-        for z in ends_first(line):
-            r.fold_b(z, place.a)
-        for z in ends_first(line):
-            r.fold_a(z)
-        for k in range(line):
-            r.pass_up(line - 1 - k)
-            r.pass_down(k)
+def part_of(place, slot):
+    line = place.line
+    group, z = slot // line, slot % line
+    flip_a, flip_b = group % 2, group // 2
+    a = place.a + flip_a * (1 - 2 * place.a)
+    b = place.b + flip_b * (1 - 2 * place.b)
+    return place.part(z, a, b)
+
+
+def halves(place, width):
+    half = width // 2
+    mine = pl.ds(pl.multiple_of(place.core * half, 128), half)
+    theirs = pl.ds(pl.multiple_of((1 - place.core) * half, 128), half)
+    return mine, theirs
 
 
 def weights_kernel(
@@ -772,46 +798,50 @@
     local_sems,
 ):
     place = Place(line)
-    half = cot_ref.shape[1] // 2
-    span = pl.ds(pl.multiple_of(place.core * half, 128), half)
+    span, _ = halves(place, cot_ref.shape[1])
     own = []
-    for i, (src, dst) in enumerate(
-        ((query_ref, query_all), (key_ref, key_all), (value_ref, value_all), (out_ref, out_all), (cot_ref, cot_all))
-    ):
+    blocks = ((query_ref, query_all), (key_ref, key_all), (value_ref, value_all), (out_ref, out_all))
+    for i, (src, dst) in enumerate(blocks):
         own.append(pltpu.make_async_copy(src, dst.at[place.me], local_sems.at[i]))
-        own[-1].start()
+    own.append(pltpu.make_async_copy(cot_ref, cot_all.at[place.z], local_sems.at[4]))
+    for c in own:
+        c.start()
     enter(place)
     note = Notes(place, note_ref, notes, note_send, note_recv, False)
     note.start()
     for c in own:
         c.wait()
     gathers = [
-        Gather(place, lambda p, ref=ref: ref.at[p], sends.at[i], recvs.at[i])
+        Gather(place, lambda s, ref=ref: ref.at[part_of(place, s)], sends.at[i], recvs.at[i], True)
         for i, ref in enumerate((query_all, key_all, value_all, out_all))
     ]
-    gathers.append(Gather(place, lambda p: cot_all.at[p, :, span], sends.at[4], recvs.at[4]))
-    gather_all(gathers)
-    swap_halves(place, cot_all, span, twin_sems)
+    cot_view = lambda s: cot_all.at[s, :, span]
+    cot_gather = Gather(place, cot_view, sends.at[4], recvs.at[4])
+    twin = Twin(place, cot_view, cot_view, twin_sems.at[0], twin_sems.at[1])
+    gathers.append(cot_gather)
+    gather_all(gathers, [None] * 4 + [twin.start])
+    for g in gathers[:4]:
+        g.take_rest()
+
+    def rest(slot, carry):
+        cot_gather.take(slot)
+        twin.start(slot)
+        return carry
+
+    lax.fori_loop(2 * line, 4 * line, rest, 0)
+    for g in gathers:
+        g.settle()
+
+    def other(slot, carry):
+        @pl.when(slot != place.z)
+        def _():
+            twin.wait_send(slot)
+            twin.take(slot)
+
+        return carry
+
+    lax.fori_loop(0, 4 * line, other, 0)
     note.finish()
-
-
-def swap_halves(place, ref, span, sems):
-    def twin(part):
-        view = ref.at[part, :, span]
-        return remote(view, view, sems.at[0, part], sems.at[1, part], place.twin())
-
-    def begin(offset, carry):
-        twin(place.peer(offset)).start()
-        return carry
-
-    def end(offset, carry):
-        copy = twin(place.peer(offset))
-        copy.wait_send()
-        copy.wait_recv()
-        return carry
-
-    lax.fori_loop(1, place.count, begin, 0)
-    lax.fori_loop(1, place.count, end, 0)
 
 
 ANY = pl.BlockSpec(memory_space=pl.ANY)
@@ -834,7 +864,7 @@
         in_specs=[ANY] * 5 + [IN_VMEM],
         out_specs=[ANY] * 5 + [IN_VMEM],
         scratch_shapes=[
-            pltpu.SemaphoreType.DMA((5, 3 * line + count)),
+            pltpu.SemaphoreType.DMA((5, 5 * line)),
             pltpu.SemaphoreType.DMA((5, count)),
             pltpu.SemaphoreType.DMA((count,)),
             pltpu.SemaphoreType.DMA((count,)),
@@ -844,36 +874,6 @@
         compiler_params=params(0),
         name="gather_weights",
     )(query, key, value, out, cotangent, note)
-
-
-def rows_kernel(line, rows_ref, rows_all, send, recv, twin_sems, local_sem):
-    place = Place(line)
-    half = rows_ref.shape[1] // 2
-    span = pl.ds(pl.multiple_of(place.core * half, 128), half)
-    own = pltpu.make_async_copy(rows_ref, rows_all.at[place.me], local_sem)
-    own.start()
-    enter(place)
-    own.wait()
-    gather_all([Gather(place, lambda p: rows_all.at[p, :, span], send, recv)])
-    swap_halves(place, rows_all, span, twin_sems)
-
-
-def gather_rows(line, rows):
-    count = 4 * line
-    return pl.pallas_call(
-        functools.partial(rows_kernel, line),
-        out_shape=jax.ShapeDtypeStruct((count, *rows.shape), BF16),
-        in_specs=[ANY],
-        out_specs=ANY,
-        scratch_shapes=[
-            pltpu.SemaphoreType.DMA((3 * line + count,)),
-            pltpu.SemaphoreType.DMA((count,)),
-            pltpu.SemaphoreType.DMA((2, count)),
-            pltpu.SemaphoreType.DMA,
-        ],
-        compiler_params=params(1),
-        name="gather_rows",
-    )(rows)
 
 
 def swap_kernel(line, mine_ref, sum_ref, other, sems):
@@ -901,110 +901,221 @@
 
 def experts_kernel(
     line,
-    grads_ref,
-    outs_ref,
-    grads_sum,
-    outs_sum,
-    parts,
-    arrived,
+    rows_ref,
+    cot_ref,
+    notes_ref,
+    gate_ref,
+    up_ref,
+    down_ref,
+    d_rows_ref,
+    mix_ref,
+    grad_gate_ref,
+    grad_up_ref,
+    grad_down_ref,
+    rows,
+    cots,
+    active,
+    d_gate,
+    d_up,
+    grad_stage,
+    mix_stage,
+    grad_parts,
+    mix_parts,
+    grads,
+    total,
     from_b,
     from_a,
     from_z,
-    total,
-    sends,
-    recvs,
+    reduce_send,
+    reduce_recv,
+    gather_send,
+    gather_recv,
     twin_sems,
+    load_sems,
     last_sems,
-    local_sems,
+    store_sems,
 ):
     place = Place(line)
-    width = grads_ref.shape[2]
-    half = width // 2
-    mine = pl.ds(pl.multiple_of(place.core * half, 128), half)
-    theirs = pl.ds(pl.multiple_of((1 - place.core) * half, 128), half)
+    count = 4 * line
+    length, width = rows_ref.shape
+    hidden = gate_ref.shape[1]
+    mine, theirs = halves(place, width)
+
+    def load(slot):
+        return pltpu.make_async_copy(cot_ref.at[slot], cots.at[slot], load_sems.at[slot])
+
+    def begin(slot, carry):
+        load(slot).start()
+        return carry
+
+    lax.fori_loop(0, count, begin, 0)
+    rows[place.z] = rows_ref[...]
     enter(place)
-    order = [(z, a, b) for b in (1, 0) for a in (1, 0) for z in ends_first(line)]
-
-    def at(spot):
-        z, a, b = spot
-        flip = lambda own, other: own + other * (1 - 2 * own)
-        return place.part(z, flip(place.a, a), flip(place.b, b))
-
-    def load(i, ref, spot):
-        part = at(spot)
-        return pltpu.make_async_copy(ref.at[part, :, mine], parts.at[i, part], local_sems.at[i, part])
-
-    def share(i, ref, spot):
-        part = at(spot)
-        return remote(
-            ref.at[part, :, theirs],
-            arrived.at[i, part],
-            twin_sems.at[i, 0, part],
-            twin_sems.at[i, 1, part],
-            place.twin(),
-        )
-
-    sources = (grads_ref, outs_ref)
-    for i, ref in enumerate(sources):
-        for spot in order:
-            share(i, ref, spot).start()
-            load(i, ref, spot).start()
-    reduces = [
-        Reduce(place, parts.at[i], from_b.at[i], from_a.at[i], from_z.at[i], (sends.at[i], recvs.at[i]))
-        for i in range(2)
-    ]
-    for i, ref in enumerate(sources):
-        for spot in order:
-            part = at(spot)
-            load(i, ref, spot).wait()
-            share(i, ref, spot).wait_recv()
-            reduces[i]._add(part, arrived[i, part])
-            z, a, b = spot
-            if b == 1:
-                reduces[i].send_b(z, place.a + a * (1 - 2 * place.a))
-    reduce_rest(reduces)
-    copies = []
-    for i, out in enumerate((grads_sum, outs_sum)):
-        reduces[i].result(total.at[i])
-        out[:, mine] = total[i]
-        copies.append(
-            remote(total.at[i], out.at[:, mine], last_sems.at[0, i], last_sems.at[1, i], place.twin())
-        )
-        copies[-1].start()
-    for r in reduces:
-        r.settle()
-    for i, ref in enumerate(sources):
-        for spot in order:
-            share(i, ref, spot).wait_send()
-    for c in copies:
+    view = lambda s: rows.at[s, :, mine]
+    gather = Gather(place, view, gather_send, gather_recv)
+    row_twin = Twin(place, view, view, twin_sems.at[0], twin_sems.at[1])
+    grad_twin = Twin(
+        place, lambda s: grad_stage.at[s, :, theirs], lambda s: grad_parts.at[s], twin_sems.at[2], twin_sems.at[3]
+    )
+    mix_twin = Twin(
+        place, lambda s: mix_stage.at[s, :, theirs], lambda s: mix_parts.at[s], twin_sems.at[4], twin_sems.at[5]
+    )
+    reduce = Reduce(place, grad_parts, from_b, from_a, from_z, reduce_send, reduce_recv)
+    gather_all([gather], [row_twin.start])
+
+    def fold(slot):
+        grad_twin.take(slot)
+        reduce._add(slot, grad_stage[slot, :, mine])
+        pl.when(slot >= 2 * line)(lambda: reduce.send_b(slot - 2 * line))
+
+    def column(slot):
+        return jnp.transpose(notes_ref[part_of(place, slot)])[:, 0:1]
+
+    def step(tile, carry):
+        first = 2 * tile
+        pair = (first, first + 1)
+        two = pl.ds(first, 2)
+        flat = pl.ds(pl.multiple_of(first * length, 2 * length), 2 * length)
+        for slot in pair:
+            pl.when(slot != place.z)(lambda slot=slot: row_twin.take(slot))
+            load(slot).wait()
+        x = rows[two].reshape(2 * length, width)
+        gate = jnp.concatenate([column(slot) for slot in pair], axis=0)
+        gate_pre = jnp.dot(x, gate_ref[...], preferred_element_type=F32)
+        up_pre = jnp.dot(x, up_ref[...], preferred_element_type=F32)
+        sigmoid = 1.0 / (1.0 + jnp.exp(-gate_pre))
+        silu = gate_pre * sigmoid
+        act = (silu * up_pre).astype(BF16)
+        active[flat, :] = act
+        mix = contract_cols(act, down_ref[...])
+        mix_stage[two] = (gate * mix).astype(BF16).reshape(2, length, width)
+        d_out = (gate * (RESIDUAL * cots[two].reshape(2 * length, width).astype(F32))).astype(BF16)
+        cots[two] = d_out.reshape(2, length, width)
+        d_act = jnp.dot(d_out, down_ref[...], preferred_element_type=F32)
+        d_g = (d_act * up_pre * sigmoid * (1.0 + gate_pre * (1.0 - sigmoid))).astype(BF16)
+        d_u = (d_act * silu).astype(BF16)
+        d_gate[flat, :] = d_g
+        d_up[flat, :] = d_u
+        d_in = contract_cols(d_g, gate_ref[...]) + contract_cols(d_u, up_ref[...])
+        grad_stage[two] = d_in.astype(BF16).reshape(2, length, width)
+        for slot in pair:
+            grad_twin.start(slot)
+            mix_twin.start(slot)
+
+        group = (tile + 1) // (line // 2)
+
+        @pl.when(jnp.logical_or(group == 1, group == 3))
+        def _():
+            for slot in (first + 2, first + 3):
+                slot = slot + line * (3 - group) // 2
+                gather.take(slot)
+                row_twin.start(slot)
+
+        @pl.when(jnp.logical_and(tile > 0, (first - 1) // line != 1))
+        def _():
+            for slot in (first - 2, first - 1):
+                fold(slot)
+
+        return carry
+
+    lax.fori_loop(0, 2 * line, step, 0)
+    for slot in (count - 2, count - 1):
+        fold(slot)
+
+    def fold_late(slot, carry):
+        fold(slot)
+        return carry
+
+    lax.fori_loop(line, 2 * line, fold_late, 0)
+
+    def weight_grad(number, left, right, out_ref):
+        left = left.reshape(count * length, left.shape[2]) if len(left.shape) == 3 else left
+
+        def some(i, carry):
+            span = pl.ds(pl.multiple_of(i * 512, 512), 512)
+            grads[number, span, :] = contract_rows(left[:, span], right[...])
+            return carry
+
+        lax.fori_loop(0, width // 512, some, 0)
+        store = pltpu.make_async_copy(grads.at[number], out_ref, store_sems.at[number])
+        store.start()
+        return store
+
+    stores = [weight_grad(0, cots, active, grad_down_ref)]
+    reduce.fold_line_own()
+    stores.append(weight_grad(1, rows, d_gate, grad_gate_ref))
+    reduce.fold_line_a()
+    stores.append(weight_grad(2, rows, d_up, grad_up_ref))
+    reduce.finish_line()
+
+    def mix_fold(slot, carry):
+        mix_twin.take(slot)
+        mix_parts[slot] = (mix_parts[slot].astype(F32) + mix_stage[slot, :, mine].astype(F32)).astype(BF16)
+        return carry
+
+    lax.fori_loop(0, count, mix_fold, 0)
+    stores.append(pltpu.make_async_copy(mix_parts, mix_ref, store_sems.at[3]))
+    stores[-1].start()
+    reduce.result(total)
+    d_rows_ref[:, mine] = total[...]
+    last = remote(total, d_rows_ref.at[:, mine], last_sems.at[0], last_sems.at[1], place.twin())
+    last.start()
+    reduce.settle()
+    gather.settle()
+
+    def settle(slot, carry):
+        pl.when(slot != place.z)(lambda: row_twin.wait_send(slot))
+        grad_twin.wait_send(slot)
+        mix_twin.wait_send(slot)
+        return carry
+
+    lax.fori_loop(0, count, settle, 0)
+    for c in stores:
         c.wait()
-
-
-def reduce_experts(line, grads, outs):
-    count, rows, width = grads.shape
-    half = width // 2
-    full = jax.ShapeDtypeStruct((rows, width), F32)
+    last.wait()
+
+
+def run_experts(line, rows, cots, notes, gate, up, down):
+    count = 4 * line
+    length, width = rows.shape
+    half, hidden = width // 2, gate.shape[1]
+    grad = jax.ShapeDtypeStruct((width, hidden), F32)
     return pl.pallas_call(
         functools.partial(experts_kernel, line),
-        out_shape=[full, full],
-        in_specs=[ANY, ANY],
-        out_specs=[IN_VMEM, IN_VMEM],
+        out_shape=[
+            jax.ShapeDtypeStruct((length, width), F32),
+            jax.ShapeDtypeStruct((count, length, half), BF16),
+            grad,
+            grad,
+            grad,
+        ],
+        in_specs=[IN_VMEM, ANY, IN_VMEM, IN_VMEM, IN_VMEM, IN_VMEM],
+        out_specs=[IN_VMEM, ANY, ANY, ANY, ANY],
         scratch_shapes=[
-            pltpu.VMEM((2, count, rows, half), BF16),
-            pltpu.VMEM((2, count, rows, half), BF16),
-            pltpu.VMEM((2, 2 * line, rows, half), BF16),
-            pltpu.VMEM((2, line, rows, half), BF16),
-            pltpu.VMEM((2, 2 * line, rows, half), BF16),
-            pltpu.VMEM((2, rows, half), F32),
-            pltpu.SemaphoreType.DMA((2, 5 * line)),
-            pltpu.SemaphoreType.DMA((2, 5 * line)),
-            pltpu.SemaphoreType.DMA((2, 2, count)),
-            pltpu.SemaphoreType.DMA((2, 2)),
-            pltpu.SemaphoreType.DMA((2, count)),
+            pltpu.VMEM((count, length, width), BF16),
+            pltpu.VMEM((count, length, width), BF16),
+            pltpu.VMEM((count * length, hidden), BF16),
+            pltpu.VMEM((count * length, hidden), BF16),
+            pltpu.VMEM((count * length, hidden), BF16),
+            pltpu.VMEM((count, length, width), BF16),
+            pltpu.VMEM((count, length, width), BF16),
+            pltpu.VMEM((count, length, half), BF16),
+            pltpu.VMEM((count, length, half), BF16),
+            pltpu.VMEM((3, width, hidden), F32),
+            pltpu.VMEM((length, half), F32),
+        ]
+        + reduce_scratch(line, (length, half))
+        + [
+            pltpu.SemaphoreType.DMA((5 * line,)),
+            pltpu.SemaphoreType.DMA((count,)),
+            pltpu.SemaphoreType.DMA((6, count)),
+            pltpu.SemaphoreType.DMA((count,)),
+            pltpu.SemaphoreType.DMA((2,)),
+            pltpu.SemaphoreType.DMA((4,)),
         ],
         compiler_params=params(2),
-        name="reduce_experts",
-    )(grads, outs)
+        name="run_experts",
+    )(rows, cots, notes, gate, up, down)
 
 
 def grads_kernel(
@@ -1013,26 +1124,34 @@
     key_ref,
     value_ref,
     out_ref,
+    mix_ref,
     peak_ref,
     gain_ref,
     query_sum,
     key_sum,
     value_sum,
     out_sum,
+    mix_sum,
     peaks,
     gains,
     *scratch,
 ):
     place = Place(line)
-    from_b, from_a, from_z = scratch[0:4], scratch[4:8], scratch[8:12]
-    work = scratch[12:16]
-    sends, recvs, note_sends, note_recvs, local_sems = scratch[16:]
-    loads = [
-        pltpu.make_async_copy(src, dst, local_sems.at[i])
-        for i, (src, dst) in enumerate(zip((query_ref, key_ref, value_ref, out_ref), work))
-    ]
-    for c in loads:
-        c.start()
+    count = 4 * line
+    work, rest = scratch[:5], scratch[5:30]
+    total, last_sems, note_sends, note_recvs, local_sems = scratch[30:]
+    reduces = [Reduce(place, work[i], *rest[5 * i : 5 * i + 5]) for i in range(5)]
+
+    def loads(i, slot):
+        source = mix_ref.at[slot] if i == 4 else (query_ref, key_ref, value_ref, out_ref)[i].at[part_of(place, slot)]
+        return pltpu.make_async_copy(source, work[i].at[slot], local_sems.at[i, slot])
+
+    def begin(slot, carry):
+        for i in range(5):
+            loads(i, slot).start()
+        return carry
+
+    lax.fori_loop(0, count, begin, 0)
     enter(place)
     notes = [
         Notes(place, peak_ref, peaks, note_sends.at[0], note_recvs.at[0], True),
@@ -1040,49 +1159,62 @@
     ]
     for n in notes:
         n.start()
-    for c in loads:
-        c.wait()
-    reduces = [
-        Reduce(place, work[i], from_b[i], from_a[i], from_z[i], (sends.at[i], recvs.at[i]))
-        for i in (3, 0, 1, 2)
-    ]
-    for r in reduces:
-        for a in (1 - place.a, place.a):
-            for z in ends_first(line):
-                r.send_b(z, a)
-    reduce_rest(reduces)
-    for r, out in zip(reduces, (out_sum, query_sum, key_sum, value_sum)):
-        r.result(out)
+
+    def loaded(slot, carry):
+        for i in range(5):
+            loads(i, slot).wait()
+        return carry
+
+    lax.fori_loop(0, count, loaded, 0)
+    order = [reduces[i] for i in (4, 3, 0, 1, 2)]
+    mine, _ = halves(place, mix_sum.shape[1])
+    for r in order:
+        for k in [line + z for z in ends_first(line)] + ends_first(line):
+            r.send_b(k)
+    for r in order:
+        r.fold_line_a()
+        r.fold_line_own()
+        r.finish_line()
+    outs = (query_sum, key_sum, value_sum, out_sum, total)
+    reduces[4].result(total)
+    mix_sum[:, mine] = total[...]
+    last = remote(total, mix_sum.at[:, mine], last_sems.at[0], last_sems.at[1], place.twin())
+    last.start()
+    for i in (3, 0, 1, 2):
+        reduces[i].result(outs[i])
     for r in reduces:
         r.settle()
     for n in notes:
         n.finish()
-
-
-def reduce_grads(line, grads, peak, gain):
+    last.wait()
+
+
+def reduce_grads(line, grads, mix, peak, gain):
     count = 4 * line
-    blocks = [g.shape[1:] for g in grads]
-    many = lambda n: [pltpu.VMEM((n, *s), BF16) for s in blocks]
+    blocks = [g.shape[1:] for g in grads] + [mix.shape[1:]]
+    rows, half = blocks[4]
     return pl.pallas_call(
         functools.partial(grads_kernel, line),
-        out_shape=[jax.ShapeDtypeStruct(s, F32) for s in blocks]
-        + [jax.ShapeDtypeStruct((count, *peak.shape), F32), jax.ShapeDtypeStruct(gain.shape, F32)],
-        in_specs=[ANY] * 4 + [IN_VMEM] * 2,
-        out_specs=[IN_VMEM] * 6,
-        scratch_shapes=many(2 * line)
-        + many(line)
-        + many(2 * line)
-        + many(count)
+        out_shape=[jax.ShapeDtypeStruct(s, F32) for s in blocks[:4]]
         + [
-            pltpu.SemaphoreType.DMA((4, 5 * line)),
-            pltpu.SemaphoreType.DMA((4, 5 * line)),
+            jax.ShapeDtypeStruct((rows, 2 * half), F32),
+            jax.ShapeDtypeStruct((count, *peak.shape), F32),
+            jax.ShapeDtypeStruct(gain.shape, F32),
+        ],
+        in_specs=[ANY] * 5 + [IN_VMEM] * 2,
+        out_specs=[IN_VMEM] * 7,
+        scratch_shapes=[pltpu.VMEM((count, *s), BF16) for s in blocks]
+        + [x for s in blocks for x in reduce_scratch(line, s)]
+        + [
+            pltpu.VMEM((rows, half), F32),
+            pltpu.SemaphoreType.DMA((2,)),
             pltpu.SemaphoreType.DMA((2, count)),
             pltpu.SemaphoreType.DMA((2, count)),
-            pltpu.SemaphoreType.DMA((4,)),
+            pltpu.SemaphoreType.DMA((5, count)),
         ],
         compiler_params=params(3),
         name="reduce_grads",
-    )(*grads, peak, gain)
+    )(*grads, mix, peak, gain)
 
 
 def note_tiles(*rows):
@@ -1135,7 +1267,6 @@
     key_weight = key_all.reshape(model_width, kv_cols)
     value_weight = value_all.reshape(model_width, kv_cols)
     out_w = out_all.reshape(model_width, q_cols)
-    expert_gate = notes[:, 0, :length].reshape(count * length, 1)
     attn_gain_f = notes[:, 1, :shard].reshape(model_width)
     moe_gain_f = notes[:, 2, :shard].reshape(model_width)
     inputs = tokens.astype(F32)
@@ -1181,20 +1312,9 @@
     inv_moe = lax.rsqrt(jnp.mean(hidden * hidden, axis=1, keepdims=True) + EPSILON)
     unit_moe = hidden * inv_moe
     moe_in = (unit_moe * moe_gain_f).astype(BF16)
-    expert_in = gather_rows(line, moe_in).reshape(count * length, model_width)
-    gate_w, up_w, down_w = (w_gate[0], w_up[0], w_down[0])
-    expert_out, kept_acts = expert_forward(expert_in, gate_w, up_w, down_w)
-    grad_rows = (
-        expert_gate * (RESIDUAL * cot_all.reshape(count * length, model_width).astype(F32))
-    ).astype(BF16)
-    d_inputs, grad_gate, grad_up, grad_down = expert_backward(
-        expert_in, grad_rows, gate_w, up_w, down_w, kept_acts
-    )
-    mix_out = (expert_gate * expert_out).astype(BF16).reshape(count, length, model_width)
-    d_moe_in, expert_mix = reduce_experts(
-        line, d_inputs.astype(BF16).reshape(count, length, model_width), mix_out
-    )
-    output = (hidden + RESIDUAL * expert_mix).astype(BF16)
+    d_moe_in, mix_parts, grad_gate, grad_up, grad_down = run_experts(
+        line, moe_in, cot_all, notes, w_gate[0], w_up[0], w_down[0]
+    )
     grad_output = cotangent.astype(F32)
     scaled_moe = d_moe_in * moe_gain_f
     grad_moe_gain = jnp.sum(d_moe_in * unit_moe, axis=0)
@@ -1241,9 +1361,10 @@
     )
     peak_tile = note_tiles(own_peak)[0]
     gain_tiles = note_tiles(grad_attn_gain.reshape(count, shard), grad_moe_gain.reshape(count, shard))
-    grad_query, grad_key, grad_value, grad_out, peaks, gains = reduce_grads(
-        line, grads, peak_tile, gain_tiles
-    )
+    grad_query, grad_key, grad_value, grad_out, expert_mix, peaks, gains = reduce_grads(
+        line, grads, mix_parts, peak_tile, gain_tiles
+    )
+    output = (hidden + RESIDUAL * expert_mix).astype(BF16)
     head_peak = jnp.max(peaks[:, 0, :q_heads], axis=0)
     gain_sums = jnp.sum(gains, axis=0)
     scale_factor = CLIP_LIMIT / jnp.maximum(head_peak, CLIP_LIMIT)
@@ -1278,7 +1399,7 @@
     count, ranks = lax.axis_size("dp"), lax.axis_size("tensor")
     rows_bytes = count * tokens.shape[0] * tokens.shape[1] * 2
     whole_experts = w_gate.shape[2] * ranks == FFE
-    dense = whole_experts and ranks == 2 and count % 4 == 0 and rows_bytes <= DENSE_BYTES
+    dense = whole_experts and ranks == 2 and count % 8 == 0 and rows_bytes <= DENSE_BYTES
     return on_device_dense(*args) if dense else on_device_general(*args)
 
 

time: 479 us -> 444 us (0.927); the launches traced: 473 us -> 443 us
  matrix products: 62.9 us -> 24.8 us
  Pallas kernels: 350 us -> 370 us
  other arithmetic: 35.7 us -> 25.6 us
    pallas_call x1, Pallas kernels: 92.3 us -> 125 us  [reduce_grads(): pl.pallas_call(functools.partial(grads_kernel, line), out_shape=[jax.Shap...]
    pallas_call x2 -> x1, Pallas kernels: 135 us -> 117 us  [run_experts(): pl.pallas_call(functools.partial(experts_kernel, line), out_shape=[jax.Sh...]
    dot_general x3 -> x0, matrix products: 13.4 us -> none  [the longest x1 6.13 us: expert_forward(): gate_pre = jnp.dot(inputs, gate_w, preferred_element_type=jnp.float32)]
    dot_general x7 -> x4, matrix products: 16 us -> 4.24 us  [contract_cols(): lax.dot_general(left, right, (((1,), (1,)), ((), ())), preferred_element_...]
    dot_general x7 -> x4, matrix products: 16.6 us -> 7.18 us  [contract_rows(): lax.dot_general(left, right, (((0,), (0,)), ((), ())), preferred_element_...]
    convert_element_type x2 -> x0, other arithmetic: 7.45 us -> none  [on_device_dense(): grad_rows = (expert_gate * (RESIDUAL * cot_all.reshape(count * length, mo...]
    pallas_call x1, Pallas kernels: 114 us -> 119 us  [gather_weights(): pl.pallas_call(functools.partial(weights_kernel, line), out_shape=[jax.Sh...]
    unnamed x102 -> x83, local copies, waits for them, and re-layouts: 8.41 us -> 12.1 us
where the time goes in v2:
time: 444 us; the launch traced here: 443 us
  Pallas kernels  370 us (83%)
  other arithmetic  25.6 us (6%)
  matrix products  24.8 us (6%)
  local copies, waits for them, and re-layouts  21.7 us (5%)
    pallas_call x1, Pallas kernels, reduce_grads(): pl.pallas_call(functools.partial(grads_kernel, line), out_shape=[jax.Shap...  125 us
    pallas_call x1, Pallas kernels, gather_weights(): pl.pallas_call(functools.partial(weights_kernel, line), out_shape=[jax.Sh...  119 us
    pallas_call x1, Pallas kernels, run_experts(): pl.pallas_call(functools.partial(experts_kernel, line), out_shape=[jax.Sh...  117 us
    unnamed x83, local copies, waits for them, and re-layouts  12.1 us

profile of v2, /device:TPU:0, one launch (start us, length us, event | category | flops | bytes accessed | tf_op | source)
XLA Modules:
  0.0 443.0 jit_solution(10831989077681112070)
XLA Ops:
  0.7 0.8 convert_reduce_fusion
  1.5 0.9 select_reduce_fusion.5
  3.3 0.7 select_reduce_fusion.4
  4.0 0.8 multiply_cosine_fusion
  6.9 0.7 select_reduce_fusion
  9.7 119.4 %gather_weights.1 = (bf16[16,96,768]{2,1,0:T(8,128)(2,1)}, bf16[16,96,256]{2,1,0:T(8,128)(2,1)}, bf16[16,96,256]{2,1,0:T(8,128)(2,1)}, bf16[16,96,768]{2,1,0:T(8...) custom-call(bf16[96,768]{1,0:T(8,128)(2,1)} %query_ref.1, bf16[96,256]{1,0:T(8,128)(2,1)} %key_ref.1, ...), custom_call_target="tpu_custom_call" | custom-call | tf_op jit(solution)/shard_map/gather_weights/pallas_call | solution.py:860
  129.1 1.7 slice_reduce_fusion.1
  131.4 1.4 copy.54
  133.0 1.1 fusion.25
  134.1 1.4 subtract_convert_fusion.1
  135.5 2.5 copy.55
  138.0 2.6 fusion.23
  141.5 1.9 fusion.71
  143.4 1.8 convolution_convert_fusion.6
  145.2 0.9 copy.52
  146.2 1.6 convolution_convert_fusion.5
  147.8 1.8 fusion.73.mine_ref
  149.5 4.4 twin_sum.2
  154.0 1.3 multiply_reduce_fusion.3
  155.4 0.9 multiply_convert_fusion.2.rows_ref
  156.3 117.4 %run_experts.1 = (f32[128,1536]{1,0:T(8,128)}, bf16[16,128,768]{2,1,0:T(8,128)(2,1)}, f32[1536,256]{1,0:T(8,128)}, f32[1536,256]{1,0:T(8,128)}, f32[1536,256]{1,0:T(8,128)}) custom-call(bf16[128,1536]{1,0:T(8,128)(2,1)} %multiply_convert_fusion.2.rows_ref, bf16[16,128,1536]{2,1,0:T(8,128)(2,1)} %get-tuple-element.36.cot_ref, ...), custom_call_target="tpu_custom_call" | custom-call | tf_op jit(solution)/shard_map/run_experts/pallas_call | solution.py:1083
  273.7 1.6 multiply_reduce_fusion
  275.3 1.4 multiply_add_fusion
  277.7 1.3 fusion.12
  279.0 1.2 multiply_reduce_fusion.1
  281.0 0.8 copy-done.4
  281.8 0.9 fusion.74
  283.2 1.2 fusion.1.mine_ref
  284.4 3.7 twin_sum.3
  288.1 1.4 fusion.18
  291.8 2.2 convolution_convert_fusion
  294.0 1.3 convolution_convert_fusion.2
  295.4 1.3 convolution_convert_fusion.3
  296.7 2.3 convolution_convert_fusion.1
  299.0 124.6 %reduce_grads.1 = (f32[96,768]{1,0:T(8,128)}, f32[96,256]{1,0:T(8,128)}, f32[96,256]{1,0:T(8,128)}, f32[96,768]{1,0:T(8,128)}, f32[128,1536]{1,0:T(8,128)}, /*in...) custom-call(bf16[16,96,768]{2,1,0:T(8,128)(2,1)} %bitcast.148, bf16[16,96,256]{2,1,0:T(8,128)(2,1)} %bitcast.150, ...), custom_call_target="tpu_custom_call" | custom-call | tf_op jit(solution)/shard_map/reduce_grads/pallas_call | solution.py:1196
  423.7 2.6 fusion.21
  426.3 0.9 slice_reduce_fusion
  427.3 1.7 convert_multiply_fusion.2
  429.3 1.5 convert_multiply_fusion.3
  430.8 0.9 reduce_sum.185
  432.1 1.8 copy.76
  434.0 1.5 copy.77
  435.5 1.5 copy.78
  437.0 1.7 copy.79
  438.7 1.1 copy.80
  439.9 1.1 copy.81
  441.0 0.8 copy-done.7
  441.9 1.1 copy.82
  (131 shorter events, 12.1 us)
Async XLA Ops:
  0.6 132.2 %copy-start = (bf16[128,1536]{1,0:T(8,128)(2,1)S(1)}, bf16[128,1536]{1,0:T(8,128)(2,1)}, u32[]{:S(2)}) copy-start(bf16[128,1536]{1,0:T(8,128)(2,1)} %param.15) | copy-start | bytes 1179652
  2.4 2.4 copy-start.36
  9.0 0.7 copy-start.21
  129.1 6.5 %copy-start.3 = (bf16[16,96,768]{2,1,0:T(8,128)(2,1)S(1)}, bf16[16,96,768]{2,1,0:T(8,128)(2,1)}, u32[]{:S(2)}) copy-start(bf16[16,96,768]{2,1,0:T(8,128)(2,1)} %get-tuple-element.34) | copy-start | bytes 7077892
  133.0 2.5 copy-start.29
  138.0 2.7 copy-start.14
  138.0 2.8 copy-start.34
  138.0 2.8 copy-start.35
  138.0 2.8 copy-start.37
  138.0 3.4 copy-start.23
  138.0 3.4 copy-start.25
  138.0 5.3 %copy-start.11 = (bf16[16,96,256]{2,1,0:T(8,128)(2,1)S(1)}, bf16[16,96,256]{2,1,0:T(8,128)(2,1)}, u32[]{:S(2)}) copy-start(bf16[16,96,256]{2,1,0:T(8,128)(2,1)} %get-tuple-element.32) | copy-start | bytes 2359300
  140.7 2.6 copy-start.17
  140.8 2.6 copy-start.19
  141.5 1.9 copy-start.31
  143.4 4.4 copy-start.1
  146.2 3.4 copy-start.27
  149.5 5.8 %copy-start.28 = (f32[16,96]{1,0:T(8,128)S(1)}, f32[16,96]{1,0:T(8,128)}, u32[]{:S(2)}) copy-start(f32[16,96]{1,0:T(8,128)} %get-tuple-element.53) | copy-start | bytes 18436
  156.3 119.0 %copy-start.10 = (bf16[128,1536]{1,0:T(8,128)(2,1)S(1)}, bf16[128,1536]{1,0:T(8,128)(2,1)}, u32[]{:S(2)}) copy-start(bf16[128,1536]{1,0:T(8,128)(2,1)} %cot_ref.1) | copy-start | bytes 1179652
  273.7 3.0 copy-start.2
  276.7 0.9 copy-start.18
  276.7 0.9 copy-start.20
  276.7 0.9 copy-start.24
  276.7 0.9 copy-start.26
  276.8 0.9 copy-start.33
  277.4 1.6 copy-start.13
  279.0 1.6 copy-start.15
  280.2 1.7 copy-start.4
  280.9 1.9 copy-start.6
  281.8 1.4 copy-start.12
  282.7 5.3 %copy-start.16 = (f32[1536]{0:T(1024)S(1)}, f32[1536]{0:T(1024)}, u32[]{:S(2)}) copy-start(f32[1536]{0:T(1024)} %mul.324) | copy-start | bytes 18436
  282.8 5.3 %copy-start.30 = (f32[128]{0:T(128)S(1)}, f32[128]{0:T(128)}, u32[]{:S(2)}) copy-start(f32[128]{0:T(128)} %copy-done.29) | copy-start | bytes 1540
  283.2 6.6 %copy-start.22 = (f32[16,4,128]{2,1,0:T(4,128)S(1)}, f32[16,4,128]{2,1,0:T(4,128)}, u32[]{:S(2)}) copy-start(f32[16,4,128]{2,1,0:T(4,128)} %copy-done.21) | copy-start | bytes 98308
  283.2 7.3 %copy-start.32 = (pred[128,128]{0,1:T(8,128)(4,1)S(1)}, pred[128,128]{0,1:T(8,128)(4,1)}, u32[]{:S(2)}) copy-start(pred[128,128]{0,1:T(8,128)(4,1)} %copy-done.31) | copy-start | bytes 49156
  299.0 124.7 %copy-start.5 = (f32[128,1536]{1,0:T(8,128)S(1)}, f32[128,1536]{1,0:T(8,128)}, u32[]{:S(2)}) copy-start(f32[128,1536]{1,0:T(8,128)} %twin_sum.3) | copy-start | bytes 2359300
  423.7 15.0 %copy-start.9 = (f32[1536,256]{1,0:T(8,128)S(1)}, f32[1536,256]{1,0:T(8,128)}, u32[]{:S(2)}) copy-start(f32[1536,256]{1,0:T(8,128)} %get-tuple-element.45) | copy-start | bytes 4718596
  432.1 7.7 %copy-start.8 = (f32[1536,256]{1,0:T(8,128)S(1)}, f32[1536,256]{1,0:T(8,128)}, u32[]{:S(2)}) copy-start(f32[1536,256]{1,0:T(8,128)} %get-tuple-element.46) | copy-start | bytes 4718596
  439.9 2.0 copy-start.7

commit v3 on v2

--- a/solution.py
+++ b/solution.py
@@ -590,12 +590,13 @@
 def gather_all(gathers, thens=None):
     line = gathers[0].place.line
     thens = thens or [None] * len(gathers)
-    for g in gathers:
-        g.start()
-    for step in range(1, line + 1):
-        for g, then in zip(gathers, thens):
+    gathers[0].start()
+    for i, (g, then) in enumerate(zip(gathers, thens)):
+        for step in range(1, line + 1):
             if step < line:
                 g.along(step, then)
+            if step == line - 1 and i + 1 < len(gathers):
+                gathers[i + 1].start()
             g.across(step - 1, then)
 
 
@@ -649,11 +650,15 @@
         line = self.place.line
         return self._copy(self.parts.at[line + z], self.from_a.at[z], 2 * line + z, self.place.beside_a())
 
-    def _along(self, z, way):
-        place = self.place
-        slot = way * place.line + z
-        device = place.up() if way == 0 else place.down()
-        return self._copy(self.parts.at[z], self.from_z.at[slot], 3 * place.line + slot, device)
+    def _to_z(self, target):
+        place, line = self.place, self.place.line
+        return remote(
+            self.parts.at[target],
+            self.from_z.at[place.z],
+            self.send_sem.at[3 * line + target],
+            self.recv_sem.at[3 * line + place.z],
+            (place.me + 4 * (target - place.z), place.core),
+        )
 
     def _add(self, slot, block):
         self.parts[slot] = (self.parts[slot].astype(F32) + block.astype(F32)).astype(BF16)
@@ -672,29 +677,10 @@
         self._to_a(z).wait_recv()
         self._add(z, self.from_a[z])
 
-    def pass_up(self, z):
+    def send_line(self):
         place = self.place
-
-        @pl.when(place.z < z)
-        def _():
-            @pl.when(place.z > 0)
-            def _():
-                self._along(z, 0).wait_recv()
-                self._add(z, self.from_z[z])
-
-            self._along(z, 0).start()
-
-    def pass_down(self, z):
-        place, line = self.place, self.place.line
-
-        @pl.when(place.z > z)
-        def _():
-            @pl.when(place.z < line - 1)
-            def _():
-                self._along(z, 1).wait_recv()
-                self._add(z, self.from_z[line + z])
-
-            self._along(z, 1).start()
+        for z in ends_first(place.line):
+            pl.when(place.z != z)(lambda z=z: self._to_z(z).start())
 
     def fold_line_a(self):
         line = self.place.line
@@ -707,27 +693,25 @@
             self.fold_b(z)
 
     def finish_line(self):
-        line = self.place.line
-        for z in ends_first(line):
+        for z in ends_first(self.place.line):
             self.fold_a(z)
-        for k in range(line):
-            self.pass_up(line - 1 - k)
-            self.pass_down(k)
+        self.send_line()
 
     def result(self, out):
         place, line = self.place, self.place.line
-        z = place.z
-        out[...] = self.parts[z].astype(F32)
-
-        @pl.when(z > 0)
-        def _():
-            self._along(z, 0).wait_recv()
-            out[...] += self.from_z[z].astype(F32)
-
-        @pl.when(z < line - 1)
-        def _():
-            self._along(z, 1).wait_recv()
-            out[...] += self.from_z[line + z].astype(F32)
+        out[...] = self.parts[place.z].astype(F32)
+
+        def add(z, carry):
+            @pl.when(z != place.z)
+            def _():
+                remote(
+                    self.parts.at[z], self.from_z.at[z], self.send_sem.at[0], self.recv_sem.at[3 * line + z], place.up()
+                ).wait_recv()
+                out[...] += self.from_z[z].astype(F32)
+
+            return carry
+
+        lax.fori_loop(0, line, add, 0)
 
     def settle(self):
         place, line = self.place, self.place.line
@@ -736,20 +720,43 @@
             self._to_b(z).wait_send()
             self._to_b(line + z).wait_send()
             self._to_a(z).wait_send()
-            pl.when(place.z < z)(lambda: self._along(z, 0).wait_send())
-            pl.when(place.z > z)(lambda: self._along(z, 1).wait_send())
+            pl.when(place.z != z)(lambda: self._to_z(z).wait_send())
             return carry
 
         lax.fori_loop(0, line, wait, 0)
+
+
+AHEAD = 4
+
+
+def reduce_all(reduces, finish):
+    line = reduces[0].place.line
+    ks = [line + z for z in ends_first(line)] + ends_first(line)
+    steps = [(i, k) for i in range(len(reduces)) for k in ks]
+    for i, k in steps[:AHEAD]:
+        reduces[i].send_b(k)
+    for at, (i, k) in enumerate(steps):
+        if at + AHEAD < len(steps):
+            ahead, block = steps[at + AHEAD]
+            reduces[ahead].send_b(block)
+        reduces[i].fold_b(k)
+        if k >= line:
+            reduces[i].send_a(k - line)
+        if k == ks[line - 1] and i > 0:
+            reduces[i - 1].finish_line()
+        if k == ks[-1] and i > 0:
+            finish(i - 1)
+    reduces[-1].finish_line()
+    finish(len(reduces) - 1)
 
 
 def reduce_scratch(line, block):
     return [
         pltpu.VMEM((2 * line, *block), BF16),
         pltpu.VMEM((line, *block), BF16),
-        pltpu.VMEM((2 * line, *block), BF16),
-        pltpu.SemaphoreType.DMA((5 * line,)),
-        pltpu.SemaphoreType.DMA((5 * line,)),
+        pltpu.VMEM((line, *block), BF16),
+        pltpu.SemaphoreType.DMA((4 * line,)),
+        pltpu.SemaphoreType.DMA((4 * line,)),
     ]
 
 
@@ -1166,22 +1173,19 @@
         return carry
 
     lax.fori_loop(0, count, loaded, 0)
-    order = [reduces[i] for i in (4, 3, 0, 1, 2)]
     mine, _ = halves(place, mix_sum.shape[1])
-    for r in order:
-        for k in [line + z for z in ends_first(line)] + ends_first(line):
-            r.send_b(k)
-    for r in order:
-        r.fold_line_a()
-        r.fold_line_own()
-        r.finish_line()
     outs = (query_sum, key_sum, value_sum, out_sum, total)
-    reduces[4].result(total)
-    mix_sum[:, mine] = total[...]
+    order = (4, 3, 0, 1, 2)
     last = remote(total, mix_sum.at[:, mine], last_sems.at[0], last_sems.at[1], place.twin())
-    last.start()
-    for i in (3, 0, 1, 2):
+
+    def finish(at):
+        i = order[at]
         reduces[i].result(outs[i])
+        if i == 4:
+            mix_sum[:, mine] = total[...]
+            last.start()
+
+    reduce_all([reduces[i] for i in order], finish)
     for r in reduces:
         r.settle()
     for n in notes:

time: 444 us -> 409 us (0.921)
  Pallas kernels: 370 us -> 334 us
    pallas_call x1, Pallas kernels: 125 us -> 107 us  [reduce_grads(): pl.pallas_call(functools.partial(grads_kernel, line), out_shape=[jax.Shap...]
    pallas_call x1, Pallas kernels: 117 us -> 101 us  [run_experts(): pl.pallas_call(functools.partial(experts_kernel, line), out_shape=[jax.Sh...]
where the time goes in v3:
time: 409 us; the launch traced here: 407 us
  Pallas kernels  334 us (82%)
  other arithmetic  25.6 us (6%)
  matrix products  24.8 us (6%)
  local copies, waits for them, and re-layouts  21.7 us (5%)
    pallas_call x1, Pallas kernels, gather_weights(): pl.pallas_call(functools.partial(weights_kernel, line), out_shape=[jax.Sh...  118 us
    pallas_call x1, Pallas kernels, reduce_grads(): pl.pallas_call(functools.partial(grads_kernel, line), out_shape=[jax.Shap...  107 us
    pallas_call x1, Pallas kernels, run_experts(): pl.pallas_call(functools.partial(experts_kernel, line), out_shape=[jax.Sh...  101 us
    unnamed x83, local copies, waits for them, and re-layouts  12.1 us

profile of v3, /device:TPU:0, one launch (start us, length us, event | category | flops | bytes accessed | tf_op | source)
XLA Modules:
  0.0 407.3 jit_solution(9724743653973628101)
XLA Ops:
  0.7 0.8 convert_reduce_fusion
  1.5 0.9 select_reduce_fusion.5
  3.3 0.7 select_reduce_fusion.4
  4.0 0.8 multiply_cosine_fusion
  6.9 0.7 select_reduce_fusion
  9.7 117.8 %gather_weights.1 = (bf16[16,96,768]{2,1,0:T(8,128)(2,1)}, bf16[16,96,256]{2,1,0:T(8,128)(2,1)}, bf16[16,96,256]{2,1,0:T(8,128)(2,1)}, bf16[16,96,768]{2,1,0:T(8...) custom-call(bf16[96,768]{1,0:T(8,128)(2,1)} %query_ref.1, bf16[96,256]{1,0:T(8,128)(2,1)} %key_ref.1, ...), custom_call_target="tpu_custom_call" | custom-call | tf_op jit(solution)/shard_map/gather_weights/pallas_call | solution.py:867
  127.5 1.7 slice_reduce_fusion.1
  129.8 1.4 copy.54
  131.4 1.1 fusion.25
  132.5 1.4 subtract_convert_fusion.1
  133.9 2.5 copy.55
  136.5 2.6 fusion.23
  139.9 1.9 fusion.71
  141.8 1.8 convolution_convert_fusion.6
  143.6 0.9 copy.52
  144.6 1.6 convolution_convert_fusion.5
  146.2 1.8 fusion.73.mine_ref
  148.0 4.4 %twin_sum.2 = f32[128,1536]{1,0:T(8,128)} custom-call(f32[128,1536]{1,0:T(8,128)} %fusion.73.mine_ref), custom_call_target="tpu_custom_call" | custom-call | tf_op jit(solution)/shard_map/twin_sum/pallas_call | solution.py:898
  152.4 1.3 multiply_reduce_fusion.3
  153.8 0.9 multiply_convert_fusion.2.rows_ref
  154.7 101.1 %run_experts.1 = (f32[128,1536]{1,0:T(8,128)}, bf16[16,128,768]{2,1,0:T(8,128)(2,1)}, f32[1536,256]{1,0:T(8,128)}, f32[1536,256]{1,0:T(8,128)}, f32[1536,256]{1,0:T(8,128)}) custom-call(bf16[128,1536]{1,0:T(8,128)(2,1)} %multiply_convert_fusion.2.rows_ref, bf16[16,128,1536]{2,1,0:T(8,128)(2,1)} %get-tuple-element.36.cot_ref, ...), custom_call_target="tpu_custom_call" | custom-call | tf_op jit(solution)/shard_map/run_experts/pallas_call | solution.py:1090
  255.8 1.6 multiply_reduce_fusion
  257.4 1.4 multiply_add_fusion
  259.7 1.3 fusion.12
  261.1 1.2 multiply_reduce_fusion.1
  263.0 0.8 copy-done.4
  263.9 0.9 fusion.74
  265.3 1.2 fusion.1.mine_ref
  266.4 3.7 twin_sum.3
  270.2 1.4 fusion.18
  273.9 2.2 convolution_convert_fusion
  276.1 1.3 convolution_convert_fusion.2
  277.4 1.3 convolution_convert_fusion.3
  278.8 2.3 convolution_convert_fusion.1
  281.1 106.9 %reduce_grads.1 = (f32[96,768]{1,0:T(8,128)}, f32[96,256]{1,0:T(8,128)}, f32[96,256]{1,0:T(8,128)}, f32[96,768]{1,0:T(8,128)}, f32[128,1536]{1,0:T(8,128)}, /*in...) custom-call(bf16[16,96,768]{2,1,0:T(8,128)(2,1)} %bitcast.148, bf16[16,96,256]{2,1,0:T(8,128)(2,1)} %bitcast.150, ...), custom_call_target="tpu_custom_call" | custom-call | tf_op jit(solution)/shard_map/reduce_grads/pallas_call | solution.py:1200
  388.0 2.6 fusion.21
  390.6 0.9 slice_reduce_fusion
  391.6 1.7 convert_multiply_fusion.2
  393.6 1.5 convert_multiply_fusion.3
  395.1 0.9 reduce_sum.185
  396.5 1.8 copy.76
  398.3 1.5 copy.77
  399.8 1.5 copy.78
  401.4 1.7 copy.79
  403.1 1.1 copy.80
  404.2 1.1 copy.81
  405.3 0.8 copy-done.7
  406.2 1.1 copy.82
  (131 shorter events, 12.1 us)
Async XLA Ops:
  0.6 130.6 %copy-start = (bf16[128,1536]{1,0:T(8,128)(2,1)S(1)}, bf16[128,1536]{1,0:T(8,128)(2,1)}, u32[]{:S(2)}) copy-start(bf16[128,1536]{1,0:T(8,128)(2,1)} %param.15) | copy-start | bytes 1179652
  2.4 2.4 copy-start.36
  9.0 0.7 copy-start.21
  127.5 6.5 %copy-start.3 = (bf16[16,96,768]{2,1,0:T(8,128)(2,1)S(1)}, bf16[16,96,768]{2,1,0:T(8,128)(2,1)}, u32[]{:S(2)}) copy-start(bf16[16,96,768]{2,1,0:T(8,128)(2,1)} %get-tuple-element.34) | copy-start | bytes 7077892
  131.4 2.5 copy-start.29
  136.4 2.7 copy-start.14
  136.4 2.8 copy-start.34
  136.4 2.8 copy-start.35
  136.4 2.8 copy-start.37
  136.4 3.4 copy-start.23
  136.4 3.4 copy-start.25
  136.5 5.3 %copy-start.11 = (bf16[16,96,256]{2,1,0:T(8,128)(2,1)S(1)}, bf16[16,96,256]{2,1,0:T(8,128)(2,1)}, u32[]{:S(2)}) copy-start(bf16[16,96,256]{2,1,0:T(8,128)(2,1)} %get-tuple-element.32) | copy-start | bytes 2359300
  139.2 2.6 copy-start.17
  139.2 2.6 copy-start.19
  139.9 1.9 copy-start.31
  141.8 4.4 %copy-start.1 = (bf16[16,96,768]{2,1,0:T(8,128)(2,1)S(1)}, bf16[16,96,768]{2,1,0:T(8,128)(2,1)}, u32[]{:S(2)}) copy-start(bf16[16,96,768]{2,1,0:T(8,128)(2,1)} %get-tuple-element.35) | copy-start | bytes 7077892
  144.6 3.4 copy-start.27
  148.0 5.8 %copy-start.28 = (f32[16,96]{1,0:T(8,128)S(1)}, f32[16,96]{1,0:T(8,128)}, u32[]{:S(2)}) copy-start(f32[16,96]{1,0:T(8,128)} %get-tuple-element.53) | copy-start | bytes 18436
  154.7 102.7 %copy-start.10 = (bf16[128,1536]{1,0:T(8,128)(2,1)S(1)}, bf16[128,1536]{1,0:T(8,128)(2,1)}, u32[]{:S(2)}) copy-start(bf16[128,1536]{1,0:T(8,128)(2,1)} %cot_ref.1) | copy-start | bytes 1179652
  255.8 3.0 copy-start.2
  258.8 0.9 copy-start.18
  258.8 0.9 copy-start.20
  258.8 0.9 copy-start.24
  258.8 0.9 copy-start.26
  258.8 0.9 copy-start.33
  259.5 1.6 copy-start.13
  261.0 1.6 copy-start.15
  262.2 1.7 copy-start.4
  262.9 1.9 copy-start.6
  263.9 1.4 copy-start.12
  264.8 5.3 %copy-start.16 = (f32[1536]{0:T(1024)S(1)}, f32[1536]{0:T(1024)}, u32[]{:S(2)}) copy-start(f32[1536]{0:T(1024)} %mul.324) | copy-start | bytes 18436
  264.8 5.3 %copy-start.30 = (f32[128]{0:T(128)S(1)}, f32[128]{0:T(128)}, u32[]{:S(2)}) copy-start(f32[128]{0:T(128)} %copy-done.29) | copy-start | bytes 1540
  265.3 6.6 %copy-start.22 = (f32[16,4,128]{2,1,0:T(4,128)S(1)}, f32[16,4,128]{2,1,0:T(4,128)}, u32[]{:S(2)}) copy-start(f32[16,4,128]{2,1,0:T(4,128)} %copy-done.21) | copy-start | bytes 98308
  265.3 7.3 %copy-start.32 = (pred[128,128]{0,1:T(8,128)(4,1)S(1)}, pred[128,128]{0,1:T(8,128)(4,1)}, u32[]{:S(2)}) copy-start(pred[128,128]{0,1:T(8,128)(4,1)} %copy-done.31) | copy-start | bytes 49156
  281.1 106.9 %copy-start.5 = (f32[128,1536]{1,0:T(8,128)S(1)}, f32[128,1536]{1,0:T(8,128)}, u32[]{:S(2)}) copy-start(f32[128,1536]{1,0:T(8,128)} %twin_sum.3) | copy-start | bytes 2359300
  388.0 15.0 %copy-start.9 = (f32[1536,256]{1,0:T(8,128)S(1)}, f32[1536,256]{1,0:T(8,128)}, u32[]{:S(2)}) copy-start(f32[1536,256]{1,0:T(8,128)} %get-tuple-element.45) | copy-start | bytes 4718596
  396.5 7.7 %copy-start.8 = (f32[1536,256]{1,0:T(8,128)S(1)}, f32[1536,256]{1,0:T(8,128)}, u32[]{:S(2)}) copy-start(f32[1536,256]{1,0:T(8,128)} %get-tuple-element.46) | copy-start | bytes 4718596
  404.2 2.0 copy-start.7

commit v4 on v3

--- a/solution.py
+++ b/solution.py
@@ -634,8 +634,8 @@
 
 
 class Reduce:
-    def __init__(self, place, parts, from_b, from_a, from_z, send_sem, recv_sem):
-        self.place, self.parts = place, parts
+    def __init__(self, place, parts, from_b, from_a, from_z, send_sem, recv_sem, index=lambda slot: slot):
+        self.place, self.parts, self.index = place, parts, index
         self.from_b, self.from_a, self.from_z = from_b, from_a, from_z
         self.send_sem, self.recv_sem = send_sem, recv_sem
 
@@ -644,16 +644,17 @@
 
     def _to_b(self, k):
         line = self.place.line
-        return self._copy(self.parts.at[2 * line + k], self.from_b.at[k], k, self.place.beside_b())
+        return self._copy(self.parts.at[self.index(2 * line + k)], self.from_b.at[k], k, self.place.beside_b())
 
     def _to_a(self, z):
         line = self.place.line
-        return self._copy(self.parts.at[line + z], self.from_a.at[z], 2 * line + z, self.place.beside_a())
+        block = self.parts.at[self.index(line + z)]
+        return self._copy(block, self.from_a.at[z], 2 * line + z, self.place.beside_a())
 
     def _to_z(self, target):
         place, line = self.place, self.place.line
         return remote(
-            self.parts.at[target],
+            self.parts.at[self.index(target)],
             self.from_z.at[place.z],
             self.send_sem.at[3 * line + target],
             self.recv_sem.at[3 * line + place.z],
@@ -661,7 +662,8 @@
         )
 
     def _add(self, slot, block):
-        self.parts[slot] = (self.parts[slot].astype(F32) + block.astype(F32)).astype(BF16)
+        at = self.index(slot)
+        self.parts[at] = (self.parts[at].astype(F32) + block.astype(F32)).astype(BF16)
 
     def send_b(self, k):
         self._to_b(k).start()
@@ -699,13 +701,13 @@
 
     def result(self, out):
         place, line = self.place, self.place.line
-        out[...] = self.parts[place.z].astype(F32)
+        out[...] = self.parts[self.index(place.z)].astype(F32)
 
         def add(z, carry):
             @pl.when(z != place.z)
             def _():
                 remote(
-                    self.parts.at[z], self.from_z.at[z], self.send_sem.at[0], self.recv_sem.at[3 * line + z], place.up()
+                    self.from_z.at[z], self.from_z.at[z], self.send_sem.at[0], self.recv_sem.at[3 * line + z], place.up()
                 ).wait_recv()
                 out[...] += self.from_z[z].astype(F32)
 
@@ -729,25 +731,39 @@
 AHEAD = 4
 
 
-def reduce_all(reduces, finish):
-    line = reduces[0].place.line
-    ks = [line + z for z in ends_first(line)] + ends_first(line)
-    steps = [(i, k) for i in range(len(reduces)) for k in ks]
-    for i, k in steps[:AHEAD]:
-        reduces[i].send_b(k)
-    for at, (i, k) in enumerate(steps):
-        if at + AHEAD < len(steps):
-            ahead, block = steps[at + AHEAD]
-            reduces[ahead].send_b(block)
-        reduces[i].fold_b(k)
-        if k >= line:
-            reduces[i].send_a(k - line)
-        if k == ks[line - 1] and i > 0:
-            reduces[i - 1].finish_line()
-        if k == ks[-1] and i > 0:
-            finish(i - 1)
-    reduces[-1].finish_line()
-    finish(len(reduces) - 1)
+class Reductions:
+    def __init__(self, reduces, finish):
+        self.reduces, self.finish, self.at = reduces, finish, 0
+        line = self.line = reduces[0].place.line
+        self.ks = [line + z for z in ends_first(line)] + ends_first(line)
+        self.steps = [(i, k) for i in range(len(reduces)) for k in self.ks]
+
+    def start(self):
+        for i, k in self.steps[:AHEAD]:
+            self.reduces[i].send_b(k)
+
+    def run(self, number):
+        for _ in range(number):
+            self._step()
+
+    def _step(self):
+        if self.at + AHEAD < len(self.steps):
+            ahead, block = self.steps[self.at + AHEAD]
+            self.reduces[ahead].send_b(block)
+        i, k = self.steps[self.at]
+        self.at += 1
+        self.reduces[i].fold_b(k)
+        if k >= self.line:
+            self.reduces[i].send_a(k - self.line)
+        if k == self.ks[self.line - 1] and i > 0:
+            self.reduces[i - 1].finish_line()
+        if k == self.ks[-1] and i > 0:
+            self.finish(i - 1)
+
+    def complete(self):
+        self.run(len(self.steps) - self.at)
+        self.reduces[-1].finish_line()
+        self.finish(len(self.reduces) - 1)
 
 
 def reduce_scratch(line, block):
@@ -783,29 +799,87 @@
     return mine, theirs
 
 
-def weights_kernel(
+def place_half(chunk, have, want, lane):
+    chunk = chunk if have == want else pltpu.roll(chunk, HEAD_SIZE, 1)
+    return jnp.where(lane // HEAD_SIZE == want, chunk, 0.0)
+
+
+def rope_chunk(chunk, tables, sign):
+    ahead = pltpu.roll(chunk, 128 - HEAD_SIZE // 2, 1)
+    behind = pltpu.roll(chunk, HEAD_SIZE // 2, 1)
+    return chunk * tables[0] + sign * (ahead * tables[1] + behind * tables[2])
+
+
+def chunk_of(ref, j):
+    return ref[:, 128 * j : 128 * (j + 1)]
+
+
+def pair_of(ref, j, group_size, lane):
+    both = []
+    for half in (0, 1):
+        group = (2 * j + half) // group_size
+        both.append(place_half(chunk_of(ref, group // 2).astype(F32), group % 2, half, lane))
+    return jnp.concatenate(both, axis=0).astype(BF16)
+
+
+def spread_gains(notes, shard, width):
+    total = jnp.zeros((8, width), F32)
+    for p in range(notes.shape[0]):
+        row = jnp.concatenate([notes[p], jnp.zeros((8, width - 128), F32)], axis=1)
+        total += pltpu.roll(row, shard * p, 1) if p else row
+    return total
+
+
+def forward_kernel(
     line,
+    group_size,
+    tokens_ref,
     query_ref,
     key_ref,
     value_ref,
     out_ref,
     cot_ref,
     note_ref,
+    tables_ref,
+    allowed_ref,
+    moe_in_ref,
+    hidden_ref,
+    normed_ref,
+    head_out_ref,
+    queries_ref,
+    keys_ref,
+    values_ref,
+    probs_ref,
+    peak_ref,
+    gains_ref,
+    notes,
+    query_keep,
+    key_keep,
+    value_keep,
+    out_keep,
+    cot_keep,
     query_all,
     key_all,
     value_all,
     out_all,
     cot_all,
-    notes,
+    mix_mine,
+    mix_other,
     sends,
     recvs,
     note_send,
     note_recv,
     twin_sems,
     local_sems,
+    keep_sems,
+    mix_sems,
 ):
     place = Place(line)
-    span, _ = halves(place, cot_ref.shape[1])
+    count = 4 * line
+    length, width = tokens_ref.shape
+    shard, q_cols = query_ref.shape
+    chunks = q_cols // 128
+    span, _ = halves(place, width)
     own = []
     blocks = ((query_ref, query_all), (key_ref, key_all), (value_ref, value_all), (out_ref, out_all))
     for i, (src, dst) in enumerate(blocks):
@@ -815,7 +889,6 @@
         c.start()
     enter(place)
     note = Notes(place, note_ref, notes, note_send, note_recv, False)
-    note.start()
     for c in own:
         c.wait()
     gathers = [
@@ -823,20 +896,117 @@
         for i, ref in enumerate((query_all, key_all, value_all, out_all))
     ]
     cot_view = lambda s: cot_all.at[s, :, span]
-    cot_gather = Gather(place, cot_view, sends.at[4], recvs.at[4])
+    cot = Gather(place, cot_view, sends.at[4], recvs.at[4])
     twin = Twin(place, cot_view, cot_view, twin_sems.at[0], twin_sems.at[1])
-    gathers.append(cot_gather)
-    gather_all(gathers, [None] * 4 + [twin.start])
-    for g in gathers[:4]:
+    out = gathers[3]
+    for g in gathers[:3]:
+        g.start()
+    note.start()
+    inputs = tokens_ref[...].astype(F32)
+    inv_attn = lax.rsqrt(jnp.mean(inputs * inputs, axis=1, keepdims=True) + EPSILON)
+    for g in gathers[:3]:
+        g.along(1)
+    note.finish()
+    gains_ref[...] = spread_gains(notes, shard, width)
+    normed_ref[...] = (inputs * inv_attn * gains_ref[1:2, :]).astype(BF16)
+    for g in gathers[:3]:
+        g.across(0)
+    for step in range(2, line + 1):
+        for g in gathers[:3]:
+            if step < line:
+                g.along(step)
+            g.across(step - 1)
+        if step == line - 1:
+            out.start()
+    for g in gathers[:3]:
         g.take_rest()
+    normed = normed_ref[...]
+    tables = [tables_ref[i] for i in range(3)]
+    query_lin = jnp.dot(normed, query_all[...].reshape(width, q_cols), preferred_element_type=F32)
+    for j in range(chunks):
+        queries_ref[:, 128 * j : 128 * (j + 1)] = rope_chunk(
+            query_lin[:, 128 * j : 128 * (j + 1)], tables, 1.0
+        ).astype(BF16)
+    out.along(1)
+    out.across(0)
+    kv_cols = key_ref.shape[1]
+    key_lin = jnp.dot(normed, key_all[...].reshape(width, kv_cols), preferred_element_type=F32)
+    for j in range(kv_cols // 128):
+        keys_ref[:, 128 * j : 128 * (j + 1)] = rope_chunk(
+            key_lin[:, 128 * j : 128 * (j + 1)], tables, 1.0
+        ).astype(BF16)
+    values_ref[...] = jnp.dot(
+        normed, value_all[...].reshape(width, kv_cols), preferred_element_type=F32
+    ).astype(BF16)
+    lane = lax.broadcasted_iota(jnp.int32, (length, 128), 1)
+    small_lane = lax.broadcasted_iota(jnp.int32, (8, 128), 1)
+    allowed = allowed_ref[...] > 0.0
+    peaks = jnp.zeros((8, 128), F32)
+    between = {
+        0: lambda: (out.along(2), out.across(1)),
+        1: lambda: out.along(3) if line > 3 else None,
+        2: lambda: (cot.start(), out.across(2)),
+        3: lambda: out.across(3) if line > 3 else None,
+    }
+    for j in range(chunks):
+        both = contract_cols(chunk_of(queries_ref, j), pair_of(keys_ref, j, group_size, lane)) * SCORE_SCALE
+        low = []
+        for half in (0, 1):
+            scores = jnp.where(allowed, both[:, length * half : length * (half + 1)], NEGATIVE)
+            row_max = jnp.max(scores, axis=1, keepdims=True)
+            peak = jnp.max(row_max, axis=0, keepdims=True)
+            peaks = jnp.where(small_lane == 2 * j + half, peak, peaks)
+            expo = jnp.exp(scores - row_max)
+            prob = expo / jnp.sum(expo, axis=1, keepdims=True)
+            probs_ref[j, :, length * half : length * (half + 1)] = prob
+            low.append(prob.astype(BF16))
+        mixed = jnp.dot(
+            jnp.concatenate(low, axis=1),
+            pair_of(values_ref, j, group_size, lane),
+            preferred_element_type=F32,
+        )
+        head_out_ref[:, 128 * j : 128 * (j + 1)] = mixed.astype(BF16)
+        if j in between:
+            between[j]()
+    peak_ref[...] = peaks
+    keeps = [
+        pltpu.make_async_copy(src, dst, keep_sems.at[i])
+        for i, (src, dst) in enumerate(
+            (
+                (query_all, query_keep),
+                (key_all, key_keep),
+                (value_all, value_keep),
+                (out_all, out_keep),
+                (cot_all, cot_keep),
+            )
+        )
+    ]
+    for c in keeps[:3]:
+        c.start()
+    out.take_rest()
+    keeps[3].start()
+    mix_mine[...] = contract_cols(head_out_ref[...], out_all[...].reshape(width, q_cols))
+    swap = remote(mix_mine, mix_other, mix_sems.at[0], mix_sems.at[1], place.twin())
+    swap.start()
+    cot.along(1, twin.start)
+    cot.across(0, twin.start)
+    swap.wait()
+    hidden = tokens_ref[...].astype(F32) + RESIDUAL * (mix_mine[...] + mix_other[...])
+    hidden_ref[...] = hidden
+    inv_moe = lax.rsqrt(jnp.mean(hidden * hidden, axis=1, keepdims=True) + EPSILON)
+    moe_in_ref[...] = (hidden * inv_moe * gains_ref[2:3, :]).astype(BF16)
+    for step in range(2, line + 1):
+        if step < line:
+            cot.along(step, twin.start)
+        cot.across(step - 1, twin.start)
 
     def rest(slot, carry):
-        cot_gather.take(slot)
+        cot.take(slot)
         twin.start(slot)
         return carry
 
-    lax.fori_loop(2 * line, 4 * line, rest, 0)
-    for g in gathers:
+    lax.fori_loop(2 * line, count, rest, 0)
+    for g in gathers + [cot]:
         g.settle()
 
     def other(slot, carry):
@@ -847,8 +1017,10 @@
 
         return carry
 
-    lax.fori_loop(0, 4 * line, other, 0)
-    note.finish()
+    lax.fori_loop(0, count, other, 0)
+    keeps[4].start()
+    for c in keeps:
+        c.wait()
 
 
 ANY = pl.BlockSpec(memory_space=pl.ANY)
@@ -861,49 +1033,46 @@
     )
 
 
-def gather_weights(line, query, key, value, out, cotangent, note):
+def run_forward(line, group_size, tokens, query, key, value, out, cotangent, note, tables, allowed):
     count = 4 * line
-    shapes = [query.shape, key.shape, value.shape, out.shape, cotangent.shape]
+    length, width = tokens.shape
+    q_cols, kv_cols = query.shape[1], key.shape[1]
+    blocks = [x.shape for x in (query, key, value, out, cotangent)]
+    shape = jax.ShapeDtypeStruct
+    outs = [
+        shape((length, width), BF16),
+        shape((length, width), F32),
+        shape((length, width), BF16),
+        shape((length, q_cols), BF16),
+        shape((length, q_cols), BF16),
+        shape((length, kv_cols), BF16),
+        shape((length, kv_cols), BF16),
+        shape((q_cols // 128, length, 2 * length), F32),
+        shape((8, 128), F32),
+        shape((8, width), F32),
+        shape(note.shape, F32),
+    ]
     return pl.pallas_call(
-        functools.partial(weights_kernel, line),
-        out_shape=[jax.ShapeDtypeStruct((count, *s), BF16) for s in shapes]
-        + [jax.ShapeDtypeStruct(note.shape, F32)],
-        in_specs=[ANY] * 5 + [IN_VMEM],
-        out_specs=[ANY] * 5 + [IN_VMEM],
-        scratch_shapes=[
+        functools.partial(forward_kernel, line, group_size),
+        out_shape=outs + [shape((count, *s), BF16) for s in blocks],
+        in_specs=[IN_VMEM] + [ANY] * 5 + [IN_VMEM] * 3,
+        out_specs=[IN_VMEM] * len(outs) + [ANY] * 5,
+        scratch_shapes=[pltpu.VMEM((count, *s), BF16) for s in blocks]
+        + [
+            pltpu.VMEM((length, width), F32),
+            pltpu.VMEM((length, width), F32),
             pltpu.SemaphoreType.DMA((5, 5 * line)),
             pltpu.SemaphoreType.DMA((5, count)),
             pltpu.SemaphoreType.DMA((count,)),
             pltpu.SemaphoreType.DMA((count,)),
             pltpu.SemaphoreType.DMA((2, count)),
             pltpu.SemaphoreType.DMA((5,)),
+            pltpu.SemaphoreType.DMA((5,)),
+            pltpu.SemaphoreType.DMA((2,)),
         ],
         compiler_params=params(0),
-        name="gather_weights",
-    )(query, key, value, out, cotangent, note)
-
-
-def swap_kernel(line, mine_ref, sum_ref, other, sems):
-    place = Place(line)
-    barrier = pltpu.get_barrier_semaphore()
-    pl.semaphore_signal(barrier, inc=1, device_id=place.twin(), device_id_type=MESH_IDS)
-    pl.semaphore_wait(barrier, 1)
-    copy = remote(mine_ref, other, sems.at[0], sems.at[1], place.twin())
-    copy.start()
-    copy.wait()
-    sum_ref[...] = mine_ref[...].astype(F32) + other[...].astype(F32)
-
-
-def twin_sum(line, number, mine):
-    return pl.pallas_call(
-        functools.partial(swap_kernel, line),
-        out_shape=jax.ShapeDtypeStruct(mine.shape, F32),
-        in_specs=[IN_VMEM],
-        out_specs=IN_VMEM,
-        scratch_shapes=[pltpu.VMEM(mine.shape, mine.dtype), pltpu.SemaphoreType.DMA((2,))],
-        compiler_params=params(number),
-        name="twin_sum",
-    )(mine)
+        name="run_forward",
+    )(tokens, query, key, value, out, cotangent, note, tables, allowed)
 
 
 def experts_kernel(
@@ -1125,100 +1294,327 @@
     )(rows, cots, notes, gate, up, down)
 
 
-def grads_kernel(
+def backward_kernel(
     line,
-    query_ref,
-    key_ref,
-    value_ref,
-    out_ref,
+    group_size,
+    tokens_ref,
+    hidden_ref,
+    d_rows_ref,
+    cot_ref,
+    normed_ref,
+    head_out_ref,
+    queries_ref,
+    keys_ref,
+    values_ref,
+    probs_ref,
+    gains_ref,
+    peak_ref,
+    tables_ref,
+    query_keep,
+    key_keep,
+    value_keep,
+    out_keep,
     mix_ref,
-    peak_ref,
-    gain_ref,
+    input_grad_ref,
+    output_ref,
     query_sum,
     key_sum,
     value_sum,
     out_sum,
-    mix_sum,
-    peaks,
-    gains,
+    notes,
     *scratch,
 ):
     place = Place(line)
     count = 4 * line
-    work, rest = scratch[:5], scratch[5:30]
-    total, last_sems, note_sends, note_recvs, local_sems = scratch[30:]
-    reduces = [Reduce(place, work[i], *rest[5 * i : 5 * i + 5]) for i in range(5)]
-
-    def loads(i, slot):
-        source = mix_ref.at[slot] if i == 4 else (query_ref, key_ref, value_ref, out_ref)[i].at[part_of(place, slot)]
-        return pltpu.make_async_copy(source, work[i].at[slot], local_sems.at[i, slot])
+    length, width = tokens_ref.shape
+    q_cols, kv_cols = queries_ref.shape[1], keys_ref.shape[1]
+    shard = width // count
+    chunks = q_cols // 128
+    (query_all, key_all, value_all, out_all), work = scratch[:4], scratch[4:9]
+    rest = scratch[9:34]
+    (
+        total,
+        d_heads,
+        d_query,
+        d_key,
+        d_value,
+        part_mine,
+        part_other,
+        d_hidden_keep,
+        mix_total,
+        note,
+        weight_sems,
+        load_sems,
+        last_sems,
+        part_sems,
+        note_sends,
+        note_recvs,
+    ) = scratch[34:]
+    by_part = lambda slot: part_of(place, slot)
+    reduces = [
+        Reduce(place, work[i], *rest[5 * i : 5 * i + 5], *(() if i == 4 else (by_part,))) for i in range(5)
+    ]
+
+    def load(slot):
+        return pltpu.make_async_copy(mix_ref.at[slot], work[4].at[slot], load_sems.at[slot])
 
     def begin(slot, carry):
-        for i in range(5):
-            loads(i, slot).start()
+        load(slot).start()
         return carry
 
+    def loaded(slot, carry):
+        load(slot).wait()
+        return carry
+
     lax.fori_loop(0, count, begin, 0)
+    weights = [
+        pltpu.make_async_copy(src, dst, weight_sems.at[i])
+        for i, (src, dst) in enumerate(
+            ((out_keep, out_all), (query_keep, query_all), (key_keep, key_all), (value_keep, value_all))
+        )
+    ]
+    for c in weights:
+        c.start()
     enter(place)
-    notes = [
-        Notes(place, peak_ref, peaks, note_sends.at[0], note_recvs.at[0], True),
-        Notes(place, gain_ref, gains, note_sends.at[1], note_recvs.at[1], False),
-    ]
-    for n in notes:
-        n.start()
-
-    def loaded(slot, carry):
-        for i in range(5):
-            loads(i, slot).wait()
-        return carry
-
     lax.fori_loop(0, count, loaded, 0)
-    mine, _ = halves(place, mix_sum.shape[1])
+    mine, theirs = halves(place, width)
     outs = (query_sum, key_sum, value_sum, out_sum, total)
     order = (4, 3, 0, 1, 2)
-    last = remote(total, mix_sum.at[:, mine], last_sems.at[0], last_sems.at[1], place.twin())
+    last = remote(total, mix_total.at[:, mine], last_sems.at[0], last_sems.at[1], place.twin())
 
     def finish(at):
         i = order[at]
         reduces[i].result(outs[i])
         if i == 4:
-            mix_sum[:, mine] = total[...]
+            mix_total[:, mine] = total[...]
             last.start()
 
-    reduce_all([reduces[i] for i in order], finish)
+    run = Reductions([reduces[i] for i in order], finish)
+    run.start()
+    hidden = hidden_ref[...]
+    inv_moe = lax.rsqrt(jnp.mean(hidden * hidden, axis=1, keepdims=True) + EPSILON)
+    unit_moe = hidden * inv_moe
+    d_rows = d_rows_ref[...]
+    scaled = d_rows * gains_ref[2:3, :]
+    d_hidden = cot_ref[...].astype(F32) + inv_moe * (
+        scaled - unit_moe * jnp.mean(scaled * unit_moe, axis=1, keepdims=True)
+    )
+    d_hidden_keep[...] = d_hidden
+    moe_gain = jnp.sum(d_rows * unit_moe, axis=0, keepdims=True)
+    d_attn = (RESIDUAL * d_hidden).astype(BF16)
+    run.run(2)
+    work[3][...] = contract_rows(d_attn, head_out_ref[...]).astype(BF16).reshape(count, shard, q_cols)
+    run.run(2)
+    weights[0].wait()
+    d_heads[...] = jnp.dot(
+        d_attn, out_all[...].reshape(width, q_cols), preferred_element_type=F32
+    ).astype(BF16)
+    run.run(1)
+    lane = lax.broadcasted_iota(jnp.int32, (length, 128), 1)
+    d_key[...] = jnp.zeros_like(d_key)
+    d_value[...] = jnp.zeros_like(d_value)
+    tables = [tables_ref[i] for i in range(3)]
+    for j in range(chunks):
+        d_out = chunk_of(d_heads, j)
+        keys = pair_of(keys_ref, j, group_size, lane)
+        d_prob = contract_cols(d_out, pair_of(values_ref, j, group_size, lane))
+        low, d_scores = [], []
+        for half in (0, 1):
+            side = slice(length * half, length * (half + 1))
+            prob = probs_ref[j, :, side]
+            grad = d_prob[:, side]
+            inner = jnp.sum(prob * grad, axis=1, keepdims=True)
+            d_scores.append((prob * (grad - inner)).astype(BF16))
+            low.append(prob.astype(BF16))
+        d_scores = jnp.concatenate(d_scores, axis=1)
+        d_values = contract_rows(jnp.concatenate(low, axis=1), d_out)
+        d_keys = contract_rows(d_scores, chunk_of(queries_ref, j)) * SCORE_SCALE
+        turned = rope_chunk(
+            jnp.dot(d_scores, keys, preferred_element_type=F32) * SCORE_SCALE, tables, -1.0
+        )
+        d_query[:, 128 * j : 128 * (j + 1)] = turned.astype(BF16)
+        for half in (0, 1):
+            group = (2 * j + half) // group_size
+            side = slice(length * half, length * (half + 1))
+            cols = slice(128 * (group // 2), 128 * (group // 2 + 1))
+            d_key[:, cols] += place_half(d_keys[side], half, group % 2, lane)
+            d_value[:, cols] += place_half(d_values[side], half, group % 2, lane)
+        run.run(1)
+    normed = normed_ref[...]
+    work[0][...] = contract_rows(normed, d_query[...]).astype(BF16).reshape(count, shard, q_cols)
+    d_key_lin = jnp.concatenate(
+        [rope_chunk(chunk_of(d_key, j), tables, -1.0) for j in range(kv_cols // 128)], axis=1
+    ).astype(BF16)
+    d_value_lin = d_value[...].astype(BF16)
+    run.run(2)
+    work[1][...] = contract_rows(normed, d_key_lin).astype(BF16).reshape(count, shard, kv_cols)
+    work[2][...] = contract_rows(normed, d_value_lin).astype(BF16).reshape(count, shard, kv_cols)
+    run.run(2)
+    for c in weights[1:]:
+        c.wait()
+    part_mine[...] = (
+        contract_cols(d_query[...], query_all[...].reshape(width, q_cols))
+        + contract_cols(d_key_lin, key_all[...].reshape(width, kv_cols))
+        + contract_cols(d_value_lin, value_all[...].reshape(width, kv_cols))
+    )
+    swap = remote(part_mine, part_other, part_sems.at[0], part_sems.at[1], place.twin())
+    swap.start()
+    run.run(2)
+    swap.wait()
+    d_normed = part_mine[...] + part_other[...]
+    inputs = tokens_ref[...].astype(F32)
+    inv_attn = lax.rsqrt(jnp.mean(inputs * inputs, axis=1, keepdims=True) + EPSILON)
+    unit_attn = inputs * inv_attn
+    scaled = d_normed * gains_ref[1:2, :]
+    input_grad_ref[...] = d_hidden_keep[...] + inv_attn * (
+        scaled - unit_attn * jnp.mean(scaled * unit_attn, axis=1, keepdims=True)
+    )
+    attn_gain = jnp.sum(d_normed * unit_attn, axis=0, keepdims=True)
+    rows = jnp.concatenate([attn_gain, moe_gain, jnp.zeros((6, width), F32)], axis=0)
+    row = lax.broadcasted_iota(jnp.int32, (8, 128), 0)
+    peaks = jnp.broadcast_to(peak_ref[0:1, :], (8, 128))
+    for p in range(count):
+        turned = pltpu.roll(rows, width - shard * p, 1) if p else rows
+        note[p] = jnp.where(row == 2, peaks, turned[:, :128])
+    exchange = Notes(place, note, notes, note_sends, note_recvs, False)
+    exchange.start()
+    run.complete()
     for r in reduces:
         r.settle()
-    for n in notes:
-        n.finish()
     last.wait()
-
-
-def reduce_grads(line, grads, mix, peak, gain):
+    output_ref[...] = (hidden_ref[...] + RESIDUAL * mix_total[...]).astype(BF16)
+    exchange.finish()
+
+
+def run_backward(line, group_size, kept, keeps, mix):
     count = 4 * line
-    blocks = [g.shape[1:] for g in grads] + [mix.shape[1:]]
-    rows, half = blocks[4]
+    tokens, queries, keys = kept[0], kept[6], kept[7]
+    length, width = tokens.shape
+    q_cols, kv_cols = queries.shape[1], keys.shape[1]
+    blocks = [x.shape[1:] for x in keeps] + [mix.shape[1:]]
+    half = width // 2
+    shape = jax.ShapeDtypeStruct
+    outs = (
+        [shape((length, width), F32), shape((length, width), BF16)]
+        + [shape(s, F32) for s in blocks[:4]]
+        + [shape((count, 8, 128), F32)]
+    )
     return pl.pallas_call(
-        functools.partial(grads_kernel, line),
-        out_shape=[jax.ShapeDtypeStruct(s, F32) for s in blocks[:4]]
-        + [
-            jax.ShapeDtypeStruct((rows, 2 * half), F32),
-            jax.ShapeDtypeStruct((count, *peak.shape), F32),
-            jax.ShapeDtypeStruct(gain.shape, F32),
-        ],
-        in_specs=[ANY] * 5 + [IN_VMEM] * 2,
-        out_specs=[IN_VMEM] * 7,
-        scratch_shapes=[pltpu.VMEM((count, *s), BF16) for s in blocks]
+        functools.partial(backward_kernel, line, group_size),
+        out_shape=outs,
+        in_specs=[IN_VMEM] * len(kept) + [ANY] * 5,
+        out_specs=[IN_VMEM] * len(outs),
+        scratch_shapes=[pltpu.VMEM(x.shape, BF16) for x in keeps]
+        + [pltpu.VMEM((count, *s), BF16) for s in blocks]
         + [x for s in blocks for x in reduce_scratch(line, s)]
         + [
-            pltpu.VMEM((rows, half), F32),
+            pltpu.VMEM((length, half), F32),
+            pltpu.VMEM((length, q_cols), BF16),
+            pltpu.VMEM((length, q_cols), BF16),
+            pltpu.VMEM((length, kv_cols), F32),
+            pltpu.VMEM((length, kv_cols), F32),
+            pltpu.VMEM((length, width), F32),
+            pltpu.VMEM((length, width), F32),
+            pltpu.VMEM((length, width), F32),
+            pltpu.VMEM((length, width), F32),
+            pltpu.VMEM((count, 8, 128), F32),
+            pltpu.SemaphoreType.DMA((4,)),
+            pltpu.SemaphoreType.DMA((count,)),
             pltpu.SemaphoreType.DMA((2,)),
-            pltpu.SemaphoreType.DMA((2, count)),
-            pltpu.SemaphoreType.DMA((2, count)),
-            pltpu.SemaphoreType.DMA((5, count)),
+            pltpu.SemaphoreType.DMA((2,)),
+            pltpu.SemaphoreType.DMA((count,)),
+            pltpu.SemaphoreType.DMA((count,)),
         ],
         compiler_params=params(3),
-        name="reduce_grads",
-    )(*grads, mix, peak, gain)
+        name="run_backward",
+    )(*kept, *keeps, mix)
+
+
+def finish_kernel(
+    group_size,
+    output_in,
+    input_grad_in,
+    query_in,
+    key_in,
+    value_in,
+    out_in,
+    notes,
+    query_ref,
+    key_ref,
+    gate_in,
+    up_in,
+    down_in,
+    output,
+    input_grad,
+    grad_query,
+    grad_key,
+    grad_value,
+    grad_out,
+    gains,
+    clipped_query,
+    clipped_key,
+    grad_gate,
+    grad_up,
+    grad_down,
+    sems,
+):
+    pairs = ((gate_in, grad_gate), (up_in, grad_up), (down_in, grad_down))
+    copies = [pltpu.make_async_copy(src, dst.at[0], sems.at[i]) for i, (src, dst) in enumerate(pairs)]
+    for c in copies:
+        c.start()
+    output[...] = output_in[...]
+    input_grad[...] = input_grad_in[...]
+    grad_query[...] = query_in[...]
+    grad_key[...] = key_in[...]
+    grad_value[...] = value_in[...]
+    grad_out[...] = out_in[...]
+    total, peaks = notes[0], notes[0]
+    for p in range(1, notes.shape[0]):
+        total = total + notes[p]
+        peaks = jnp.maximum(peaks, notes[p])
+    gains[...] = total
+    factor = CLIP_LIMIT / jnp.maximum(peaks, CLIP_LIMIT)
+    root = jnp.sqrt(factor)
+    lane = lax.broadcasted_iota(jnp.int32, (8, 128), 1)
+
+    def scale(h):
+        return jnp.max(jnp.where(lane == h, root, 0.0), axis=1, keepdims=True)[2:3, :]
+
+    heads = query_ref.shape[1] // HEAD_SIZE
+    wide = lax.broadcasted_iota(jnp.int32, (1, 128), 1)
+    scales = [scale(h) for h in range(heads)]
+    for j in range(heads // 2):
+        row = jnp.where(wide < HEAD_SIZE, scales[2 * j], scales[2 * j + 1])
+        cols = slice(128 * j, 128 * (j + 1))
+        clipped_query[:, cols] = query_ref[:, cols].astype(F32) * row
+    least = [
+        functools.reduce(jnp.minimum, scales[group_size * g : group_size * (g + 1)])
+        for g in range(heads // group_size)
+    ]
+    for j in range(len(least) // 2):
+        row = jnp.where(wide < HEAD_SIZE, least[2 * j], least[2 * j + 1])
+        cols = slice(128 * j, 128 * (j + 1))
+        clipped_key[:, cols] = key_ref[:, cols].astype(F32) * row
+    for c in copies:
+        c.wait()
+
+
+def finish(group_size, found, notes, query, key, expert_grads):
+    shape = jax.ShapeDtypeStruct
+    outs = [shape(x.shape, x.dtype) for x in found] + [
+        shape((8, 128), F32),
+        shape(query.shape, F32),
+        shape(key.shape, F32),
+    ]
+    return pl.pallas_call(
+        functools.partial(finish_kernel, group_size),
+        out_shape=outs + [shape((1, *g.shape), F32) for g in expert_grads],
+        in_specs=[IN_VMEM] * 9 + [ANY] * 3,
+        out_specs=[IN_VMEM] * 9 + [ANY] * 3,
+        scratch_shapes=[pltpu.SemaphoreType.DMA((3,))],
+        compiler_params=pltpu.CompilerParams(vmem_limit_bytes=56 * 2**20),
+        name="finish",
+    )(*found, notes, query, key, *expert_grads)
 
 
 def note_tiles(*rows):
@@ -1258,138 +1654,44 @@
     named = expert_ids[None, :, :] == expert_index[:, None, None]
     gate_rows = jnp.sum(jnp.where(named, gate_probs[None], 0.0), axis=2)
     own_gains = [jnp.broadcast_to(g[None], (count, shard)) for g in (attn_norm_gain, moe_norm_gain)]
-    query_all, key_all, value_all, out_all, cot_all, notes = gather_weights(
+    note = note_tiles(gate_rows, *own_gains)
+    position, allowed = tree_layout(segment_ids[0], parents[0])
+    cosine, sine = (jnp.tile(t[:, 0, :], (1, 4)) for t in rope_tables(position, HEAD_SIZE))
+    first = (jnp.arange(128) % HEAD_SIZE < HEAD_SIZE // 2)[None, :]
+    tables = jnp.stack([cosine, jnp.where(first, -sine, 0.0), jnp.where(first, 0.0, sine)])
+    (moe_in, hidden, normed, head_out, queries, keys, values, probs, peak, gains, notes, *keeps, cots) = run_forward(
         line,
+        group_size,
+        tokens,
         w_query,
         key_projection,
         value_projection,
         w_out,
         cotangent,
-        note_tiles(gate_rows, *own_gains),
-    )
-    query_w = query_all.reshape(model_width, q_cols)
-    key_weight = key_all.reshape(model_width, kv_cols)
-    value_weight = value_all.reshape(model_width, kv_cols)
-    out_w = out_all.reshape(model_width, q_cols)
-    attn_gain_f = notes[:, 1, :shard].reshape(model_width)
-    moe_gain_f = notes[:, 2, :shard].reshape(model_width)
-    inputs = tokens.astype(F32)
-    inv_attn = lax.rsqrt(jnp.mean(inputs * inputs, axis=1, keepdims=True) + EPSILON)
-    unit_attn = inputs * inv_attn
-    normalized_rows = (unit_attn * attn_gain_f).astype(BF16)
-    position, allowed = tree_layout(segment_ids[0], parents[0])
-    cosine_table, sine_values = rope_tables(position, HEAD_SIZE)
-    query_linear = jnp.dot(normalized_rows, query_w, preferred_element_type=F32).reshape(
-        length, q_heads, HEAD_SIZE
-    )
-    key_linear = jnp.dot(normalized_rows, key_weight, preferred_element_type=F32).reshape(
-        length, kv_heads, HEAD_SIZE
-    )
-    query_heads = (
-        apply_rotary(query_linear, cosine_table, sine_values)
-        .astype(BF16)
-        .reshape(length, kv_heads, group_size, HEAD_SIZE)
-    )
-    key_heads = apply_rotary(key_linear, cosine_table, sine_values).astype(BF16)
-    value_heads = (
-        jnp.dot(normalized_rows, value_weight, preferred_element_type=F32)
-        .astype(BF16)
-        .reshape(length, kv_heads, HEAD_SIZE)
-    )
-    scores = (
-        jnp.einsum("qhgd,khd->hgqk", query_heads, key_heads, preferred_element_type=F32)
-        * SCORE_SCALE
-    )
-    scores = jnp.where(allowed[None, None], scores, NEGATIVE)
-    own_peak = jnp.max(scores, axis=(2, 3)).reshape(1, q_heads)
-    row_max = jnp.max(scores, axis=3, keepdims=True)
-    expo = jnp.exp(scores - row_max)
-    prob_full = expo / jnp.sum(expo, axis=3, keepdims=True)
-    prob_low = prob_full.astype(BF16)
-    head_out = (
-        jnp.einsum("hgqk,khd->qhgd", prob_low, value_heads, preferred_element_type=F32)
-        .reshape(length, q_cols)
-        .astype(BF16)
-    )
-    attn_mix = twin_sum(line, 4, contract_cols(head_out, out_w))
-    hidden = inputs + RESIDUAL * attn_mix
-    inv_moe = lax.rsqrt(jnp.mean(hidden * hidden, axis=1, keepdims=True) + EPSILON)
-    unit_moe = hidden * inv_moe
-    moe_in = (unit_moe * moe_gain_f).astype(BF16)
-    d_moe_in, mix_parts, grad_gate, grad_up, grad_down = run_experts(
-        line, moe_in, cot_all, notes, w_gate[0], w_up[0], w_down[0]
-    )
-    grad_output = cotangent.astype(F32)
-    scaled_moe = d_moe_in * moe_gain_f
-    grad_moe_gain = jnp.sum(d_moe_in * unit_moe, axis=0)
-    d_hidden = grad_output + inv_moe * (
-        scaled_moe - unit_moe * jnp.mean(scaled_moe * unit_moe, axis=1, keepdims=True)
-    )
-    d_attn = (RESIDUAL * d_hidden).astype(BF16)
-    grad_out_w = contract_rows(d_attn, head_out)
-    d_heads = (
-        jnp.dot(d_attn, out_w, preferred_element_type=F32)
-        .astype(BF16)
-        .reshape(length, kv_heads, group_size, HEAD_SIZE)
-    )
-    d_value = jnp.einsum("hgqk,qhgd->khd", prob_low, d_heads, preferred_element_type=F32)
-    d_prob = jnp.einsum("qhgd,khd->hgqk", d_heads, value_heads, preferred_element_type=F32)
-    inner = jnp.sum(prob_full * d_prob, axis=3, keepdims=True)
-    d_scores = (prob_full * (d_prob - inner)).astype(BF16)
-    d_query_all = (
-        jnp.einsum("hgqk,khd->qhgd", d_scores, key_heads, preferred_element_type=F32) * SCORE_SCALE
-    ).reshape(length, q_heads, HEAD_SIZE)
-    d_key = (
-        jnp.einsum("hgqk,qhgd->khd", d_scores, query_heads, preferred_element_type=F32)
-        * SCORE_SCALE
-    )
-    d_query_lin = (
-        rotate_back(d_query_all, cosine_table, sine_values).astype(BF16).reshape(length, q_cols)
-    )
-    d_key_lin = rotate_back(d_key, cosine_table, sine_values).astype(BF16).reshape(length, kv_cols)
-    d_value_lin = d_value.astype(BF16).reshape(length, kv_cols)
-    grads = [
-        contract_rows(normalized_rows, g).astype(BF16).reshape(count, shard, g.shape[1])
-        for g in (d_query_lin, d_key_lin, d_value_lin)
-    ] + [grad_out_w.astype(BF16).reshape(count, shard, q_cols)]
-    d_normed_part = (
-        contract_cols(d_query_lin, query_w)
-        + contract_cols(d_key_lin, key_weight)
-        + contract_cols(d_value_lin, value_weight)
-    )
-    d_normed = twin_sum(line, 5, d_normed_part.astype(BF16))
-    scaled_attn = d_normed * attn_gain_f
-    grad_attn_gain = jnp.sum(d_normed * unit_attn, axis=0)
-    input_grad = d_hidden + inv_attn * (
-        scaled_attn - unit_attn * jnp.mean(scaled_attn * unit_attn, axis=1, keepdims=True)
-    )
-    peak_tile = note_tiles(own_peak)[0]
-    gain_tiles = note_tiles(grad_attn_gain.reshape(count, shard), grad_moe_gain.reshape(count, shard))
-    grad_query, grad_key, grad_value, grad_out, expert_mix, peaks, gains = reduce_grads(
-        line, grads, mix_parts, peak_tile, gain_tiles
-    )
-    output = (hidden + RESIDUAL * expert_mix).astype(BF16)
-    head_peak = jnp.max(peaks[:, 0, :q_heads], axis=0)
-    gain_sums = jnp.sum(gains, axis=0)
-    scale_factor = CLIP_LIMIT / jnp.maximum(head_peak, CLIP_LIMIT)
-    query_scale = jnp.repeat(jnp.sqrt(scale_factor), HEAD_SIZE)
-    key_clip_scale = jnp.repeat(
-        jnp.sqrt(jnp.min(scale_factor.reshape(kv_heads, group_size), axis=1)), HEAD_SIZE
-    )
-    clipped_query = w_query.astype(F32) * query_scale[None, :]
-    clipped_key = key_projection.astype(F32) * key_clip_scale[None, :]
+        note,
+        tables,
+        allowed.astype(F32),
+    )
+    d_moe_in, mix_parts, *expert_grads = run_experts(
+        line, moe_in, cots, notes, w_gate[0], w_up[0], w_down[0]
+    )
+    kept = (tokens, hidden, d_moe_in, cotangent, normed, head_out, queries, keys, values, probs, gains, peak, tables)
+    input_grad, output, *grads, sums = run_backward(line, group_size, kept, keeps, mix_parts)
+    output, input_grad, gq, gk, gv, go, gains, clipped_query, clipped_key, gg, gu, gd = finish(
+        group_size, (output, input_grad, *grads), sums, w_query, key_projection, expert_grads
+    )
     return (
         output,
         input_grad,
-        gain_sums[0, :shard],
-        grad_query,
-        grad_key,
-        grad_value,
-        grad_out,
-        gain_sums[1, :shard],
-        grad_gate[None],
-        grad_up[None],
-        grad_down[None],
+        gains[0, :shard],
+        gq,
+        gk,
+        gv,
+        go,
+        gains[1, :shard],
+        gg,
+        gu,
+        gd,
         clipped_query,
         clipped_key,
     )

time: 409 us -> 480 us (1.17)
  Pallas kernels: 334 us -> 466 us
  matrix products: 24.8 us -> 1.89 us
  local copies, waits for them, and re-layouts: 21.7 us -> 2.17 us
  other arithmetic: 25.6 us -> 8.32 us
    pallas_call x4 -> x3, Pallas kernels: 233 us -> 365 us  [the longest x1 147 us: finish(): pl.pallas_call(functools.partial(finish_kernel, group_size), out_shape=ou...]
    dot_general x18 -> x0, matrix products: 22.4 us -> none  [the longest x4 7.18 us: contract_rows(): lax.dot_general(left, right, (((0,), (0,)), ((), ())), preferred_element_...]
    unnamed x83 -> x0, local copies, waits for them, and re-layouts: 12.1 us -> none
    reduce_sum x5 -> x0, other arithmetic: 5.39 us -> none  [the longest x1 1.57 us: on_device_dense(): grad_moe_gain = jnp.sum(d_moe_in * unit_moe, axis=0)]
where the time goes in v4:
time: 480 us; the launch traced here: 479 us
  Pallas kernels  466 us (97%)
  other arithmetic  8.32 us (2%)
    pallas_call x1, Pallas kernels, finish(): pl.pallas_call(functools.partial(finish_kernel, group_size), out_shape=ou...  147 us
    pallas_call x1, Pallas kernels, run_forward(): pl.pallas_call(functools.partial(forward_kernel, line, group_size), out_s...  111 us
    pallas_call x1, Pallas kernels, run_backward(): pl.pallas_call(functools.partial(backward_kernel, line, group_size), out_...  107 us
    pallas_call x1, Pallas kernels, run_experts(): pl.pallas_call(functools.partial(experts_kernel, line), out_shape=[jax.Sh...  101 us

profile of v4, /device:TPU:0, one launch (start us, length us, event | category | flops | bytes accessed | tf_op | source)
XLA Modules:
  0.0 478.9 jit_solution(13052590595883839985)
XLA Ops:
  0.6 0.8 convert_reduce_fusion
  1.4 0.7 reduce_max.9
  2.1 0.7 fusion.25
  2.8 0.7 pad_convert_fusion.1
  3.5 0.7 pad_convert_fusion
  4.2 0.9 select_reduce_fusion.6
  5.1 0.2 select_reduce_fusion.2
  5.3 0.7 fusion.28
  6.0 0.7 select_reduce_fusion.5
  6.7 0.7 fusion.24
  7.4 0.7 select_reduce_fusion
  8.2 0.1 multiply_cosine_fusion
  8.3 0.7 stack.24.note_ref
  9.0 0.1 copy.37
  9.1 1.9 fusion.1.allowed_ref
  11.0 0.1 copy.35
  11.1 0.7 pad_maximum_fusion.tables_ref
  11.8 110.6 %run_forward.1 = (bf16[128,1536]{1,0:T(8,128)(2,1)}, f32[128,1536]{1,0:T(8,128)}, bf16[128,1536]{1,0:T(8,128)(2,1)}, bf16[128,768]{1,0:T(8,128)(2,1)}, bf16[128,...) custom-call(bf16[128,1536]{1,0:T(8,128)(2,1)} %tokens_ref.3, ...), custom_call_target="tpu_custom_call" | custom-call | tf_op jit(solution)/shard_map/run_forward/pallas_call | solution.py:1055
  122.5 101.1 %run_experts.1 = (f32[128,1536]{1,0:T(8,128)}, bf16[16,128,768]{2,1,0:T(8,128)(2,1)}, f32[1536,256]{1,0:T(8,128)}, f32[1536,256]{1,0:T(8,128)}, f32[1536,256]{1,0:T(8,128)}) custom-call(bf16[128,1536]{1,0:T(8,128)(2,1)} %get-tuple-element.54.rows_ref, bf16[16,128,1536]{2,1,0:T(8,128)(2,1)} %get-tuple-element.55.cot_ref, ...), custom_call_target="tpu_custom_call" | custom-call | tf_op jit(solution)/shard_map/run_experts/pallas_call | solution.py:1259
  223.6 107.0 %run_backward.1 = (f32[128,1536]{1,0:T(8,128)}, bf16[128,1536]{1,0:T(8,128)(2,1)}, f32[96,768]{1,0:T(8,128)}, f32[96,256]{1,0:T(8,128)}, f32[96,256]{1,0:T(8,128...) custom-call(bf16[128,1536]{1,0:T(8,128)(2,1)} %tokens_ref.3, f32[128,1536]{1,0:T(8,128)} %get-tuple-element.53.hidden_ref, ...), custom_call_target="tpu_custom_call" | custom-call | tf_op jit(solution)/shard_map/run_backward/pallas_call | solution.py:1502
  330.6 147.0 %finish.1 = (bf16[128,1536]{1,0:T(8,128)(2,1)}, f32[128,1536]{1,0:T(8,128)}, f32[96,768]{1,0:T(8,128)}, f32[96,256]{1,0:T(8,128)}, f32[96,256]{1,0:T(8,128)}, /*...) custom-call(bf16[128,1536]{1,0:T(8,128)(2,1)} %get-tuple-element.71., ...), custom_call_target="tpu_custom_call" | custom-call | tf_op jit(solution)/shard_map/finish/pallas_call | solution.py:1609
  477.6 1.3 slice_bitcast_fusion
  (10 shorter events, 0.1 us)

commit v5 on v4

--- a/solution.py
+++ b/solution.py
@@ -830,6 +830,63 @@
     return total
 
 
+def gate_table(logits, ids):
+    expo = jnp.exp(logits - jnp.max(logits, axis=1, keepdims=True))
+    probs = expo / jnp.sum(expo, axis=1, keepdims=True)
+    length, top = logits.shape
+    expert = lax.broadcasted_iota(jnp.int32, (length, 128), 1)
+    table = jnp.zeros((length, 128), F32)
+    for c in range(top):
+        table += jnp.where(ids[:, c : c + 1] == expert, probs[:, c : c + 1], 0.0)
+    return jnp.transpose(table)
+
+
+def write_notes(note_ref, gates, gains):
+    shard = gains[0].shape[1]
+    row = lax.broadcasted_iota(jnp.int32, (8, 128), 0)
+    pad = jnp.zeros((1, 128 - shard), F32)
+    below = jnp.zeros((8, 128), F32)
+    for i, gain in enumerate(gains):
+        below = jnp.where(row == i + 1, jnp.concatenate([gain, pad], axis=1), below)
+    for p in range(note_ref.shape[0]):
+        note_ref[p] = jnp.where(row == 0, gates[p : p + 1, :], below)
+
+
+def tree_tables(segments, parents, length):
+    row = lax.broadcasted_iota(jnp.int32, (length, length), 0)
+    lane = lax.broadcasted_iota(jnp.int32, (length, length), 1)
+
+    def total(x):
+        return jnp.sum(x.astype(F32), axis=1, keepdims=True)
+
+    own_row = segments.astype(F32)
+    own = total(jnp.where(row == lane, own_row, 0.0))
+    kinds = parents.shape[1]
+    kind = lax.broadcasted_iota(jnp.int32, (length, kinds), 1).astype(F32)
+    above = parents.astype(F32)
+    parent = total(jnp.where(kind == own, above, 0.0))
+    grand = total(jnp.where(kind == parent, above, 0.0))
+    in_parent, in_grand = own_row == parent, own_row == grand
+    start = total(jnp.where(own_row < own, 1.0, 0.0))
+    offset = jnp.where(own != 0.0, total(jnp.where(in_parent, 1.0, 0.0)), 0.0)
+    offset += jnp.where(parent != 0.0, total(jnp.where(in_grand, 1.0, 0.0)), 0.0)
+    place = lax.broadcasted_iota(jnp.int32, (length, 1), 0).astype(F32)
+    linked = jnp.logical_or(own_row == own, jnp.logical_or(in_parent, in_grand))
+    return place - start + offset, jnp.logical_and(linked, lane <= row)
+
+
+def write_tables(tables_ref, position):
+    lane = lax.broadcasted_iota(jnp.int32, (1, 128), 1)
+    half = HEAD_SIZE // 2
+    frequency = THETA ** ((lane % half).astype(F32) * (-2.0 / HEAD_SIZE))
+    angles = position * frequency
+    sine = jnp.sin(angles)
+    first = lane % HEAD_SIZE < half
+    tables_ref[0] = jnp.cos(angles)
+    tables_ref[1] = jnp.where(first, -sine, 0.0)
+    tables_ref[2] = jnp.where(first, 0.0, sine)
+
+
 def forward_kernel(
     line,
     group_size,
@@ -839,9 +896,12 @@
     value_ref,
     out_ref,
     cot_ref,
-    note_ref,
-    tables_ref,
-    allowed_ref,
+    gain_a_ref,
+    gain_m_ref,
+    logits_ref,
+    ids_ref,
+    segments_ref,
+    parents_ref,
     moe_in_ref,
     hidden_ref,
     normed_ref,
@@ -851,6 +911,7 @@
     values_ref,
     probs_ref,
     peak_ref,
+    tables_ref,
     gains_ref,
     notes,
     query_keep,
@@ -865,6 +926,7 @@
     cot_all,
     mix_mine,
     mix_other,
+    note_ref,
     sends,
     recvs,
     note_send,
@@ -901,6 +963,8 @@
     out = gathers[3]
     for g in gathers[:3]:
         g.start()
+    gains = [g[...].astype(F32) for g in (gain_a_ref, gain_m_ref)]
+    write_notes(note_ref, gate_table(logits_ref[...], ids_ref[...]), gains)
     note.start()
     inputs = tokens_ref[...].astype(F32)
     inv_attn = lax.rsqrt(jnp.mean(inputs * inputs, axis=1, keepdims=True) + EPSILON)
@@ -911,6 +975,8 @@
     normed_ref[...] = (inputs * inv_attn * gains_ref[1:2, :]).astype(BF16)
     for g in gathers[:3]:
         g.across(0)
+    position, allowed = tree_tables(segments_ref[...], parents_ref[...], length)
+    write_tables(tables_ref, position)
     for step in range(2, line + 1):
         for g in gathers[:3]:
             if step < line:
@@ -940,7 +1006,6 @@
     ).astype(BF16)
     lane = lax.broadcasted_iota(jnp.int32, (length, 128), 1)
     small_lane = lax.broadcasted_iota(jnp.int32, (8, 128), 1)
-    allowed = allowed_ref[...] > 0.0
     peaks = jnp.zeros((8, 128), F32)
     between = {
         0: lambda: (out.along(2), out.across(1)),
@@ -1033,7 +1098,7 @@
     )
 
 
-def run_forward(line, group_size, tokens, query, key, value, out, cotangent, note, tables, allowed):
+def run_forward(line, group_size, tokens, query, key, value, out, cotangent, *small):
     count = 4 * line
     length, width = tokens.shape
     q_cols, kv_cols = query.shape[1], key.shape[1]
@@ -1049,18 +1114,20 @@
         shape((length, kv_cols), BF16),
         shape((q_cols // 128, length, 2 * length), F32),
         shape((8, 128), F32),
+        shape((3, length, 128), F32),
         shape((8, width), F32),
-        shape(note.shape, F32),
+        shape((count, 8, 128), F32),
     ]
     return pl.pallas_call(
         functools.partial(forward_kernel, line, group_size),
         out_shape=outs + [shape((count, *s), BF16) for s in blocks],
-        in_specs=[IN_VMEM] + [ANY] * 5 + [IN_VMEM] * 3,
+        in_specs=[IN_VMEM] + [ANY] * 5 + [IN_VMEM] * len(small),
         out_specs=[IN_VMEM] * len(outs) + [ANY] * 5,
         scratch_shapes=[pltpu.VMEM((count, *s), BF16) for s in blocks]
         + [
             pltpu.VMEM((length, width), F32),
             pltpu.VMEM((length, width), F32),
+            pltpu.VMEM((count, 8, 128), F32),
             pltpu.SemaphoreType.DMA((5, 5 * line)),
             pltpu.SemaphoreType.DMA((5, count)),
             pltpu.SemaphoreType.DMA((count,)),
@@ -1072,7 +1139,7 @@
         ],
         compiler_params=params(0),
         name="run_forward",
-    )(tokens, query, key, value, out, cotangent, note, tables, allowed)
+    )(tokens, query, key, value, out, cotangent, *small)
 
 
 def experts_kernel(
@@ -1093,6 +1160,7 @@
     active,
     d_gate,
     d_up,
+    d_active,
     grad_stage,
     mix_stage,
     grad_parts,
@@ -1137,7 +1205,6 @@
         place, lambda s: mix_stage.at[s, :, theirs], lambda s: mix_parts.at[s], twin_sems.at[4], twin_sems.at[5]
     )
     reduce = Reduce(place, grad_parts, from_b, from_a, from_z, reduce_send, reduce_recv)
-    gather_all([gather], [row_twin.start])
 
     def fold(slot):
         grad_twin.take(slot)
@@ -1146,6 +1213,21 @@
 
     def column(slot):
         return jnp.transpose(notes_ref[part_of(place, slot)])[:, 0:1]
+
+    def tile_of(tile):
+        first = 2 * tile
+        pair = (first, first + 1)
+        gate = jnp.concatenate([column(slot) for slot in pair], axis=0)
+        return pair, pl.ds(first, 2), pl.ds(pl.multiple_of(first * length, 2 * length), 2 * length), gate
+
+    def ahead(tile, carry):
+        pair, two, flat, gate = tile_of(tile)
+        for slot in pair:
+            load(slot).wait()
+        d_out = (gate * (RESIDUAL * cots[two].reshape(2 * length, width).astype(F32))).astype(BF16)
+        cots[two] = d_out.reshape(2, length, width)
+        d_active[flat, :] = jnp.dot(d_out, down_ref[...], preferred_element_type=F32)
+        return carry
 
     def step(tile, carry):
         first = 2 * tile
@@ -1154,20 +1236,13 @@
         flat = pl.ds(pl.multiple_of(first * length, 2 * length), 2 * length)
         for slot in pair:
             pl.when(slot != place.z)(lambda slot=slot: row_twin.take(slot))
-            load(slot).wait()
         x = rows[two].reshape(2 * length, width)
-        gate = jnp.concatenate([column(slot) for slot in pair], axis=0)
         gate_pre = jnp.dot(x, gate_ref[...], preferred_element_type=F32)
         up_pre = jnp.dot(x, up_ref[...], preferred_element_type=F32)
         sigmoid = 1.0 / (1.0 + jnp.exp(-gate_pre))
         silu = gate_pre * sigmoid
-        act = (silu * up_pre).astype(BF16)
-        active[flat, :] = act
-        mix = contract_cols(act, down_ref[...])
-        mix_stage[two] = (gate * mix).astype(BF16).reshape(2, length, width)
-        d_out = (gate * (RESIDUAL * cots[two].reshape(2 * length, width).astype(F32))).astype(BF16)
-        cots[two] = d_out.reshape(2, length, width)
-        d_act = jnp.dot(d_out, down_ref[...], preferred_element_type=F32)
+        active[flat, :] = (silu * up_pre).astype(BF16)
+        d_act = d_active[flat, :]
         d_g = (d_act * up_pre * sigmoid * (1.0 + gate_pre * (1.0 - sigmoid))).astype(BF16)
         d_u = (d_act * silu).astype(BF16)
         d_gate[flat, :] = d_g
@@ -1176,8 +1251,6 @@
         grad_stage[two] = d_in.astype(BF16).reshape(2, length, width)
         for slot in pair:
             grad_twin.start(slot)
-            mix_twin.start(slot)
-
         group = (tile + 1) // (line // 2)
 
         @pl.when(jnp.logical_or(group == 1, group == 3))
@@ -1194,6 +1267,15 @@
 
         return carry
 
+    gather.start()
+    share = 2 * line // 4
+    for at in range(4):
+        lax.fori_loop(at * share, (at + 1) * share, ahead, 0)
+        steps = range(1, line + 1)[at * line // 4 : (at + 1) * line // 4]
+        for k in steps:
+            if k < line:
+                gather.along(k, row_twin.start)
+            gather.across(k - 1, row_twin.start)
     lax.fori_loop(0, 2 * line, step, 0)
     for slot in (count - 2, count - 1):
         fold(slot)
@@ -1204,25 +1286,50 @@
 
     lax.fori_loop(line, 2 * line, fold_late, 0)
 
-    def weight_grad(number, left, right, out_ref):
-        left = left.reshape(count * length, left.shape[2]) if len(left.shape) == 3 else left
-
-        def some(i, carry):
-            span = pl.ds(pl.multiple_of(i * 512, 512), 512)
-            grads[number, span, :] = contract_rows(left[:, span], right[...])
-            return carry
-
-        lax.fori_loop(0, width // 512, some, 0)
-        store = pltpu.make_async_copy(grads.at[number], out_ref, store_sems.at[number])
-        store.start()
-        return store
-
-    stores = [weight_grad(0, cots, active, grad_down_ref)]
-    reduce.fold_line_own()
-    stores.append(weight_grad(1, rows, d_gate, grad_gate_ref))
-    reduce.fold_line_a()
-    stores.append(weight_grad(2, rows, d_up, grad_up_ref))
+    def weight_grad(number, i):
+        left, right = ((cots, active), (rows, d_gate), (rows, d_up))[number]
+        left = left.reshape(count * length, width)
+        span = pl.ds(512 * i, 512)
+        grads[number, span, :] = contract_rows(left[:, span], right[...])
+
+    def store(number):
+        out_ref = (grad_down_ref, grad_gate_ref, grad_up_ref)[number]
+        stores.append(pltpu.make_async_copy(grads.at[number], out_ref, store_sems.at[number]))
+        stores[-1].start()
+
+    def mix_tile(tile, carry):
+        pair, two, flat, gate = tile_of(tile)
+        mix = contract_cols(active[flat, :], down_ref[...])
+        mix_stage[two] = (gate * mix).astype(BF16).reshape(2, length, width)
+        for slot in pair:
+            mix_twin.start(slot)
+        return carry
+
+    stores = []
+    pieces = width // 512
+    order = ends_first(line)
+    for at, z in enumerate(order):
+        lax.fori_loop(2 * line * at // line, 2 * line * (at + 1) // line, mix_tile, 0)
+        reduce.fold_b(z)
+    for at, z in enumerate(order):
+        if at < pieces:
+            weight_grad(0, at)
+        reduce.fold_b(line + z)
+        reduce.send_a(z)
+    for i in range(line, pieces):
+        weight_grad(0, i)
+    store(0)
     reduce.finish_line()
+    for i in range(pieces):
+        weight_grad(1, i)
+    store(1)
+    reduce.result(total)
+    d_rows_ref[:, mine] = total[...]
+    last = remote(total, d_rows_ref.at[:, mine], last_sems.at[0], last_sems.at[1], place.twin())
+    last.start()
+    for i in range(pieces):
+        weight_grad(2, i)
+    store(2)
 
     def mix_fold(slot, carry):
         mix_twin.take(slot)
@@ -1232,10 +1339,6 @@
     lax.fori_loop(0, count, mix_fold, 0)
     stores.append(pltpu.make_async_copy(mix_parts, mix_ref, store_sems.at[3]))
     stores[-1].start()
-    reduce.result(total)
-    d_rows_ref[:, mine] = total[...]
-    last = remote(total, d_rows_ref.at[:, mine], last_sems.at[0], last_sems.at[1], place.twin())
-    last.start()
     reduce.settle()
     gather.settle()
 
@@ -1273,6 +1376,7 @@
             pltpu.VMEM((count * length, hidden), BF16),
             pltpu.VMEM((count * length, hidden), BF16),
             pltpu.VMEM((count * length, hidden), BF16),
+            pltpu.VMEM((count * length, hidden), F32),
             pltpu.VMEM((count, length, width), BF16),
             pltpu.VMEM((count, length, width), BF16),
             pltpu.VMEM((count, length, half), BF16),
@@ -1556,11 +1660,13 @@
     grad_gate,
     grad_up,
     grad_down,
+    stage,
     sems,
 ):
     pairs = ((gate_in, grad_gate), (up_in, grad_up), (down_in, grad_down))
-    copies = [pltpu.make_async_copy(src, dst.at[0], sems.at[i]) for i, (src, dst) in enumerate(pairs)]
-    for c in copies:
+    takes = [pltpu.make_async_copy(src, stage.at[i], sems.at[0, i]) for i, (src, _) in enumerate(pairs)]
+    copies = [pltpu.make_async_copy(stage.at[i], dst.at[0], sems.at[1, i]) for i, (_, dst) in enumerate(pairs)]
+    for c in takes:
         c.start()
     output[...] = output_in[...]
     input_grad[...] = input_grad_in[...]
@@ -1568,6 +1674,9 @@
     grad_key[...] = key_in[...]
     grad_value[...] = value_in[...]
     grad_out[...] = out_in[...]
+    for take, c in zip(takes, copies):
+        take.wait()
+        c.start()
     total, peaks = notes[0], notes[0]
     for p in range(1, notes.shape[0]):
         total = total + notes[p]
@@ -1611,16 +1720,13 @@
         out_shape=outs + [shape((1, *g.shape), F32) for g in expert_grads],
         in_specs=[IN_VMEM] * 9 + [ANY] * 3,
         out_specs=[IN_VMEM] * 9 + [ANY] * 3,
-        scratch_shapes=[pltpu.SemaphoreType.DMA((3,))],
+        scratch_shapes=[
+            pltpu.VMEM((3, *expert_grads[0].shape), F32),
+            pltpu.SemaphoreType.DMA((2, 3)),
+        ],
         compiler_params=pltpu.CompilerParams(vmem_limit_bytes=56 * 2**20),
         name="finish",
     )(*found, notes, query, key, *expert_grads)
-
-
-def note_tiles(*rows):
-    tiles = [jnp.pad(r.astype(F32), ((0, 0), (0, 128 - r.shape[1]))) for r in rows]
-    tiles += [jnp.zeros_like(tiles[0])] * (8 - len(tiles))
-    return jnp.stack(tiles, axis=1)
 
 
 def on_device_dense(
@@ -1647,19 +1753,7 @@
     count = lax.axis_size("dp")
     line = count // 4
     shard = attn_norm_gain.shape[0]
-    logit_max = jnp.max(router_logits, axis=1, keepdims=True)
-    logit_exp = jnp.exp(router_logits - logit_max)
-    gate_probs = logit_exp / jnp.sum(logit_exp, axis=1, keepdims=True)
-    expert_index = jnp.arange(count, dtype=jnp.int32)
-    named = expert_ids[None, :, :] == expert_index[:, None, None]
-    gate_rows = jnp.sum(jnp.where(named, gate_probs[None], 0.0), axis=2)
-    own_gains = [jnp.broadcast_to(g[None], (count, shard)) for g in (attn_norm_gain, moe_norm_gain)]
-    note = note_tiles(gate_rows, *own_gains)
-    position, allowed = tree_layout(segment_ids[0], parents[0])
-    cosine, sine = (jnp.tile(t[:, 0, :], (1, 4)) for t in rope_tables(position, HEAD_SIZE))
-    first = (jnp.arange(128) % HEAD_SIZE < HEAD_SIZE // 2)[None, :]
-    tables = jnp.stack([cosine, jnp.where(first, -sine, 0.0), jnp.where(first, 0.0, sine)])
-    (moe_in, hidden, normed, head_out, queries, keys, values, probs, peak, gains, notes, *keeps, cots) = run_forward(
+    (moe_in, hidden, normed, head_out, queries, keys, values, probs, peak, tables, gains, notes, *keeps, cots) = run_forward(
         line,
         group_size,
         tokens,
@@ -1668,9 +1762,12 @@
         value_projection,
         w_out,
         cotangent,
-        note,
-        tables,
-        allowed.astype(F32),
+        attn_norm_gain[None],
+        moe_norm_gain[None],
+        router_logits,
+        expert_ids,
+        segment_ids,
+        parents,
     )
     d_moe_in, mix_parts, *expert_grads = run_experts(
         line, moe_in, cots, notes, w_gate[0], w_up[0], w_down[0]

time: 480 us -> 322 us (0.67)
  Pallas kernels: 466 us -> 317 us
  other arithmetic: 8.32 us -> 0 us
    pallas_call x1, Pallas kernels: 147 us -> 6.55 us  [finish(): pl.pallas_call(functools.partial(finish_kernel, group_size), out_shape=ou...]
    pallas_call x1, Pallas kernels: 101 us -> 93.1 us  [run_experts(): pl.pallas_call(functools.partial(experts_kernel, line), out_shape=[jax.Sh...]
where the time goes in v5:
time: 322 us; the launch traced here: 321 us
  Pallas kernels  317 us (98%)
  local copies, waits for them, and re-layouts  4.1 us (1%)
    pallas_call x1, Pallas kernels, run_forward(): pl.pallas_call(functools.partial(forward_kernel, line, group_size), out_s...  111 us
    pallas_call x1, Pallas kernels, run_backward(): pl.pallas_call(functools.partial(backward_kernel, line, group_size), out_...  106 us
    pallas_call x1, Pallas kernels, run_experts(): pl.pallas_call(functools.partial(experts_kernel, line), out_shape=[jax.Sh...  93.1 us
    pallas_call x1, Pallas kernels, finish(): pl.pallas_call(functools.partial(finish_kernel, group_size), out_shape=ou...  6.55 us

profile of v5, /device:TPU:0, one launch (start us, length us, event | category | flops | bytes accessed | tf_op | source)
XLA Modules:
  0.0 321.3 jit_solution(7687272509543572108)
XLA Ops:
  0.6 1.4 copy.28.logits_ref
  2.1 1.4 copy.29.ids_ref
  3.5 110.8 %run_forward.1 = (bf16[128,1536]{1,0:T(8,128)(2,1)}, f32[128,1536]{1,0:T(8,128)}, bf16[128,1536]{1,0:T(8,128)(2,1)}, bf16[128,768]{1,0:T(8,128)(2,1)}, bf16[128,...) custom-call(bf16[128,1536]{1,0:T(8,128)(2,1)} %tokens_ref.3, ...), custom_call_target="tpu_custom_call" | custom-call | tf_op jit(solution)/shard_map/run_forward/pallas_call | solution.py:1121
  114.3 93.1 %run_experts.1 = (f32[128,1536]{1,0:T(8,128)}, bf16[16,128,768]{2,1,0:T(8,128)(2,1)}, f32[1536,256]{1,0:T(8,128)}, f32[1536,256]{1,0:T(8,128)}, f32[1536,256]{1,0:T(8,128)}) custom-call(bf16[128,1536]{1,0:T(8,128)(2,1)} %get-tuple-element.55.rows_ref, bf16[16,128,1536]{2,1,0:T(8,128)(2,1)} %get-tuple-element.56.cot_ref, ...), custom_call_target="tpu_custom_call" | custom-call | tf_op jit(solution)/shard_map/run_experts/pallas_call | solution.py:1362
  207.4 106.1 %run_backward.1 = (f32[128,1536]{1,0:T(8,128)}, bf16[128,1536]{1,0:T(8,128)(2,1)}, f32[96,768]{1,0:T(8,128)}, f32[96,256]{1,0:T(8,128)}, f32[96,256]{1,0:T(8,128...) custom-call(bf16[128,1536]{1,0:T(8,128)(2,1)} %tokens_ref.3, f32[128,1536]{1,0:T(8,128)} %get-tuple-element.54.hidden_ref, ...), custom_call_target="tpu_custom_call" | custom-call | tf_op jit(solution)/shard_map/run_backward/pallas_call | solution.py:1606
  313.5 6.5 %finish.1 = (bf16[128,1536]{1,0:T(8,128)(2,1)}, f32[128,1536]{1,0:T(8,128)}, f32[96,768]{1,0:T(8,128)}, f32[96,256]{1,0:T(8,128)}, f32[96,256]{1,0:T(8,128)}, /*...) custom-call(bf16[128,1536]{1,0:T(8,128)(2,1)} %get-tuple-element.73., ...), custom_call_target="tpu_custom_call" | custom-call | tf_op jit(solution)/shard_map/finish/pallas_call | solution.py:1718
  320.1 1.3 slice_bitcast_fusion

commit v6 on v5

--- a/solution.py
+++ b/solution.py
@@ -715,43 +715,171 @@
 
         lax.fori_loop(0, line, add, 0)
 
-    def settle(self):
-        place, line = self.place, self.place.line
+    def settle_b(self):
+        def wait(k, carry):
+            self._to_b(k).wait_send()
+            return carry
+
+        lax.fori_loop(0, 2 * self.place.line, wait, 0)
+
+    def settle_a(self):
+        place = self.place
 
         def wait(z, carry):
-            self._to_b(z).wait_send()
-            self._to_b(line + z).wait_send()
             self._to_a(z).wait_send()
             pl.when(place.z != z)(lambda: self._to_z(z).wait_send())
             return carry
 
-        lax.fori_loop(0, line, wait, 0)
-
-
-AHEAD = 4
+        lax.fori_loop(0, place.line, wait, 0)
+
+    def settle(self):
+        self.settle_b()
+        self.settle_a()
+
+
+class PackedGather(Gather):
+    def __init__(self, place, dense, packed, compact, picks, mine, send_sem, recv_sem, twin_sems):
+        self.place, self.dense, self.packed, self.compact = place, dense, packed, compact
+        self.own_pick, self.other_pick = picks
+        self.mine, self.fixed = mine, False
+        self.send_sem, self.recv_sem = send_sem, recv_sem
+        view = lambda slot: compact.at[slot, :, mine]
+        self.twin = Twin(place, view, view, twin_sems.at[0], twin_sems.at[1])
+
+    def view(self, slot):
+        return self.dense.at[slot]
+
+    def _to_b(self, slot):
+        line = self.place.line
+        return remote(
+            self.packed.at[slot],
+            self.compact.at[2 * line + slot, :, self.mine],
+            self.send_sem.at[3 * line - 1 + slot],
+            self.recv_sem.at[2 * line + slot],
+            self.place.beside_b(),
+        )
+
+    def take_compact(self, slot):
+        line = self.place.line
+        self._to_b(slot - 2 * line).wait_recv()
+        self.twin.start(slot)
+
+    def take(self, slot):
+        self._copy(slot, slot, 0, self.place.beside_b()).wait_recv()
+
+    def pack(self, slot):
+        block = self.dense[slot]
+        self.packed[slot] = jnp.dot(self.other_pick[slot], block, preferred_element_type=F32).astype(BF16)
+        self._to_b(slot).start()
+        self.compact[slot, :, self.mine] = jnp.dot(
+            self.own_pick[slot], block, preferred_element_type=F32
+        ).astype(BF16)
+        self.twin.start(slot)
+
+    def start(self):
+        place = self.place
+
+        def reach(step):
+            pl.when(place.z >= step)(lambda: self._to_z(-step).start())
+            pl.when(place.z + step < place.line)(lambda: self._to_z(step).start())
+
+        reach(1)
+        self._to_a(place.z).start()
+        for step in range(2, place.line):
+            reach(step)
+        self.pack(place.z)
+
+    def along(self, step):
+        def pass_on(z):
+            self.take(z)
+            self._to_a(z).start()
+            self.pack(z)
+
+        self.near(step, pass_on)
+
+    def across(self, step):
+        line = self.place.line
+
+        def pass_on(z):
+            self.take(line + z)
+            self.pack(line + z)
+
+        self.near(step, pass_on)
+
+
+class PackedReduce(Reduce):
+    def __init__(self, place, compact, picks, *rest):
+        super().__init__(place, *rest)
+        self.compact = compact
+        self.own_pick, self.other_pick = picks
+
+    def _to_b(self, k):
+        line = self.place.line
+        return self._copy(self.compact.at[2 * line + k], self.from_b.at[k], k, self.place.beside_b())
+
+    def fold_b(self, k):
+        self._to_b(k).wait_recv()
+        own = contract_rows(self.own_pick[k], self.compact[k])
+        self.parts[k] = (own + contract_rows(self.other_pick[k], self.from_b[k])).astype(BF16)
+
+
+def selections(place, notes, own_pick, other_pick, gates=None):
+    line = place.line
+    cap, length = own_pick.shape[1:]
+    rows = [notes[part_of(place, slot)][0:1, :] for slot in range(4 * line)]
+    for slot in range(2 * line):
+        note = notes[part_of(place, slot)]
+        rows.append(jnp.where(place.core == 0, note[3:4, :], note[4:5, :]))
+    before = lax.broadcasted_iota(jnp.int32, (length, length), 0) < lax.broadcasted_iota(
+        jnp.int32, (length, length), 1
+    )
+    weights = jnp.concatenate(rows, axis=0)
+    rank = jnp.dot(
+        jnp.where(weights > 0.0, 1.0, 0.0).astype(BF16),
+        jnp.where(before, 1.0, 0.0).astype(BF16),
+        preferred_element_type=F32,
+    )
+    rank = jnp.where(weights > 0.0, rank, -1.0)
+    number = lax.broadcasted_iota(jnp.int32, (cap, length), 0).astype(F32)
+    for i in range(len(rows)):
+        pick = jnp.where(rank[i : i + 1, :] == number, 1.0, 0.0)
+        if i >= 4 * line:
+            other_pick[i - 4 * line] = pick.astype(BF16)
+            continue
+        own_pick[i] = pick.astype(BF16)
+        if gates is not None:
+            gates[cap * i : cap * (i + 1), :] = jnp.sum(pick * rows[i], axis=1, keepdims=True)
+
+
+AHEAD = 8
 
 
 class Reductions:
     def __init__(self, reduces, finish):
-        self.reduces, self.finish, self.at = reduces, finish, 0
+        self.reduces, self.finish = reduces, finish
+        self.at = self.sent = self.limit = 0
         line = self.line = reduces[0].place.line
         self.ks = [line + z for z in ends_first(line)] + ends_first(line)
         self.steps = [(i, k) for i in range(len(reduces)) for k in self.ks]
 
-    def start(self):
-        for i, k in self.steps[:AHEAD]:
+    def ready(self, number):
+        self.limit = 2 * self.line * number
+        self._send()
+
+    def _send(self):
+        while self.sent < min(self.at + AHEAD, self.limit):
+            i, k = self.steps[self.sent]
             self.reduces[i].send_b(k)
+            self.sent += 1
 
     def run(self, number):
         for _ in range(number):
             self._step()
 
     def _step(self):
-        if self.at + AHEAD < len(self.steps):
-            ahead, block = self.steps[self.at + AHEAD]
-            self.reduces[ahead].send_b(block)
         i, k = self.steps[self.at]
         self.at += 1
+        self._send()
         self.reduces[i].fold_b(k)
         if k >= self.line:
             self.reduces[i].send_a(k - self.line)
@@ -830,26 +958,29 @@
     return total
 
 
-def gate_table(logits, ids):
-    expo = jnp.exp(logits - jnp.max(logits, axis=1, keepdims=True))
-    probs = expo / jnp.sum(expo, axis=1, keepdims=True)
-    length, top = logits.shape
-    expert = lax.broadcasted_iota(jnp.int32, (length, 128), 1)
-    table = jnp.zeros((length, 128), F32)
+def gate_table(logits, ids, experts):
+    expo = jnp.exp(logits - jnp.max(logits, axis=0, keepdims=True))
+    probs = expo / jnp.sum(expo, axis=0, keepdims=True)
+    top, length = logits.shape
+    expert = lax.broadcasted_iota(jnp.int32, (experts, length), 0)
+    table = jnp.zeros((experts, length), F32)
     for c in range(top):
-        table += jnp.where(ids[:, c : c + 1] == expert, probs[:, c : c + 1], 0.0)
-    return jnp.transpose(table)
+        table += jnp.where(ids[c : c + 1, :] == expert, probs[c : c + 1, :], 0.0)
+    return table
 
 
 def write_notes(note_ref, gates, gains):
     shard = gains[0].shape[1]
     row = lax.broadcasted_iota(jnp.int32, (8, 128), 0)
     pad = jnp.zeros((1, 128 - shard), F32)
-    below = jnp.zeros((8, 128), F32)
+    shared = jnp.zeros((8, 128), F32)
     for i, gain in enumerate(gains):
-        below = jnp.where(row == i + 1, jnp.concatenate([gain, pad], axis=1), below)
+        shared = jnp.where(row == i + 1, jnp.concatenate([gain, pad], axis=1), shared)
     for p in range(note_ref.shape[0]):
-        note_ref[p] = jnp.where(row == 0, gates[p : p + 1, :], below)
+        tile = shared
+        for at, e in ((0, p), (3, p + 1 - 2 * (p % 2)), (4, p + 2 - 4 * (p // 2 % 2))):
+            tile = jnp.where(row == at, gates[e : e + 1, :], tile)
+        note_ref[p] = tile
 
 
 def tree_tables(segments, parents, length):
@@ -923,7 +1054,11 @@
     key_all,
     value_all,
     out_all,
+    cot_dense,
+    cot_packed,
     cot_all,
+    own_pick,
+    other_pick,
     mix_mine,
     mix_other,
     note_ref,
@@ -946,7 +1081,7 @@
     blocks = ((query_ref, query_all), (key_ref, key_all), (value_ref, value_all), (out_ref, out_all))
     for i, (src, dst) in enumerate(blocks):
         own.append(pltpu.make_async_copy(src, dst.at[place.me], local_sems.at[i]))
-    own.append(pltpu.make_async_copy(cot_ref, cot_all.at[place.z], local_sems.at[4]))
+    own.append(pltpu.make_async_copy(cot_ref.at[:, span], cot_dense.at[place.z], local_sems.at[4]))
     for c in own:
         c.start()
     enter(place)
@@ -957,14 +1092,14 @@
         Gather(place, lambda s, ref=ref: ref.at[part_of(place, s)], sends.at[i], recvs.at[i], True)
         for i, ref in enumerate((query_all, key_all, value_all, out_all))
     ]
-    cot_view = lambda s: cot_all.at[s, :, span]
-    cot = Gather(place, cot_view, sends.at[4], recvs.at[4])
-    twin = Twin(place, cot_view, cot_view, twin_sems.at[0], twin_sems.at[1])
+    picks = (own_pick, other_pick)
+    cot = PackedGather(place, cot_dense, cot_packed, cot_all, picks, span, sends.at[4], recvs.at[4], twin_sems)
+    twin = cot.twin
     out = gathers[3]
     for g in gathers[:3]:
         g.start()
     gains = [g[...].astype(F32) for g in (gain_a_ref, gain_m_ref)]
-    write_notes(note_ref, gate_table(logits_ref[...], ids_ref[...]), gains)
+    write_notes(note_ref, gate_table(logits_ref[...], ids_ref[...], count), gains)
     note.start()
     inputs = tokens_ref[...].astype(F32)
     inv_attn = lax.rsqrt(jnp.mean(inputs * inputs, axis=1, keepdims=True) + EPSILON)
@@ -977,6 +1112,7 @@
         g.across(0)
     position, allowed = tree_tables(segments_ref[...], parents_ref[...], length)
     write_tables(tables_ref, position)
+    selections(place, notes, own_pick, other_pick)
     for step in range(2, line + 1):
         for g in gathers[:3]:
             if step < line:
@@ -984,6 +1120,7 @@
             g.across(step - 1)
         if step == line - 1:
             out.start()
+            cot.start()
     for g in gathers[:3]:
         g.take_rest()
     normed = normed_ref[...]
@@ -993,8 +1130,6 @@
         queries_ref[:, 128 * j : 128 * (j + 1)] = rope_chunk(
             query_lin[:, 128 * j : 128 * (j + 1)], tables, 1.0
         ).astype(BF16)
-    out.along(1)
-    out.across(0)
     kv_cols = key_ref.shape[1]
     key_lin = jnp.dot(normed, key_all[...].reshape(width, kv_cols), preferred_element_type=F32)
     for j in range(kv_cols // 128):
@@ -1007,12 +1142,12 @@
     lane = lax.broadcasted_iota(jnp.int32, (length, 128), 1)
     small_lane = lax.broadcasted_iota(jnp.int32, (8, 128), 1)
     peaks = jnp.zeros((8, 128), F32)
-    between = {
-        0: lambda: (out.along(2), out.across(1)),
-        1: lambda: out.along(3) if line > 3 else None,
-        2: lambda: (cot.start(), out.across(2)),
-        3: lambda: out.across(3) if line > 3 else None,
-    }
+    for step in range(1, line + 1):
+        if step < line:
+            out.along(step)
+            cot.along(step)
+        out.across(step - 1)
+        cot.across(step - 1)
     for j in range(chunks):
         both = contract_cols(chunk_of(queries_ref, j), pair_of(keys_ref, j, group_size, lane)) * SCORE_SCALE
         low = []
@@ -1031,8 +1166,6 @@
             preferred_element_type=F32,
         )
         head_out_ref[:, 128 * j : 128 * (j + 1)] = mixed.astype(BF16)
-        if j in between:
-            between[j]()
     peak_ref[...] = peaks
     keeps = [
         pltpu.make_async_copy(src, dst, keep_sems.at[i])
@@ -1053,21 +1186,14 @@
     mix_mine[...] = contract_cols(head_out_ref[...], out_all[...].reshape(width, q_cols))
     swap = remote(mix_mine, mix_other, mix_sems.at[0], mix_sems.at[1], place.twin())
     swap.start()
-    cot.along(1, twin.start)
-    cot.across(0, twin.start)
     swap.wait()
     hidden = tokens_ref[...].astype(F32) + RESIDUAL * (mix_mine[...] + mix_other[...])
     hidden_ref[...] = hidden
     inv_moe = lax.rsqrt(jnp.mean(hidden * hidden, axis=1, keepdims=True) + EPSILON)
     moe_in_ref[...] = (hidden * inv_moe * gains_ref[2:3, :]).astype(BF16)
-    for step in range(2, line + 1):
-        if step < line:
-            cot.along(step, twin.start)
-        cot.across(step - 1, twin.start)
 
     def rest(slot, carry):
-        cot.take(slot)
-        twin.start(slot)
+        cot.take_compact(slot)
         return carry
 
     lax.fori_loop(2 * line, count, rest, 0)
@@ -1075,11 +1201,8 @@
         g.settle()
 
     def other(slot, carry):
-        @pl.when(slot != place.z)
-        def _():
-            twin.wait_send(slot)
-            twin.take(slot)
-
+        twin.wait_send(slot)
+        twin.take(slot)
         return carry
 
     lax.fori_loop(0, count, other, 0)
@@ -1098,11 +1221,17 @@
     )
 
 
+def capacity_of(length, experts):
+    most = 4 * (9 * length * TOP // (32 * experts))
+    return min(-(-most // 16) * 16, length)
+
+
 def run_forward(line, group_size, tokens, query, key, value, out, cotangent, *small):
     count = 4 * line
     length, width = tokens.shape
     q_cols, kv_cols = query.shape[1], key.shape[1]
-    blocks = [x.shape for x in (query, key, value, out, cotangent)]
+    half, cap = width // 2, capacity_of(length, count)
+    blocks = [x.shape for x in (query, key, value, out)] + [(cap, width)]
     shape = jax.ShapeDtypeStruct
     outs = [
         shape((length, width), BF16),
@@ -1123,8 +1252,13 @@
         out_shape=outs + [shape((count, *s), BF16) for s in blocks],
         in_specs=[IN_VMEM] + [ANY] * 5 + [IN_VMEM] * len(small),
         out_specs=[IN_VMEM] * len(outs) + [ANY] * 5,
-        scratch_shapes=[pltpu.VMEM((count, *s), BF16) for s in blocks]
+        scratch_shapes=[pltpu.VMEM((count, *s), BF16) for s in blocks[:4]]
         + [
+            pltpu.VMEM((2 * line, length, half), BF16),
+            pltpu.VMEM((2 * line, cap, half), BF16),
+            pltpu.VMEM((count, cap, width), BF16),
+            pltpu.VMEM((count, cap, length), BF16),
+            pltpu.VMEM((2 * line, cap, length), BF16),
             pltpu.VMEM((length, width), F32),
             pltpu.VMEM((length, width), F32),
             pltpu.VMEM((count, 8, 128), F32),
@@ -1155,23 +1289,30 @@
     grad_gate_ref,
     grad_up_ref,
     grad_down_ref,
+    dense,
+    packed,
     rows,
     cots,
+    own_pick,
+    other_pick,
+    gates,
     active,
     d_gate,
     d_up,
     d_active,
     grad_stage,
     mix_stage,
-    grad_parts,
-    mix_parts,
+    grad_compact,
+    mix_compact,
+    grad_dense,
+    mix_dense,
     grads,
     total,
-    from_b,
+    grad_from_b,
+    mix_from_b,
     from_a,
     from_z,
-    reduce_send,
-    reduce_recv,
+    reduce_sems,
     gather_send,
     gather_recv,
     twin_sems,
@@ -1181,62 +1322,51 @@
 ):
     place = Place(line)
     count = 4 * line
-    length, width = rows_ref.shape
-    hidden = gate_ref.shape[1]
+    cap, width = rows.shape[1:]
+    tile_rows = line * cap
     mine, theirs = halves(place, width)
-
-    def load(slot):
-        return pltpu.make_async_copy(cot_ref.at[slot], cots.at[slot], load_sems.at[slot])
-
-    def begin(slot, carry):
-        load(slot).start()
-        return carry
-
-    lax.fori_loop(0, count, begin, 0)
-    rows[place.z] = rows_ref[...]
+    load = pltpu.make_async_copy(cot_ref, cots, load_sems)
+    load.start()
+    dense[place.z] = rows_ref[:, mine]
+    picks = (own_pick, other_pick)
+    selections(place, notes_ref, own_pick, other_pick, gates)
     enter(place)
-    view = lambda s: rows.at[s, :, mine]
-    gather = Gather(place, view, gather_send, gather_recv)
-    row_twin = Twin(place, view, view, twin_sems.at[0], twin_sems.at[1])
+    gather = PackedGather(place, dense, packed, rows, picks, mine, gather_send, gather_recv, twin_sems)
     grad_twin = Twin(
-        place, lambda s: grad_stage.at[s, :, theirs], lambda s: grad_parts.at[s], twin_sems.at[2], twin_sems.at[3]
+        place,
+        lambda s: grad_stage.at[s, :, theirs],
+        lambda s: grad_compact.at[s],
+        twin_sems.at[2],
+        twin_sems.at[3],
     )
     mix_twin = Twin(
-        place, lambda s: mix_stage.at[s, :, theirs], lambda s: mix_parts.at[s], twin_sems.at[4], twin_sems.at[5]
-    )
-    reduce = Reduce(place, grad_parts, from_b, from_a, from_z, reduce_send, reduce_recv)
-
-    def fold(slot):
-        grad_twin.take(slot)
-        reduce._add(slot, grad_stage[slot, :, mine])
-        pl.when(slot >= 2 * line)(lambda: reduce.send_b(slot - 2 * line))
-
-    def column(slot):
-        return jnp.transpose(notes_ref[part_of(place, slot)])[:, 0:1]
-
-    def tile_of(tile):
-        first = 2 * tile
-        pair = (first, first + 1)
-        gate = jnp.concatenate([column(slot) for slot in pair], axis=0)
-        return pair, pl.ds(first, 2), pl.ds(pl.multiple_of(first * length, 2 * length), 2 * length), gate
-
-    def ahead(tile, carry):
-        pair, two, flat, gate = tile_of(tile)
-        for slot in pair:
-            load(slot).wait()
-        d_out = (gate * (RESIDUAL * cots[two].reshape(2 * length, width).astype(F32))).astype(BF16)
-        cots[two] = d_out.reshape(2, length, width)
+        place, lambda s: mix_stage.at[s, :, theirs], lambda s: mix_compact.at[s], twin_sems.at[4], twin_sems.at[5]
+    )
+    reduce = PackedReduce(
+        place, grad_compact, picks, grad_dense, grad_from_b, from_a, from_z, reduce_sems.at[0], reduce_sems.at[1]
+    )
+    mix_reduce = PackedReduce(
+        place, mix_compact, picks, mix_dense, mix_from_b, None, None, reduce_sems.at[2], reduce_sems.at[3]
+    )
+
+    def group_of(group):
+        return pl.ds(line * group, line), pl.ds(tile_rows * group, tile_rows)
+
+    def slots_of(group):
+        return [line * group + z for z in range(line)]
+
+    def ahead(group):
+        some, flat = group_of(group)
+        cot = cots[some].reshape(tile_rows, width).astype(F32)
+        d_out = (gates[flat, :] * (RESIDUAL * cot)).astype(BF16)
+        cots[some] = d_out.reshape(line, cap, width)
         d_active[flat, :] = jnp.dot(d_out, down_ref[...], preferred_element_type=F32)
-        return carry
-
-    def step(tile, carry):
-        first = 2 * tile
-        pair = (first, first + 1)
-        two = pl.ds(first, 2)
-        flat = pl.ds(pl.multiple_of(first * length, 2 * length), 2 * length)
-        for slot in pair:
-            pl.when(slot != place.z)(lambda slot=slot: row_twin.take(slot))
-        x = rows[two].reshape(2 * length, width)
+
+    def work(group):
+        some, flat = group_of(group)
+        for slot in slots_of(group):
+            gather.twin.take(slot)
+        x = rows[some].reshape(tile_rows, width)
         gate_pre = jnp.dot(x, gate_ref[...], preferred_element_type=F32)
         up_pre = jnp.dot(x, up_ref[...], preferred_element_type=F32)
         sigmoid = 1.0 / (1.0 + jnp.exp(-gate_pre))
@@ -1248,81 +1378,88 @@
         d_gate[flat, :] = d_g
         d_up[flat, :] = d_u
         d_in = contract_cols(d_g, gate_ref[...]) + contract_cols(d_u, up_ref[...])
-        grad_stage[two] = d_in.astype(BF16).reshape(2, length, width)
-        for slot in pair:
+        grad_stage[some] = d_in.astype(BF16).reshape(line, cap, width)
+        for slot in slots_of(group):
             grad_twin.start(slot)
-        group = (tile + 1) // (line // 2)
-
-        @pl.when(jnp.logical_or(group == 1, group == 3))
-        def _():
-            for slot in (first + 2, first + 3):
-                slot = slot + line * (3 - group) // 2
-                gather.take(slot)
-                row_twin.start(slot)
-
-        @pl.when(jnp.logical_and(tile > 0, (first - 1) // line != 1))
-        def _():
-            for slot in (first - 2, first - 1):
-                fold(slot)
-
-        return carry
-
-    gather.start()
-    share = 2 * line // 4
-    for at in range(4):
-        lax.fori_loop(at * share, (at + 1) * share, ahead, 0)
-        steps = range(1, line + 1)[at * line // 4 : (at + 1) * line // 4]
-        for k in steps:
-            if k < line:
-                gather.along(k, row_twin.start)
-            gather.across(k - 1, row_twin.start)
-    lax.fori_loop(0, 2 * line, step, 0)
-    for slot in (count - 2, count - 1):
-        fold(slot)
-
-    def fold_late(slot, carry):
-        fold(slot)
-        return carry
-
-    lax.fori_loop(line, 2 * line, fold_late, 0)
+
+    def mix_work(group):
+        some, flat = group_of(group)
+        mix = gates[flat, :] * contract_cols(active[flat, :], down_ref[...])
+        mix_stage[some] = mix.astype(BF16).reshape(line, cap, width)
+        for slot in slots_of(group):
+            mix_twin.start(slot)
+
+    def fold(twin, stage, compact, group, send=None):
+        def one(slot, carry):
+            twin.take(slot)
+            compact[slot] = (compact[slot].astype(F32) + stage[slot, :, mine].astype(F32)).astype(BF16)
+            if send is not None:
+                send(slot - 2 * line)
+            return carry
+
+        lax.fori_loop(line * group, line * (group + 1), one, 0)
+
+    def take_group(group):
+        for slot in slots_of(group):
+            gather.take_compact(slot)
 
     def weight_grad(number, i):
         left, right = ((cots, active), (rows, d_gate), (rows, d_up))[number]
-        left = left.reshape(count * length, width)
+        left = left.reshape(count * cap, width)
         span = pl.ds(512 * i, 512)
         grads[number, span, :] = contract_rows(left[:, span], right[...])
+
+    stores = []
 
     def store(number):
         out_ref = (grad_down_ref, grad_gate_ref, grad_up_ref)[number]
         stores.append(pltpu.make_async_copy(grads.at[number], out_ref, store_sems.at[number]))
         stores[-1].start()
 
-    def mix_tile(tile, carry):
-        pair, two, flat, gate = tile_of(tile)
-        mix = contract_cols(active[flat, :], down_ref[...])
-        mix_stage[two] = (gate * mix).astype(BF16).reshape(2, length, width)
-        for slot in pair:
-            mix_twin.start(slot)
-        return carry
-
-    stores = []
+    grad_fold = functools.partial(fold, grad_twin, grad_stage, grad_compact)
+    mix_fold = functools.partial(fold, mix_twin, mix_stage, mix_compact)
+    gather.start()
+    load.wait()
+    for at in range(max(line, 4)):
+        if at < 4:
+            ahead(at)
+        if at < line:
+            if at + 1 < line:
+                gather.along(at + 1)
+            gather.across(at)
+    work(0)
+    take_group(2)
+    work(2)
+    work(1)
+    take_group(3)
+    grad_fold(2, reduce.send_b)
+    work(3)
+    grad_fold(3, reduce.send_b)
+    mix_work(1)
+    grad_fold(0)
+    mix_work(2)
+    grad_fold(1)
+    mix_work(3)
+    mix_fold(2, mix_reduce.send_b)
+    mix_work(0)
     pieces = width // 512
     order = ends_first(line)
+    for z in order:
+        reduce.fold_b(z)
+    weight_grad(0, 0)
     for at, z in enumerate(order):
-        lax.fori_loop(2 * line * at // line, 2 * line * (at + 1) // line, mix_tile, 0)
-        reduce.fold_b(z)
-    for at, z in enumerate(order):
-        if at < pieces:
-            weight_grad(0, at)
         reduce.fold_b(line + z)
         reduce.send_a(z)
-    for i in range(line, pieces):
+    mix_fold(3, mix_reduce.send_b)
+    for i in range(1, pieces):
         weight_grad(0, i)
     store(0)
     reduce.finish_line()
     for i in range(pieces):
         weight_grad(1, i)
     store(1)
+    mix_fold(0)
+    mix_fold(1)
     reduce.result(total)
     d_rows_ref[:, mine] = total[...]
     last = remote(total, d_rows_ref.at[:, mine], last_sems.at[0], last_sems.at[1], place.twin())
@@ -1330,20 +1467,16 @@
     for i in range(pieces):
         weight_grad(2, i)
     store(2)
-
-    def mix_fold(slot, carry):
-        mix_twin.take(slot)
-        mix_parts[slot] = (mix_parts[slot].astype(F32) + mix_stage[slot, :, mine].astype(F32)).astype(BF16)
-        return carry
-
-    lax.fori_loop(0, count, mix_fold, 0)
-    stores.append(pltpu.make_async_copy(mix_parts, mix_ref, store_sems.at[3]))
+    for k in range(2 * line):
+        mix_reduce.fold_b(k)
+    stores.append(pltpu.make_async_copy(mix_dense, mix_ref, store_sems.at[3]))
     stores[-1].start()
     reduce.settle()
+    mix_reduce.settle_b()
     gather.settle()
 
     def settle(slot, carry):
-        pl.when(slot != place.z)(lambda: row_twin.wait_send(slot))
+        gather.twin.wait_send(slot)
         grad_twin.wait_send(slot)
         mix_twin.wait_send(slot)
         return carry
@@ -1357,13 +1490,14 @@
 def run_experts(line, rows, cots, notes, gate, up, down):
     count = 4 * line
     length, width = rows.shape
+    cap = cots.shape[1]
     half, hidden = width // 2, gate.shape[1]
     grad = jax.ShapeDtypeStruct((width, hidden), F32)
     return pl.pallas_call(
         functools.partial(experts_kernel, line),
         out_shape=[
             jax.ShapeDtypeStruct((length, width), F32),
-            jax.ShapeDtypeStruct((count, length, half), BF16),
+            jax.ShapeDtypeStruct((2 * line, length, half), BF16),
             grad,
             grad,
             grad,
@@ -1371,25 +1505,34 @@
         in_specs=[IN_VMEM, ANY, IN_VMEM, IN_VMEM, IN_VMEM, IN_VMEM],
         out_specs=[IN_VMEM, ANY, ANY, ANY, ANY],
         scratch_shapes=[
-            pltpu.VMEM((count, length, width), BF16),
-            pltpu.VMEM((count, length, width), BF16),
-            pltpu.VMEM((count * length, hidden), BF16),
-            pltpu.VMEM((count * length, hidden), BF16),
-            pltpu.VMEM((count * length, hidden), BF16),
-            pltpu.VMEM((count * length, hidden), F32),
-            pltpu.VMEM((count, length, width), BF16),
-            pltpu.VMEM((count, length, width), BF16),
-            pltpu.VMEM((count, length, half), BF16),
-            pltpu.VMEM((count, length, half), BF16),
+            pltpu.VMEM((2 * line, length, half), BF16),
+            pltpu.VMEM((2 * line, cap, half), BF16),
+            pltpu.VMEM((count, cap, width), BF16),
+            pltpu.VMEM((count, cap, width), BF16),
+            pltpu.VMEM((count, cap, length), BF16),
+            pltpu.VMEM((2 * line, cap, length), BF16),
+            pltpu.VMEM((count * cap, 1), F32),
+            pltpu.VMEM((count * cap, hidden), BF16),
+            pltpu.VMEM((count * cap, hidden), BF16),
+            pltpu.VMEM((count * cap, hidden), BF16),
+            pltpu.VMEM((count * cap, hidden), F32),
+            pltpu.VMEM((count, cap, width), BF16),
+            pltpu.VMEM((count, cap, width), BF16),
+            pltpu.VMEM((count, cap, half), BF16),
+            pltpu.VMEM((count, cap, half), BF16),
+            pltpu.VMEM((2 * line, length, half), BF16),
+            pltpu.VMEM((2 * line, length, half), BF16),
             pltpu.VMEM((3, width, hidden), F32),
             pltpu.VMEM((length, half), F32),
-        ]
-        + reduce_scratch(line, (length, half))
-        + [
+            pltpu.VMEM((2 * line, cap, half), BF16),
+            pltpu.VMEM((2 * line, cap, half), BF16),
+            pltpu.VMEM((line, length, half), BF16),
+            pltpu.VMEM((line, length, half), BF16),
+            pltpu.SemaphoreType.DMA((4, 4 * line)),
             pltpu.SemaphoreType.DMA((5 * line,)),
             pltpu.SemaphoreType.DMA((count,)),
             pltpu.SemaphoreType.DMA((6, count)),
-            pltpu.SemaphoreType.DMA((count,)),
+            pltpu.SemaphoreType.DMA,
             pltpu.SemaphoreType.DMA((2,)),
             pltpu.SemaphoreType.DMA((4,)),
         ],
@@ -1470,7 +1613,7 @@
         load(slot).wait()
         return carry
 
-    lax.fori_loop(0, count, begin, 0)
+    lax.fori_loop(0, 2 * line, begin, 0)
     weights = [
         pltpu.make_async_copy(src, dst, weight_sems.at[i])
         for i, (src, dst) in enumerate(
@@ -1480,21 +1623,20 @@
     for c in weights:
         c.start()
     enter(place)
-    lax.fori_loop(0, count, loaded, 0)
+    lax.fori_loop(0, 2 * line, loaded, 0)
     mine, theirs = halves(place, width)
     outs = (query_sum, key_sum, value_sum, out_sum, total)
-    order = (4, 3, 0, 1, 2)
+    order = (3, 0, 1, 2)
+    mix = reduces[4]
+    for z in ends_first(line):
+        mix.send_a(z)
     last = remote(total, mix_total.at[:, mine], last_sems.at[0], last_sems.at[1], place.twin())
 
     def finish(at):
         i = order[at]
         reduces[i].result(outs[i])
-        if i == 4:
-            mix_total[:, mine] = total[...]
-            last.start()
 
     run = Reductions([reduces[i] for i in order], finish)
-    run.start()
     hidden = hidden_ref[...]
     inv_moe = lax.rsqrt(jnp.mean(hidden * hidden, axis=1, keepdims=True) + EPSILON)
     unit_moe = hidden * inv_moe
@@ -1506,18 +1648,17 @@
     d_hidden_keep[...] = d_hidden
     moe_gain = jnp.sum(d_rows * unit_moe, axis=0, keepdims=True)
     d_attn = (RESIDUAL * d_hidden).astype(BF16)
-    run.run(2)
     work[3][...] = contract_rows(d_attn, head_out_ref[...]).astype(BF16).reshape(count, shard, q_cols)
-    run.run(2)
+    run.ready(1)
     weights[0].wait()
     d_heads[...] = jnp.dot(
         d_attn, out_all[...].reshape(width, q_cols), preferred_element_type=F32
     ).astype(BF16)
-    run.run(1)
     lane = lax.broadcasted_iota(jnp.int32, (length, 128), 1)
     d_key[...] = jnp.zeros_like(d_key)
     d_value[...] = jnp.zeros_like(d_value)
     tables = [tables_ref[i] for i in range(3)]
+    mix.finish_line()
     for j in range(chunks):
         d_out = chunk_of(d_heads, j)
         keys = pair_of(keys_ref, j, group_size, lane)
@@ -1546,6 +1687,7 @@
         run.run(1)
     normed = normed_ref[...]
     work[0][...] = contract_rows(normed, d_query[...]).astype(BF16).reshape(count, shard, q_cols)
+    run.ready(2)
     d_key_lin = jnp.concatenate(
         [rope_chunk(chunk_of(d_key, j), tables, -1.0) for j in range(kv_cols // 128)], axis=1
     ).astype(BF16)
@@ -1553,7 +1695,11 @@
     run.run(2)
     work[1][...] = contract_rows(normed, d_key_lin).astype(BF16).reshape(count, shard, kv_cols)
     work[2][...] = contract_rows(normed, d_value_lin).astype(BF16).reshape(count, shard, kv_cols)
+    run.ready(4)
     run.run(2)
+    mix.result(total)
+    mix_total[:, mine] = total[...]
+    last.start()
     for c in weights[1:]:
         c.wait()
     part_mine[...] = (
@@ -1563,7 +1709,7 @@
     )
     swap = remote(part_mine, part_other, part_sems.at[0], part_sems.at[1], place.twin())
     swap.start()
-    run.run(2)
+    run.run(4)
     swap.wait()
     d_normed = part_mine[...] + part_other[...]
     inputs = tokens_ref[...].astype(F32)
@@ -1583,8 +1729,9 @@
     exchange = Notes(place, note, notes, note_sends, note_recvs, False)
     exchange.start()
     run.complete()
-    for r in reduces:
+    for r in reduces[:4]:
         r.settle()
+    mix.settle_a()
     last.wait()
     output_ref[...] = (hidden_ref[...] + RESIDUAL * mix_total[...]).astype(BF16)
     exchange.finish()
@@ -1609,7 +1756,8 @@
         in_specs=[IN_VMEM] * len(kept) + [ANY] * 5,
         out_specs=[IN_VMEM] * len(outs),
         scratch_shapes=[pltpu.VMEM(x.shape, BF16) for x in keeps]
-        + [pltpu.VMEM((count, *s), BF16) for s in blocks]
+        + [pltpu.VMEM((count, *s), BF16) for s in blocks[:4]]
+        + [pltpu.VMEM(mix.shape, BF16)]
         + [x for s in blocks for x in reduce_scratch(line, s)]
         + [
             pltpu.VMEM((length, half), F32),
@@ -1654,7 +1802,8 @@
     grad_key,
     grad_value,
     grad_out,
-    gains,
+    gain_a,
+    gain_m,
     clipped_query,
     clipped_key,
     grad_gate,
@@ -1681,7 +1830,9 @@
     for p in range(1, notes.shape[0]):
         total = total + notes[p]
         peaks = jnp.maximum(peaks, notes[p])
-    gains[...] = total
+    shard = gain_a.shape[1]
+    gain_a[...] = total[0:1, :shard]
+    gain_m[...] = total[1:2, :shard]
     factor = CLIP_LIMIT / jnp.maximum(peaks, CLIP_LIMIT)
     root = jnp.sqrt(factor)
     lane = lax.broadcasted_iota(jnp.int32, (8, 128), 1)
@@ -1710,8 +1861,10 @@
 
 def finish(group_size, found, notes, query, key, expert_grads):
     shape = jax.ShapeDtypeStruct
+    shard = query.shape[0]
     outs = [shape(x.shape, x.dtype) for x in found] + [
-        shape((8, 128), F32),
+        shape((1, shard), F32),
+        shape((1, shard), F32),
         shape(query.shape, F32),
         shape(key.shape, F32),
     ]
@@ -1719,7 +1872,7 @@
         functools.partial(finish_kernel, group_size),
         out_shape=outs + [shape((1, *g.shape), F32) for g in expert_grads],
         in_specs=[IN_VMEM] * 9 + [ANY] * 3,
-        out_specs=[IN_VMEM] * 9 + [ANY] * 3,
+        out_specs=[IN_VMEM] * 10 + [ANY] * 3,
         scratch_shapes=[
             pltpu.VMEM((3, *expert_grads[0].shape), F32),
             pltpu.SemaphoreType.DMA((2, 3)),
@@ -1764,8 +1917,8 @@
         cotangent,
         attn_norm_gain[None],
         moe_norm_gain[None],
-        router_logits,
-        expert_ids,
+        router_logits.T,
+        expert_ids.T,
         segment_ids,
         parents,
     )
@@ -1774,18 +1927,18 @@
     )
     kept = (tokens, hidden, d_moe_in, cotangent, normed, head_out, queries, keys, values, probs, gains, peak, tables)
     input_grad, output, *grads, sums = run_backward(line, group_size, kept, keeps, mix_parts)
-    output, input_grad, gq, gk, gv, go, gains, clipped_query, clipped_key, gg, gu, gd = finish(
+    output, input_grad, gq, gk, gv, go, gain_a, gain_m, clipped_query, clipped_key, gg, gu, gd = finish(
         group_size, (output, input_grad, *grads), sums, w_query, key_projection, expert_grads
     )
     return (
         output,
         input_grad,
-        gains[0, :shard],
+        gain_a[0],
         gq,
         gk,
         gv,
         go,
-        gains[1, :shard],
+        gain_m[0],
         gg,
         gu,
         gd,

time: 322 us -> 289 us (0.90)
  Pallas kernels: 317 us -> 288 us
  local copies, waits for them, and re-layouts: 4.1 us -> 0 us
    pallas_call x1, Pallas kernels: 106 us -> 88.6 us  [run_backward(): pl.pallas_call(functools.partial(backward_kernel, line, group_size), out_...]
    pallas_call x1, Pallas kernels: 111 us -> 105 us  [run_forward(): pl.pallas_call(functools.partial(forward_kernel, line, group_size), out_s...]
    pallas_call x1, Pallas kernels: 93.1 us -> 88.2 us  [run_experts(): pl.pallas_call(functools.partial(experts_kernel, line), out_shape=[jax.Sh...]
where the time goes in v6:
time: 289 us
  Pallas kernels  288 us (100%)
    pallas_call x1, Pallas kernels, run_forward(): pl.pallas_call(functools.partial(forward_kernel, line, group_size), out_s...  105 us
    pallas_call x1, Pallas kernels, run_backward(): pl.pallas_call(functools.partial(backward_kernel, line, group_size), out_...  88.6 us
    pallas_call x1, Pallas kernels, run_experts(): pl.pallas_call(functools.partial(experts_kernel, line), out_shape=[jax.Sh...  88.2 us
    pallas_call x1, Pallas kernels, finish(): pl.pallas_call(functools.partial(finish_kernel, group_size), out_shape=ou...  6.55 us

profile of v6, /device:TPU:0, one launch (start us, length us, event | category | flops | bytes accessed | tf_op | source)
XLA Modules:
  0.0 288.7 jit_solution(4938708968266687837)
XLA Ops:
  0.6 104.6 %run_forward.1 = (bf16[128,1536]{1,0:T(8,128)(2,1)}, f32[128,1536]{1,0:T(8,128)}, bf16[128,1536]{1,0:T(8,128)(2,1)}, bf16[128,768]{1,0:T(8,128)(2,1)}, bf16[128,...) custom-call(bf16[128,1536]{1,0:T(8,128)(2,1)} %tokens_ref.3, ...), custom_call_target="tpu_custom_call" | custom-call | tf_op jit(solution)/shard_map/run_forward/pallas_call | solution.py:1250
  105.2 88.2 %run_experts.1 = (f32[128,1536]{1,0:T(8,128)}, bf16[8,128,768]{2,1,0:T(8,128)(2,1)}, f32[1536,256]{1,0:T(8,128)}, f32[1536,256]{1,0:T(8,128)}, f32[1536,256]{1,0:T(8,128)}) custom-call(bf16[128,1536]{1,0:T(8,128)(2,1)} %get-tuple-element.56.rows_ref, bf16[16,80,1536]{2,1,0:T(8,128)(2,1)} %get-tuple-element.57.cot_ref, ...), custom_call_target="tpu_custom_call" | custom-call | tf_op jit(solution)/shard_map/run_experts/pallas_call | solution.py:1496
  193.4 88.6 %run_backward.1 = (f32[128,1536]{1,0:T(8,128)}, bf16[128,1536]{1,0:T(8,128)(2,1)}, f32[96,768]{1,0:T(8,128)}, f32[96,256]{1,0:T(8,128)}, f32[96,256]{1,0:T(8,128...) custom-call(bf16[128,1536]{1,0:T(8,128)(2,1)} %tokens_ref.3, f32[128,1536]{1,0:T(8,128)} %get-tuple-element.55.hidden_ref, ...), custom_call_target="tpu_custom_call" | custom-call | tf_op jit(solution)/shard_map/run_backward/pallas_call | solution.py:1753
  282.0 6.6 %finish.1 = (bf16[128,1536]{1,0:T(8,128)(2,1)}, f32[128,1536]{1,0:T(8,128)}, f32[96,768]{1,0:T(8,128)}, f32[96,256]{1,0:T(8,128)}, f32[96,256]{1,0:T(8,128)}, /*...) custom-call(bf16[128,1536]{1,0:T(8,128)(2,1)} %get-tuple-element.74., ...), custom_call_target="tpu_custom_call" | custom-call | tf_op jit(solution)/shard_map/finish/pallas_call | solution.py:1871

commit v7 on v6

--- a/solution.py
+++ b/solution.py
@@ -506,18 +506,18 @@
         there = self.view(source if self.fixed else target)
         return remote(self.view(source), there, self.send_sem.at[sem], self.recv_sem.at[target], device)
 
-    def _to_z(self, step):
+    def _to_z(self, z, way):
         place = self.place
-        own = place.z
-        return self._copy(own, own, step + place.line - 1, (place.me + 4 * step, place.core))
+        device = place.up() if way == 0 else place.down()
+        return self._copy(z, z, way * place.line + z, device)
 
     def _to_a(self, z):
         line = self.place.line
-        return self._copy(z, line + z, 2 * line - 1 + z, self.place.beside_a())
+        return self._copy(z, line + z, 2 * line + z, self.place.beside_a())
 
     def _to_b(self, slot):
         line = self.place.line
-        return self._copy(slot, 2 * line + slot, 3 * line - 1 + slot, self.place.beside_b())
+        return self._copy(slot, 2 * line + slot, 3 * line + slot, self.place.beside_b())
 
     def take(self, slot):
         self._copy(slot, slot, 0, self.place.beside_b()).wait_recv()
@@ -530,39 +530,44 @@
             pl.when(place.z >= step)(lambda: action(place.z - step))
             pl.when(place.z + step < place.line)(lambda: action(place.z + step))
 
+    def hand_on(self, slot):
+        self._to_b(slot).start()
+
     def start(self):
         place = self.place
-
-        def reach(step):
-            pl.when(place.z >= step)(lambda: self._to_z(-step).start())
-            pl.when(place.z + step < place.line)(lambda: self._to_z(step).start())
-
-        reach(1)
-        self._to_a(place.z).start()
-        self._to_b(place.z).start()
-        for step in range(2, place.line):
-            reach(step)
-
-    def along(self, step, then=None):
+        pl.when(place.z < place.line - 1)(lambda: self._to_z(place.z, 0).start())
+        pl.when(place.z > 0)(lambda: self._to_z(place.z, 1).start())
+        self._to_a(self.place.z).start()
+        self.hand_on(self.place.z)
+
+    def along(self, step):
+        place = self.place
+
         def pass_on(z):
             self.take(z)
+            pl.when(jnp.logical_and(z < place.z, place.z < place.line - 1))(lambda: self._to_z(z, 0).start())
+            pl.when(jnp.logical_and(z > place.z, place.z > 0))(lambda: self._to_z(z, 1).start())
             self._to_a(z).start()
-            self._to_b(z).start()
-            if then is not None:
-                then(z)
+            self.hand_on(z)
 
         self.near(step, pass_on)
 
-    def across(self, step, then=None):
+    def across(self, step):
         line = self.place.line
 
         def pass_on(z):
             self.take(line + z)
-            self._to_b(line + z).start()
-            if then is not None:
-                then(line + z)
+            self.hand_on(line + z)
 
         self.near(step, pass_on)
+
+    def step(self, number):
+        if number == 0:
+            self.start()
+            return
+        if number < self.place.line:
+            self.along(number)
+        self.across(number - 1)
 
     def settle(self):
         place = self.place
@@ -572,7 +577,8 @@
             self._to_a(z).wait_send()
             self._to_b(z).wait_send()
             self._to_b(line + z).wait_send()
-            pl.when(z != place.z)(lambda: self._to_z(z - place.z).wait_send())
+            pl.when(jnp.logical_and(z <= place.z, place.z < line - 1))(lambda: self._to_z(z, 0).wait_send())
+            pl.when(jnp.logical_and(z >= place.z, place.z > 0))(lambda: self._to_z(z, 1).wait_send())
             return carry
 
         lax.fori_loop(0, line, wait, 0)
@@ -587,17 +593,21 @@
         lax.fori_loop(0, 2 * line, wait, 0)
 
 
-def gather_all(gathers, thens=None):
-    line = gathers[0].place.line
-    thens = thens or [None] * len(gathers)
-    gathers[0].start()
-    for i, (g, then) in enumerate(zip(gathers, thens)):
-        for step in range(1, line + 1):
-            if step < line:
-                g.along(step, then)
-            if step == line - 1 and i + 1 < len(gathers):
-                gathers[i + 1].start()
-            g.across(step - 1, then)
+class Pipeline:
+    def __init__(self, gathers, lag):
+        self.gathers, self.lag, self.at = gathers, lag, 0
+        self.steps = gathers[0].place.line + 1
+
+    def run(self, number):
+        for _ in range(number):
+            for i, g in enumerate(self.gathers):
+                step = self.at - self.lag * i
+                if 0 <= step < self.steps:
+                    g.step(step)
+            self.at += 1
+
+    def until(self, index):
+        self.run(max(0, self.lag * index + self.steps - self.at))
 
 
 class Twin:
@@ -679,11 +689,6 @@
         self._to_a(z).wait_recv()
         self._add(z, self.from_a[z])
 
-    def send_line(self):
-        place = self.place
-        for z in ends_first(place.line):
-            pl.when(place.z != z)(lambda z=z: self._to_z(z).start())
-
     def fold_line_a(self):
         line = self.place.line
         for z in ends_first(line):
@@ -697,7 +702,7 @@
     def finish_line(self):
         for z in ends_first(self.place.line):
             self.fold_a(z)
-        self.send_line()
+            pl.when(self.place.z != z)(lambda z=z: self._to_z(z).start())
 
     def result(self, out):
         place, line = self.place, self.place.line
@@ -754,7 +759,7 @@
         return remote(
             self.packed.at[slot],
             self.compact.at[2 * line + slot, :, self.mine],
-            self.send_sem.at[3 * line - 1 + slot],
+            self.send_sem.at[3 * line + slot],
             self.recv_sem.at[2 * line + slot],
             self.place.beside_b(),
         )
@@ -767,7 +772,7 @@
     def take(self, slot):
         self._copy(slot, slot, 0, self.place.beside_b()).wait_recv()
 
-    def pack(self, slot):
+    def hand_on(self, slot):
         block = self.dense[slot]
         self.packed[slot] = jnp.dot(self.other_pick[slot], block, preferred_element_type=F32).astype(BF16)
         self._to_b(slot).start()
@@ -775,36 +780,6 @@
             self.own_pick[slot], block, preferred_element_type=F32
         ).astype(BF16)
         self.twin.start(slot)
-
-    def start(self):
-        place = self.place
-
-        def reach(step):
-            pl.when(place.z >= step)(lambda: self._to_z(-step).start())
-            pl.when(place.z + step < place.line)(lambda: self._to_z(step).start())
-
-        reach(1)
-        self._to_a(place.z).start()
-        for step in range(2, place.line):
-            reach(step)
-        self.pack(place.z)
-
-    def along(self, step):
-        def pass_on(z):
-            self.take(z)
-            self._to_a(z).start()
-            self.pack(z)
-
-        self.near(step, pass_on)
-
-    def across(self, step):
-        line = self.place.line
-
-        def pass_on(z):
-            self.take(line + z)
-            self.pack(line + z)
-
-        self.near(step, pass_on)
 
 
 class PackedReduce(Reduce):
@@ -918,6 +893,19 @@
     a = place.a + flip_a * (1 - 2 * place.a)
     b = place.b + flip_b * (1 - 2 * place.b)
     return place.part(z, a, b)
+
+
+PIECES = 2
+
+
+def pieces_of(place, width):
+    piece = width // 2 // PIECES
+
+    def spans(core):
+        starts = [pl.multiple_of((core * PIECES + i) * piece, 128) for i in range(PIECES)]
+        return [pl.ds(start, piece) for start in starts]
+
+    return spans(place.core), spans(1 - place.core), piece
 
 
 def halves(place, width):
@@ -1076,12 +1064,13 @@
     length, width = tokens_ref.shape
     shard, q_cols = query_ref.shape
     chunks = q_cols // 128
-    span, _ = halves(place, width)
+    spans, _, piece = pieces_of(place, width)
     own = []
     blocks = ((query_ref, query_all), (key_ref, key_all), (value_ref, value_all), (out_ref, out_all))
     for i, (src, dst) in enumerate(blocks):
         own.append(pltpu.make_async_copy(src, dst.at[place.me], local_sems.at[i]))
-    own.append(pltpu.make_async_copy(cot_ref.at[:, span], cot_dense.at[place.z], local_sems.at[4]))
+    for i in range(PIECES):
+        own.append(pltpu.make_async_copy(cot_ref.at[:, spans[i]], cot_dense.at[i, place.z], local_sems.at[4 + i]))
     for c in own:
         c.start()
     enter(place)
@@ -1093,34 +1082,38 @@
         for i, ref in enumerate((query_all, key_all, value_all, out_all))
     ]
     picks = (own_pick, other_pick)
-    cot = PackedGather(place, cot_dense, cot_packed, cot_all, picks, span, sends.at[4], recvs.at[4], twin_sems)
-    twin = cot.twin
+    cots = [
+        PackedGather(
+            place,
+            cot_dense.at[i],
+            cot_packed.at[i],
+            cot_all,
+            picks,
+            spans[i],
+            sends.at[4 + i],
+            recvs.at[4 + i],
+            twin_sems.at[i],
+        )
+        for i in range(PIECES)
+    ]
     out = gathers[3]
-    for g in gathers[:3]:
-        g.start()
+    pipeline = Pipeline([gathers[i] for i in (1, 2, 0, 3)] + cots, 1)
+    pipeline.run(1)
     gains = [g[...].astype(F32) for g in (gain_a_ref, gain_m_ref)]
     write_notes(note_ref, gate_table(logits_ref[...], ids_ref[...], count), gains)
     note.start()
     inputs = tokens_ref[...].astype(F32)
     inv_attn = lax.rsqrt(jnp.mean(inputs * inputs, axis=1, keepdims=True) + EPSILON)
-    for g in gathers[:3]:
-        g.along(1)
+    pipeline.run(1)
     note.finish()
     gains_ref[...] = spread_gains(notes, shard, width)
     normed_ref[...] = (inputs * inv_attn * gains_ref[1:2, :]).astype(BF16)
-    for g in gathers[:3]:
-        g.across(0)
+    pipeline.run(1)
     position, allowed = tree_tables(segments_ref[...], parents_ref[...], length)
     write_tables(tables_ref, position)
+    pipeline.run(1)
     selections(place, notes, own_pick, other_pick)
-    for step in range(2, line + 1):
-        for g in gathers[:3]:
-            if step < line:
-                g.along(step)
-            g.across(step - 1)
-        if step == line - 1:
-            out.start()
-            cot.start()
+    pipeline.until(2)
     for g in gathers[:3]:
         g.take_rest()
     normed = normed_ref[...]
@@ -1142,12 +1135,7 @@
     lane = lax.broadcasted_iota(jnp.int32, (length, 128), 1)
     small_lane = lax.broadcasted_iota(jnp.int32, (8, 128), 1)
     peaks = jnp.zeros((8, 128), F32)
-    for step in range(1, line + 1):
-        if step < line:
-            out.along(step)
-            cot.along(step)
-        out.across(step - 1)
-        cot.across(step - 1)
+    pipeline.run(1)
     for j in range(chunks):
         both = contract_cols(chunk_of(queries_ref, j), pair_of(keys_ref, j, group_size, lane)) * SCORE_SCALE
         low = []
@@ -1166,6 +1154,7 @@
             preferred_element_type=F32,
         )
         head_out_ref[:, 128 * j : 128 * (j + 1)] = mixed.astype(BF16)
+        pipeline.run(1)
     peak_ref[...] = peaks
     keeps = [
         pltpu.make_async_copy(src, dst, keep_sems.at[i])
@@ -1192,17 +1181,21 @@
     inv_moe = lax.rsqrt(jnp.mean(hidden * hidden, axis=1, keepdims=True) + EPSILON)
     moe_in_ref[...] = (hidden * inv_moe * gains_ref[2:3, :]).astype(BF16)
 
+    pipeline.until(len(pipeline.gathers) - 1)
+
     def rest(slot, carry):
-        cot.take_compact(slot)
+        for cot in cots:
+            cot.take_compact(slot)
         return carry
 
     lax.fori_loop(2 * line, count, rest, 0)
-    for g in gathers + [cot]:
+    for g in gathers + cots:
         g.settle()
 
     def other(slot, carry):
-        twin.wait_send(slot)
-        twin.take(slot)
+        for cot in cots:
+            cot.twin.wait_send(slot)
+            cot.twin.take(slot)
         return carry
 
     lax.fori_loop(0, count, other, 0)
@@ -1254,20 +1247,20 @@
         out_specs=[IN_VMEM] * len(outs) + [ANY] * 5,
         scratch_shapes=[pltpu.VMEM((count, *s), BF16) for s in blocks[:4]]
         + [
-            pltpu.VMEM((2 * line, length, half), BF16),
-            pltpu.VMEM((2 * line, cap, half), BF16),
+            pltpu.VMEM((PIECES, 2 * line, length, half // PIECES), BF16),
+            pltpu.VMEM((PIECES, 2 * line, cap, half // PIECES), BF16),
             pltpu.VMEM((count, cap, width), BF16),
             pltpu.VMEM((count, cap, length), BF16),
             pltpu.VMEM((2 * line, cap, length), BF16),
             pltpu.VMEM((length, width), F32),
             pltpu.VMEM((length, width), F32),
             pltpu.VMEM((count, 8, 128), F32),
-            pltpu.SemaphoreType.DMA((5, 5 * line)),
-            pltpu.SemaphoreType.DMA((5, count)),
+            pltpu.SemaphoreType.DMA((4 + PIECES, 5 * line)),
+            pltpu.SemaphoreType.DMA((4 + PIECES, count)),
             pltpu.SemaphoreType.DMA((count,)),
             pltpu.SemaphoreType.DMA((count,)),
-            pltpu.SemaphoreType.DMA((2, count)),
-            pltpu.SemaphoreType.DMA((5,)),
+            pltpu.SemaphoreType.DMA((PIECES, 2, count)),
+            pltpu.SemaphoreType.DMA((4 + PIECES,)),
             pltpu.SemaphoreType.DMA((5,)),
             pltpu.SemaphoreType.DMA((2,)),
         ],
@@ -1324,29 +1317,70 @@
     count = 4 * line
     cap, width = rows.shape[1:]
     tile_rows = line * cap
-    mine, theirs = halves(place, width)
+    mine, _ = halves(place, width)
+    spans, their_spans, piece = pieces_of(place, width)
     load = pltpu.make_async_copy(cot_ref, cots, load_sems)
     load.start()
-    dense[place.z] = rows_ref[:, mine]
+    for i in range(PIECES):
+        dense[i, place.z] = rows_ref[:, spans[i]]
     picks = (own_pick, other_pick)
     selections(place, notes_ref, own_pick, other_pick, gates)
     enter(place)
-    gather = PackedGather(place, dense, packed, rows, picks, mine, gather_send, gather_recv, twin_sems)
-    grad_twin = Twin(
+    gathers = [
+        PackedGather(
+            place,
+            dense.at[i],
+            packed.at[i],
+            rows,
+            picks,
+            spans[i],
+            gather_send.at[i],
+            gather_recv.at[i],
+            twin_sems.at[i],
+        )
+        for i in range(PIECES)
+    ]
+    grad_twins = [
+        Twin(
+            place,
+            lambda s, i=i: grad_stage.at[s, :, their_spans[i]],
+            lambda s, i=i: grad_compact.at[i, s],
+            twin_sems.at[PIECES + i, 0],
+            twin_sems.at[PIECES + i, 1],
+        )
+        for i in range(PIECES)
+    ]
+    mix_twin = Twin(
         place,
-        lambda s: grad_stage.at[s, :, theirs],
-        lambda s: grad_compact.at[s],
-        twin_sems.at[2],
-        twin_sems.at[3],
-    )
-    mix_twin = Twin(
-        place, lambda s: mix_stage.at[s, :, theirs], lambda s: mix_compact.at[s], twin_sems.at[4], twin_sems.at[5]
-    )
-    reduce = PackedReduce(
-        place, grad_compact, picks, grad_dense, grad_from_b, from_a, from_z, reduce_sems.at[0], reduce_sems.at[1]
-    )
+        lambda s: mix_stage.at[s, :, halves(place, width)[1]],
+        lambda s: mix_compact.at[s],
+        twin_sems.at[2 * PIECES, 0],
+        twin_sems.at[2 * PIECES, 1],
+    )
+    reduces = [
+        PackedReduce(
+            place,
+            grad_compact.at[i],
+            picks,
+            grad_dense.at[i],
+            grad_from_b.at[i],
+            from_a.at[i],
+            from_z.at[i],
+            reduce_sems.at[i, 0],
+            reduce_sems.at[i, 1],
+        )
+        for i in range(PIECES)
+    ]
     mix_reduce = PackedReduce(
-        place, mix_compact, picks, mix_dense, mix_from_b, None, None, reduce_sems.at[2], reduce_sems.at[3]
+        place,
+        mix_compact,
+        picks,
+        mix_dense,
+        mix_from_b,
+        None,
+        None,
+        reduce_sems.at[PIECES, 0],
+        reduce_sems.at[PIECES, 1],
     )
 
     def group_of(group):
@@ -1365,7 +1399,8 @@
     def work(group):
         some, flat = group_of(group)
         for slot in slots_of(group):
-            gather.twin.take(slot)
+            for g in gathers:
+                g.twin.take(slot)
         x = rows[some].reshape(tile_rows, width)
         gate_pre = jnp.dot(x, gate_ref[...], preferred_element_type=F32)
         up_pre = jnp.dot(x, up_ref[...], preferred_element_type=F32)
@@ -1379,8 +1414,9 @@
         d_up[flat, :] = d_u
         d_in = contract_cols(d_g, gate_ref[...]) + contract_cols(d_u, up_ref[...])
         grad_stage[some] = d_in.astype(BF16).reshape(line, cap, width)
-        for slot in slots_of(group):
-            grad_twin.start(slot)
+        for twin in grad_twins:
+            for slot in slots_of(group):
+                twin.start(slot)
 
     def mix_work(group):
         some, flat = group_of(group)
@@ -1389,19 +1425,25 @@
         for slot in slots_of(group):
             mix_twin.start(slot)
 
-    def fold(twin, stage, compact, group, send=None):
+    def fold(twin, stage, span, compact, group, send=None):
         def one(slot, carry):
             twin.take(slot)
-            compact[slot] = (compact[slot].astype(F32) + stage[slot, :, mine].astype(F32)).astype(BF16)
+            compact[slot] = (compact[slot].astype(F32) + stage[slot, :, span].astype(F32)).astype(BF16)
             if send is not None:
                 send(slot - 2 * line)
             return carry
 
         lax.fori_loop(line * group, line * (group + 1), one, 0)
 
+    def grad_fold(group, send=False):
+        for i in range(PIECES):
+            to_b = reduces[i].send_b if send else None
+            fold(grad_twins[i], grad_stage, spans[i], grad_compact.at[i], group, to_b)
+
     def take_group(group):
         for slot in slots_of(group):
-            gather.take_compact(slot)
+            for g in gathers:
+                g.take_compact(slot)
 
     def weight_grad(number, i):
         left, right = ((cots, active), (rows, d_gate), (rows, d_up))[number]
@@ -1416,25 +1458,22 @@
         stores.append(pltpu.make_async_copy(grads.at[number], out_ref, store_sems.at[number]))
         stores[-1].start()
 
-    grad_fold = functools.partial(fold, grad_twin, grad_stage, grad_compact)
-    mix_fold = functools.partial(fold, mix_twin, mix_stage, mix_compact)
-    gather.start()
+    mix_fold = functools.partial(fold, mix_twin, mix_stage, mine, mix_compact)
+    pipeline = Pipeline(gathers, 0)
+    pipeline.run(1)
     load.wait()
-    for at in range(max(line, 4)):
-        if at < 4:
-            ahead(at)
-        if at < line:
-            if at + 1 < line:
-                gather.along(at + 1)
-            gather.across(at)
+    for group in range(4):
+        ahead(group)
+        pipeline.run(1)
+    pipeline.until(PIECES - 1)
     work(0)
     take_group(2)
     work(2)
     work(1)
     take_group(3)
-    grad_fold(2, reduce.send_b)
+    grad_fold(2, True)
     work(3)
-    grad_fold(3, reduce.send_b)
+    grad_fold(3, True)
     mix_work(1)
     grad_fold(0)
     mix_work(2)
@@ -1442,49 +1481,59 @@
     mix_work(3)
     mix_fold(2, mix_reduce.send_b)
     mix_work(0)
-    pieces = width // 512
+    columns = width // 512
     order = ends_first(line)
-    for z in order:
-        reduce.fold_b(z)
+    for r in reduces:
+        for z in order:
+            r.fold_b(z)
     weight_grad(0, 0)
-    for at, z in enumerate(order):
-        reduce.fold_b(line + z)
-        reduce.send_a(z)
-    mix_fold(3, mix_reduce.send_b)
-    for i in range(1, pieces):
+    for at, r in enumerate(reduces):
+        for z in order:
+            r.fold_b(line + z)
+            r.send_a(z)
+        if at == 0:
+            mix_fold(3, mix_reduce.send_b)
+    for i in range(1, columns):
         weight_grad(0, i)
     store(0)
-    reduce.finish_line()
-    for i in range(pieces):
+    for r in reduces:
+        r.finish_line()
+        weight_grad(1, reduces.index(r))
+    for i in range(PIECES, columns):
         weight_grad(1, i)
     store(1)
     mix_fold(0)
     mix_fold(1)
-    reduce.result(total)
-    d_rows_ref[:, mine] = total[...]
-    last = remote(total, d_rows_ref.at[:, mine], last_sems.at[0], last_sems.at[1], place.twin())
-    last.start()
-    for i in range(pieces):
+    lasts = []
+    for i, r in enumerate(reduces):
+        r.result(total.at[i])
+        d_rows_ref[:, spans[i]] = total[i]
+        there = d_rows_ref.at[:, spans[i]]
+        lasts.append(remote(total.at[i], there, last_sems.at[0, i], last_sems.at[1, i], place.twin()))
+        lasts[-1].start()
+    for i in range(columns):
         weight_grad(2, i)
     store(2)
     for k in range(2 * line):
         mix_reduce.fold_b(k)
     stores.append(pltpu.make_async_copy(mix_dense, mix_ref, store_sems.at[3]))
     stores[-1].start()
-    reduce.settle()
+    for r in reduces:
+        r.settle()
     mix_reduce.settle_b()
-    gather.settle()
+    for g in gathers:
+        g.settle()
+
+    twins = [g.twin for g in gathers] + grad_twins + [mix_twin]
 
     def settle(slot, carry):
-        gather.twin.wait_send(slot)
-        grad_twin.wait_send(slot)
-        mix_twin.wait_send(slot)
+        for twin in twins:
+            twin.wait_send(slot)
         return carry
 
     lax.fori_loop(0, count, settle, 0)
-    for c in stores:
+    for c in stores + lasts:
         c.wait()
-    last.wait()
 
 
 def run_experts(line, rows, cots, notes, gate, up, down):
@@ -1492,6 +1541,7 @@
     length, width = rows.shape
     cap = cots.shape[1]
     half, hidden = width // 2, gate.shape[1]
+    piece = half // PIECES
     grad = jax.ShapeDtypeStruct((width, hidden), F32)
     return pl.pallas_call(
         functools.partial(experts_kernel, line),
@@ -1505,8 +1555,8 @@
         in_specs=[IN_VMEM, ANY, IN_VMEM, IN_VMEM, IN_VMEM, IN_VMEM],
         out_specs=[IN_VMEM, ANY, ANY, ANY, ANY],
         scratch_shapes=[
-            pltpu.VMEM((2 * line, length, half), BF16),
-            pltpu.VMEM((2 * line, cap, half), BF16),
+            pltpu.VMEM((PIECES, 2 * line, length, piece), BF16),
+            pltpu.VMEM((PIECES, 2 * line, cap, piece), BF16),
             pltpu.VMEM((count, cap, width), BF16),
             pltpu.VMEM((count, cap, width), BF16),
             pltpu.VMEM((count, cap, length), BF16),
@@ -1518,22 +1568,22 @@
             pltpu.VMEM((count * cap, hidden), F32),
             pltpu.VMEM((count, cap, width), BF16),
             pltpu.VMEM((count, cap, width), BF16),
+            pltpu.VMEM((PIECES, count, cap, piece), BF16),
             pltpu.VMEM((count, cap, half), BF16),
-            pltpu.VMEM((count, cap, half), BF16),
-            pltpu.VMEM((2 * line, length, half), BF16),
+            pltpu.VMEM((PIECES, 2 * line, length, piece), BF16),
             pltpu.VMEM((2 * line, length, half), BF16),
             pltpu.VMEM((3, width, hidden), F32),
-            pltpu.VMEM((length, half), F32),
+            pltpu.VMEM((PIECES, length, piece), F32),
+            pltpu.VMEM((PIECES, 2 * line, cap, piece), BF16),
             pltpu.VMEM((2 * line, cap, half), BF16),
-            pltpu.VMEM((2 * line, cap, half), BF16),
-            pltpu.VMEM((line, length, half), BF16),
-            pltpu.VMEM((line, length, half), BF16),
-            pltpu.SemaphoreType.DMA((4, 4 * line)),
-            pltpu.SemaphoreType.DMA((5 * line,)),
-            pltpu.SemaphoreType.DMA((count,)),
-            pltpu.SemaphoreType.DMA((6, count)),
+            pltpu.VMEM((PIECES, line, length, piece), BF16),
+            pltpu.VMEM((PIECES, line, length, piece), BF16),
+            pltpu.SemaphoreType.DMA((PIECES + 1, 2, 4 * line)),
+            pltpu.SemaphoreType.DMA((PIECES, 5 * line)),
+            pltpu.SemaphoreType.DMA((PIECES, count)),
+            pltpu.SemaphoreType.DMA((2 * PIECES + 1, 2, count)),
             pltpu.SemaphoreType.DMA,
-            pltpu.SemaphoreType.DMA((2,)),
+            pltpu.SemaphoreType.DMA((2, PIECES)),
             pltpu.SemaphoreType.DMA((4,)),
         ],
         compiler_params=params(2),

time: 289 us -> 257 us (0.89)
  Pallas kernels: 288 us -> 256 us
    pallas_call x1, Pallas kernels: 105 us -> 88.3 us  [run_forward(): pl.pallas_call(functools.partial(forward_kernel, line, group_size), out_s...]
    pallas_call x1, Pallas kernels: 88.2 us -> 73.2 us  [run_experts(): pl.pallas_call(functools.partial(experts_kernel, line), out_shape=[jax.Sh...]
where the time goes in v7:
time: 257 us
  Pallas kernels  256 us (100%)
    pallas_call x1, Pallas kernels, run_forward(): pl.pallas_call(functools.partial(forward_kernel, line, group_size), out_s...  88.3 us
    pallas_call x1, Pallas kernels, run_backward(): pl.pallas_call(functools.partial(backward_kernel, line, group_size), out_...  87.7 us
    pallas_call x1, Pallas kernels, run_experts(): pl.pallas_call(functools.partial(experts_kernel, line), out_shape=[jax.Sh...  73.2 us
    pallas_call x1, Pallas kernels, finish(): pl.pallas_call(functools.partial(finish_kernel, group_size), out_shape=ou...  6.55 us

profile of v7, /device:TPU:0, one launch (start us, length us, event | category | flops | bytes accessed | tf_op | source)
XLA Modules:
  0.0 256.6 jit_solution(13616567587325564275)
XLA Ops:
  0.6 88.3 %run_forward.1 = (bf16[128,1536]{1,0:T(8,128)(2,1)}, f32[128,1536]{1,0:T(8,128)}, bf16[128,1536]{1,0:T(8,128)(2,1)}, bf16[128,768]{1,0:T(8,128)(2,1)}, bf16[128,...) custom-call(bf16[128,1536]{1,0:T(8,128)(2,1)} %tokens_ref.3, ...), custom_call_target="tpu_custom_call" | custom-call | tf_op jit(solution)/shard_map/run_forward/pallas_call | solution.py:1243
  88.9 73.2 %run_experts.1 = (f32[128,1536]{1,0:T(8,128)}, bf16[8,128,768]{2,1,0:T(8,128)(2,1)}, f32[1536,256]{1,0:T(8,128)}, f32[1536,256]{1,0:T(8,128)}, f32[1536,256]{1,0:T(8,128)}) custom-call(bf16[128,1536]{1,0:T(8,128)(2,1)} %get-tuple-element.56.rows_ref, bf16[16,80,1536]{2,1,0:T(8,128)(2,1)} %get-tuple-element.57.cot_ref, ...), custom_call_target="tpu_custom_call" | custom-call | tf_op jit(solution)/shard_map/run_experts/pallas_call | solution.py:1546
  162.1 87.7 %run_backward.1 = (f32[128,1536]{1,0:T(8,128)}, bf16[128,1536]{1,0:T(8,128)(2,1)}, f32[96,768]{1,0:T(8,128)}, f32[96,256]{1,0:T(8,128)}, f32[96,256]{1,0:T(8,128...) custom-call(bf16[128,1536]{1,0:T(8,128)(2,1)} %tokens_ref.3, f32[128,1536]{1,0:T(8,128)} %get-tuple-element.55.hidden_ref, ...), custom_call_target="tpu_custom_call" | custom-call | tf_op jit(solution)/shard_map/run_backward/pallas_call | solution.py:1803
  249.8 6.6 %finish.1 = (bf16[128,1536]{1,0:T(8,128)(2,1)}, f32[128,1536]{1,0:T(8,128)}, f32[96,768]{1,0:T(8,128)}, f32[96,256]{1,0:T(8,128)}, f32[96,256]{1,0:T(8,128)}, /*...) custom-call(bf16[128,1536]{1,0:T(8,128)(2,1)} %get-tuple-element.74., ...), custom_call_target="tpu_custom_call" | custom-call | tf_op jit(solution)/shard_map/finish/pallas_call | solution.py:1921
